TPU v7x, 256 devices: a whole 4x4x8 slice. The times are simulated.
256 devices in a mesh: section: 8 (over z), expert: 32 (over y, x, core).
Axes of the slice: x: 4, y: 4, z: 8, core: 2. Of those that a mesh axis runs over, the one named last changes fastest.
Arguments:
- activations: bfloat16 [8, 4096, 2048], P('section', 'expert'), may hold values from -6 to 6
- gradients: bfloat16 [8, 4096, 2048], P('section', 'expert'), may hold values from -6 to 6
- stashed: bfloat16 [8, 4096, 2048], P('section', 'expert'), may hold values from -6 to 6
- norm_gain: bfloat16 [8, 2048], P('section'), may hold values from 0.5 to 1.5
- router: bfloat16 [8, 2048, 32], P('section'), may hold values from -0.125 to 0.125
- gate_weight: bfloat16 [8, 32, 2048, 768], P('section', 'expert'), may hold values from -0.125 to 0.125
- up_weight: bfloat16 [8, 32, 2048, 768], P('section', 'expert'), may hold values from -0.125 to 0.125
- down_weight: bfloat16 [8, 32, 768, 2048], P('section', 'expert'), may hold values from -0.21875 to 0.21875
- routes_forward: int32 [8, 4096, 2], P('section', 'expert'), may hold values from 0 to 31, all different within a row; in each aligned block of 128 rows (0 to 127, 128 to 255, ..., all dimensions but the last counted through in order) at most 12 rows name the same one
- routes_backward: int32 [8, 4096, 2], P('section', 'expert'), may hold values from 0 to 31, all different within a row; in each aligned block of 128 rows (0 to 127, 128 to 255, ..., all dimensions but the last counted through in order) at most 12 rows name the same one
Outputs:
- layer_out: bfloat16 [8, 4096, 2048], P('section', 'expert')
- input_grad: bfloat16 [8, 4096, 2048], P('section', 'expert')
Inputs may be any that keep to these rules, and one draw needn't show every extreme that they name: `routes_forward`: each token names 2 different experts. In each aligned block of 128 tokens (one index of expert's tokens of one section) no expert is named by more than 12 tokens, a bound that some block reaches. `routes_backward`: each token names 2 different experts. In each aligned block of 128 tokens (one index of expert's tokens of one section) no expert is named by more than 12 tokens, a bound that some block reaches.
All inputs are finite; a program needn't handle non-finite values.
Results may differ from a plain program's by a relative error of at most 0.0059.
Values may be sent and summed in bfloat16 or wider, within the bound.
No kernel may reach another device: no remote copies, remote signals or barrier semaphores. Data moves between devices by JAX's collectives and lax.ppermute only.
A program may use at most 128 MiB of HBM per device.

v0:
```python
import jax
import jax.numpy as jnp
from jax import lax
from jax.sharding import PartitionSpec as P

NORM_EPS = 1e-06


def passed_along(value, axis, steps):
    count = lax.axis_size(axis)
    pairs = [(source, (source + steps) % count) for source in range(count)]
    return lax.ppermute(value, axis, pairs)


def normalize(tokens, gain_row):
    values = tokens.astype(jnp.float32)
    inverse = lax.rsqrt(jnp.mean(values * values, axis=-1, keepdims=True) + NORM_EPS)
    normed = (values * inverse * gain_row.astype(jnp.float32)).astype(jnp.bfloat16)
    return (normed, inverse)


def route_weights(normed, router_mat, routes):
    logits = jnp.dot(normed, router_mat, preferred_element_type=jnp.float32)
    columns = jnp.arange(router_mat.shape[1], dtype=jnp.int32)
    matches = (routes[:, :, None] == columns[None, None, :]).astype(jnp.float32)
    picked = jnp.sum(matches * logits[:, None, :], axis=2)
    sigmoids = jax.nn.sigmoid(picked)
    totals = jnp.sum(sigmoids, axis=1, keepdims=True)
    return (sigmoids / totals, sigmoids, totals, matches)


def slot_positions(routes, expert_count, capacity):
    columns = jnp.arange(expert_count, dtype=jnp.int32)
    matches = (routes[:, :, None] == columns[None, None, :]).astype(jnp.int32)
    per_row = jnp.sum(matches, axis=1)
    earlier = jnp.cumsum(per_row, axis=0) - per_row
    slots = jnp.sum(matches * earlier[:, None, :], axis=2)
    return routes * capacity + slots


def dispatch_table(position, scales, slot_count):
    targets = jnp.arange(slot_count, dtype=jnp.int32)
    matches = position[None, :, :] == targets[:, None, None]
    return jnp.sum(jnp.where(matches, scales[None, :, :], 0.0), axis=2).astype(jnp.bfloat16)


def expert_forward(slot_rows, gate_mat, up_mat, down_mat):
    gate = jnp.dot(slot_rows, gate_mat, preferred_element_type=jnp.float32)
    upper = jnp.dot(slot_rows, up_mat, preferred_element_type=jnp.float32)
    hidden = (jax.nn.silu(gate) * upper).astype(jnp.bfloat16)
    result = jnp.dot(hidden, down_mat, preferred_element_type=jnp.float32).astype(jnp.bfloat16)
    return (result, gate, upper)


def expert_backward(slot_rows, slot_grad, gate_mat, up_mat, down_mat):
    result, gate, upper = expert_forward(slot_rows, gate_mat, up_mat, down_mat)
    dims = (((1,), (1,)), ((), ()))
    grad_hidden = lax.dot_general(slot_grad, down_mat, dims, preferred_element_type=jnp.float32)
    sigmoid_gate = jax.nn.sigmoid(gate)
    grad_up = (grad_hidden * gate * sigmoid_gate).astype(jnp.bfloat16)
    grad_gate = (grad_hidden * upper * sigmoid_gate * (1.0 + gate * (1.0 - sigmoid_gate))).astype(
        jnp.bfloat16
    )
    row_grad = lax.dot_general(grad_gate, gate_mat, dims, preferred_element_type=jnp.float32)
    row_grad = row_grad + lax.dot_general(grad_up, up_mat, dims, preferred_element_type=jnp.float32)
    return (result, row_grad.astype(jnp.bfloat16))


def router_backward(scores, weights, sigmoids, totals, matches, router_mat):
    mixed_score = jnp.sum(weights * scores, axis=1, keepdims=True)
    grad_pick = (scores - mixed_score) / totals * sigmoids * (1.0 - sigmoids)
    grad_logits = jnp.sum(grad_pick[:, :, None] * matches, axis=1)
    return jnp.dot(grad_logits, router_mat.astype(jnp.float32).T, precision=lax.Precision.HIGHEST)


def norm_backward(tokens, inverse, gain_row, grad_normed):
    values = tokens.astype(jnp.float32)
    grad_pre = grad_normed * gain_row.astype(jnp.float32)
    cubed = inverse * inverse * inverse
    return inverse * grad_pre - values * cubed * jnp.mean(grad_pre * values, axis=-1, keepdims=True)


def body(
    activations,
    gradients,
    stashed,
    norm_gain,
    router,
    gate_weight,
    up_weight,
    down_weight,
    routes_forward,
    routes_backward,
):
    arrived = passed_along(activations, "section", 1)[0]
    cotangent = passed_along(gradients, "section", -1)[0]
    owners = lax.axis_size("expert")
    per_source, model_width = arrived.shape
    top_count = routes_forward.shape[2]
    capacity = 3 * per_source * top_count // (2 * owners)
    slot_count = owners * capacity
    gate_mat = gate_weight[0, 0]
    up_mat = up_weight[0, 0]
    down_mat = down_weight[0, 0]
    gain_row = norm_gain[0]
    router_mat = router[0]
    stored = stashed[0]
    normed_f, inverse_f = normalize(arrived, gain_row)
    weights_f, sig_f, tot_f, match_f = route_weights(normed_f, router_mat, routes_forward[0])
    position_f = slot_positions(routes_forward[0], owners, capacity)
    unit_scales = jnp.ones(position_f.shape, jnp.float32)
    table_f = dispatch_table(position_f, unit_scales, slot_count)
    buffer_f = jnp.dot(table_f, normed_f, preferred_element_type=jnp.float32).astype(jnp.bfloat16)
    buffer_f = buffer_f.reshape(owners, capacity, model_width)
    normed_b, inverse_b = normalize(stored, gain_row)
    weights_b, sig_b, tot_b, match_b = route_weights(normed_b, router_mat, routes_backward[0])
    position_b = slot_positions(routes_backward[0], owners, capacity)
    table_b = dispatch_table(position_b, unit_scales, slot_count)
    buffer_b = jnp.dot(table_b, normed_b, preferred_element_type=jnp.float32).astype(jnp.bfloat16)
    buffer_b = buffer_b.reshape(owners, capacity, model_width)
    scale_round = lax.optimization_barrier(weights_b.astype(jnp.bfloat16)).astype(jnp.float32)
    scaled_table = dispatch_table(position_b, scale_round, slot_count)
    grad_buffer = jnp.dot(table_b, cotangent, preferred_element_type=jnp.float32).astype(
        jnp.bfloat16
    )
    grad_buffer = grad_buffer.reshape(owners, capacity, model_width)
    scale_slots = (
        jnp.sum(scaled_table.astype(jnp.float32), axis=1)
        .astype(jnp.bfloat16)
        .reshape(owners, capacity)
    )
    front_rows = lax.all_to_all(buffer_f, "expert", split_axis=0, concat_axis=0, tiled=True)
    back_rows = lax.all_to_all(buffer_b, "expert", split_axis=0, concat_axis=0, tiled=True)
    grad_rows = lax.all_to_all(grad_buffer, "expert", split_axis=0, concat_axis=0, tiled=True)
    scale_part = lax.all_to_all(scale_slots, "expert", split_axis=0, concat_axis=0, tiled=True)
    block_shape = front_rows.shape
    front_out = expert_forward(front_rows.reshape(-1, model_width), gate_mat, up_mat, down_mat)[0]
    slot_grad = (scale_part.astype(jnp.float32)[:, :, None] * grad_rows.astype(jnp.float32)).astype(
        jnp.bfloat16
    )
    back_out, back_grad = expert_backward(
        back_rows.reshape(-1, model_width),
        slot_grad.reshape(-1, model_width),
        gate_mat,
        up_mat,
        down_mat,
    )
    slot_scores = jnp.einsum(
        "ncd,ncd->nc", grad_rows, back_out.reshape(block_shape), preferred_element_type=jnp.float32
    ).astype(jnp.bfloat16)
    returned_f = lax.all_to_all(
        front_out.reshape(block_shape), "expert", split_axis=0, concat_axis=0, tiled=True
    )
    returned_dn = lax.all_to_all(
        back_grad.reshape(block_shape), "expert", split_axis=0, concat_axis=0, tiled=True
    )
    returned_s = lax.all_to_all(slot_scores, "expert", split_axis=0, concat_axis=0, tiled=True)
    scores_b = jnp.take(returned_s.reshape(slot_count), position_b, axis=0)
    scores = lax.optimization_barrier(scores_b).astype(jnp.float32)
    picked_f = jnp.take(returned_f.reshape(slot_count, model_width), position_f, axis=0)
    combined = jnp.sum(weights_f[:, :, None] * picked_f.astype(jnp.float32), axis=1)
    layer_out = (arrived.astype(jnp.float32) + combined).astype(jnp.bfloat16)
    picked_dn = jnp.take(returned_dn.reshape(slot_count, model_width), position_b, axis=0)
    grad_normed = jnp.sum(picked_dn.astype(jnp.float32), axis=1)
    grad_normed = grad_normed + router_backward(
        scores, weights_b, sig_b, tot_b, match_b, router_mat
    )
    input_grad = cotangent.astype(jnp.float32) + norm_backward(
        stored, inverse_b, gain_row, grad_normed
    )
    return (layer_out[None], input_grad.astype(jnp.bfloat16)[None])


def solution(mesh):
    placed = (
        P("section", "expert", None),
        P("section", "expert", None),
        P("section", "expert", None),
        P("section", None),
        P("section", None, None),
        P("section", "expert", None, None),
        P("section", "expert", None, None),
        P("section", "expert", None, None),
        P("section", "expert", None),
        P("section", "expert", None),
    )
    return jax.shard_map(
        body,
        mesh=mesh,
        in_specs=placed,
        out_specs=(P("section", "expert", None), P("section", "expert", None)),
        check_vma=False,
    )
```

profile of v0, /device:TPU:1, one launch (start us, length us, event | category | flops | bytes accessed | tf_op | source)
XLA Modules:
  0.0 233.3 jit_solution(5841721104529181901)
XLA Ops:
  0.7 6.5 %collective-permute-start.1 = (bf16[1,128,2048]{2,1,0:T(8,128)(2,1)}, bf16[1,128,2048]{2,1,0:T(8,128)(2,1)}, u32[]{:S(2)}, u32[]{:S(2)}) collective-permute-start(bf16[1,128,2048]{2,1,0:T(8,128)(2,1)} %param.13), channel_id=1, source_target_pairs={{0,224},{32,0},{64,32},{96,64},{128,96},{160,128},{192,160},{224,1... | collective-permute-start | bytes 1572872 | tf_op jit(solution)/shard_map/ppermute | solution.py:12
  13.3 8.0 %all-to-all-start.2 = ((bf16[32,1,12]{2,1,0:T(2,128)(2,1)}), bf16[32,1,12]{2,1,0:T(2,128)(2,1)S(1)}, u32[]{:S(2)}, u32[]{:S(2)}) async-start(bf16[32,1,12]{2,1,0:T(2,128)(2,1)} %all_to_all.36), calls=%async_computation.2 | async-start | bytes 32768 | tf_op jit(solution)/shard_map/all_to_all | solution.py:135
  24.3 3.6 %reshape.210 = bf16[32,12,2048]{2,1,0:T(8,128)(2,1)} reshape(bf16[384,2048]{1,0:T(8,128)(2,1)} %convolution_convert_fusion) | data formatting | bytes 3145728 | tf_op jit(solution)/shard_map/reshape | solution.py:120
  28.2 7.2 %all-to-all-start.4 = ((bf16[32,12,2048]{2,1,0:T(8,128)(2,1)}), bf16[32,12,2048]{2,1,0:T(8,128)(2,1)}, u32[]{:S(2)}, u32[]{:S(2)}) async-start(bf16[32,12,2048]{2,1,0:T(8,128)(2,1)} %reshape.210), calls=%async_computation.4 | async-start | bytes 4194304 | tf_op jit(solution)/shard_map/all_to_all | solution.py:133
  39.5 3.6 %reshape.208 = bf16[32,12,2048]{2,1,0:T(8,128)(2,1)} reshape(bf16[384,2048]{1,0:T(8,128)(2,1)} %convolution_convert_fusion.1) | data formatting | bytes 3145728 | tf_op jit(solution)/shard_map/reshape | solution.py:126
  44.4 19.8 %all-to-all-done.4 = bf16[32,12,2048]{2,1,0:T(8,128)(2,1)} async-done(((bf16[32,12,2048]{2,1,0:T(8,128)(2,1)}), bf16[32,12,2048]{2,1,0:T(8,128)(2,1)}, u32[]{:S(2)}, u32[]{:S(2)}) %all-to-all-start.4) | async-done | bytes 1572896 | tf_op jit(solution)/shard_map/all_to_all | solution.py:133
  64.2 6.0 %all-to-all-start.3 = ((bf16[32,12,2048]{2,1,0:T(8,128)(2,1)}), bf16[32,12,2048]{2,1,0:T(8,128)(2,1)}, u32[]{:S(2)}, u32[]{:S(2)}) async-start(bf16[32,12,2048]{2,1,0:T(8,128)(2,1)} %reshape.208), calls=%async_computation.3 | async-start | bytes 4194304 | tf_op jit(solution)/shard_map/all_to_all | solution.py:134
  73.0 3.6 %reshape.204 = bf16[32,12,2048]{2,1,0:T(8,128)(2,1)} reshape(bf16[384,2048]{1,0:T(8,128)(2,1)} %convolution_convert_fusion.2) | data formatting | bytes 3145728 | tf_op jit(solution)/shard_map/reshape | solution.py:114
  78.1 3.6 %reshape.211 = bf16[384,2048]{1,0:T(8,128)(2,1)} reshape(bf16[32,12,2048]{2,1,0:T(8,128)(2,1)} %all-to-all-done.4) | data formatting | bytes 3145728 | tf_op jit(solution)/shard_map/reshape | solution.py:142
  81.7 4.9 %fusion.16 = f32[384,768]{1,0:T(8,128)} fusion(bf16[384,2048]{1,0:T(8,128)(2,1)} %reshape.211, bf16[1,1,2048,768]{3,2,1,0:T(8,128)(2,1)} %param.17), kind=kOutput, calls=%fused_computation.21 | convolution fusion | flops 1207959552 | bytes 5898240 | tf_op jit(solution)/shard_map/dot_general | solution.py:48
  89.1 9.4 %all-to-all-done.3 = bf16[32,12,2048]{2,1,0:T(8,128)(2,1)} async-done(((bf16[32,12,2048]{2,1,0:T(8,128)(2,1)}), bf16[32,12,2048]{2,1,0:T(8,128)(2,1)}, u32[]{:S(2)}, u32[]{:S(2)}) %all-to-all-start.3) | async-done | bytes 1572896 | tf_op jit(solution)/shard_map/all_to_all | solution.py:134
  98.5 6.5 %all-to-all-start = ((bf16[32,12,2048]{2,1,0:T(8,128)(2,1)}), bf16[32,12,2048]{2,1,0:T(8,128)(2,1)}, u32[]{:S(2)}, u32[]{:S(2)}) async-start(bf16[32,12,2048]{2,1,0:T(8,128)(2,1)} %reshape.204), calls=%async_computation | async-start | bytes 4194304 | tf_op jit(solution)/shard_map/all_to_all | solution.py:132
  105.0 4.3 %fusion.25 = bf16[384,2048]{1,0:T(8,128)(2,1)} fusion(bf16[1,1,768,2048]{3,2,1,0:T(8,128)(2,1)S(1)} %copy-done, f32[384,768]{1,0:T(8,128)} %fusion.10, f32[384,768]{1,0:T(8,128)} %fusion.16), kind=kOutput, calls=%fused_computation.27 | convolution fusion | flops 1210515456 | bytes 7077888 | tf_op jit(solution)/shard_map/dot_general | solution.py:51
  109.3 3.6 %reshape.214 = bf16[32,12,2048]{2,1,0:T(8,128)(2,1)} reshape(bf16[384,2048]{1,0:T(8,128)(2,1)} %fusion.25) | data formatting | bytes 3145728 | tf_op jit(solution)/shard_map/reshape | solution.py:149
  112.9 4.4 %fusion.1 = (bf16[32,12]{1,0:T(8,128)(2,1)S(1)}, bf16[32,12,2048]{2,1,0:T(8,128)(2,1)}) fusion(bf16[32,12,2048]{2,1,0:T(8,128)(2,1)} %all-to-all-done.3, bf16[32,12,2048]{2,1,0:T(8,128)(2,1)} %reshape.214, f32[32,12]{1,0:T(8,128)S(1)} %bitcast.143), kind=kLoop, calls=%fused_computation.6 | loop fusion | flops 4718208 | bytes 4720896
  118.1 3.7 %reshape.209 = bf16[384,2048]{1,0:T(8,128)(2,1)} reshape(bf16[32,12,2048]{2,1,0:T(8,128)(2,1)} %get-tuple-element.15) | data formatting | bytes 3145728 | tf_op jit(solution)/shard_map/reshape | solution.py:143
  121.8 3.0 %fusion.4 = f32[384,768]{1,0:T(8,128)S(1)} fusion(bf16[384,2048]{1,0:T(8,128)(2,1)} %reshape.209, bf16[1,1,768,2048]{3,2,1,0:T(8,128)(2,1)S(1)} %copy-done), kind=kOutput, calls=%fused_computation.9 | convolution fusion | flops 1207959552 | bytes 5898240 | tf_op jit(solution)/shard_map/dot_general | solution.py:58
  125.8 3.2 %fusion.8 = f32[384,2048]{1,0:T(8,128)} fusion(bf16[1,1,2048,768]{3,2,1,0:T(8,128)(2,1)S(1)} %copy-done.10, f32[384,768]{1,0:T(8,128)S(1)} %fusion.4, f32[384,768]{1,0:T(8,128)S(1)} %copy-done.11), kind=kOutput, calls=%fused_computation.13 | convolution fusion | flops 1209729024 | bytes 8650752 | tf_op jit(solution)/shard_map/dot_general | solution.py:65
  129.0 4.3 %all-to-all-done = bf16[32,12,2048]{2,1,0:T(8,128)(2,1)} async-done(((bf16[32,12,2048]{2,1,0:T(8,128)(2,1)}), bf16[32,12,2048]{2,1,0:T(8,128)(2,1)}, u32[]{:S(2)}, u32[]{:S(2)}) %all-to-all-start) | async-done | bytes 1572896 | tf_op jit(solution)/shard_map/all_to_all | solution.py:132
  133.3 5.7 %all-to-all-start.6 = ((bf16[32,1,12]{2,1,0:T(2,128)(2,1)}), bf16[32,1,12]{2,1,0:T(2,128)(2,1)S(1)}, u32[]{:S(2)}, u32[]{:S(2)}) async-start(bf16[32,1,12]{2,1,0:T(2,128)(2,1)} %copy.59), calls=%async_computation.6 | async-start | bytes 32768 | tf_op jit(solution)/shard_map/all_to_all | solution.py:157
  139.0 6.7 %add_convert_fusion = bf16[384,2048]{1,0:T(8,128)(2,1)} fusion(f32[384,2048]{1,0:T(8,128)} %fusion.8, bf16[1,1,2048,768]{3,2,1,0:T(8,128)(2,1)} %param.17, f32[384,768]{1,0:T(8,128)} %fusion.16, f32[384,768]{1,0:T(8,128)} %copy-done.12, f32[384,768]{1,0:T(8,128)} %fusion.10), kind=kOutput, calls=%fused_computation.25 | convolution fusion | flops 1212481536 | bytes 11403264 | tf_op jit(solution)/shard_map/dot_general | solution.py:64
  145.7 3.6 %reshape.212 = bf16[32,12,2048]{2,1,0:T(8,128)(2,1)} reshape(bf16[384,2048]{1,0:T(8,128)(2,1)} %add_convert_fusion) | data formatting | bytes 3145728 | tf_op jit(solution)/shard_map/reshape | solution.py:155
  149.3 7.6 %all-to-all-start.5 = ((bf16[32,12,2048]{2,1,0:T(8,128)(2,1)}), bf16[32,12,2048]{2,1,0:T(8,128)(2,1)}, u32[]{:S(2)}, u32[]{:S(2)}) async-start(bf16[32,12,2048]{2,1,0:T(8,128)(2,1)} %reshape.212), calls=%async_computation.5 | async-start | bytes 4194304 | tf_op jit(solution)/shard_map/all_to_all | solution.py:154
  157.1 3.7 %reshape.205 = bf16[384,2048]{1,0:T(8,128)(2,1)} reshape(bf16[32,12,2048]{2,1,0:T(8,128)(2,1)} %all-to-all-done) | data formatting | bytes 3145728 | tf_op jit(solution)/shard_map/reshape | solution.py:137
  160.7 4.8 %fusion.18 = f32[384,768]{1,0:T(8,128)} fusion(bf16[384,2048]{1,0:T(8,128)(2,1)} %reshape.205, bf16[1,1,2048,768]{3,2,1,0:T(8,128)(2,1)} %param.17), kind=kOutput, calls=%fused_computation.23 | convolution fusion | flops 1207959552 | bytes 5898240 | tf_op jit(solution)/shard_map/dot_general | solution.py:48
  165.6 6.9 %fusion.22 = bf16[384,2048]{1,0:T(8,128)(2,1)} fusion(bf16[1,1,768,2048]{3,2,1,0:T(8,128)(2,1)S(1)} %copy-done, bf16[384,2048]{1,0:T(8,128)(2,1)} %reshape.205, bf16[1,1,2048,768]{3,2,1,0:T(8,128)(2,1)} %param.18, f32[384,768]{1,0:T(8,128)} %fusion.18), kind=kOutput, calls=%fused_computation.26 | convolution fusion | flops 2418475008 | bytes 10616832 | tf_op jit(solution)/shard_map/dot_general | solution.py:51
  172.5 3.6 %reshape.206 = bf16[32,12,2048]{2,1,0:T(8,128)(2,1)} reshape(bf16[384,2048]{1,0:T(8,128)(2,1)} %fusion.22) | data formatting | bytes 3145728 | tf_op jit(solution)/shard_map/reshape | solution.py:152
  178.4 7.2 %all-to-all-done.5 = bf16[32,12,2048]{2,1,0:T(8,128)(2,1)} async-done(((bf16[32,12,2048]{2,1,0:T(8,128)(2,1)}), bf16[32,12,2048]{2,1,0:T(8,128)(2,1)}, u32[]{:S(2)}, u32[]{:S(2)}) %all-to-all-start.5) | async-done | bytes 1572896 | tf_op jit(solution)/shard_map/all_to_all | solution.py:154
  185.6 6.2 %all-to-all-start.1 = ((bf16[32,12,2048]{2,1,0:T(8,128)(2,1)}), bf16[32,12,2048]{2,1,0:T(8,128)(2,1)}, u32[]{:S(2)}, u32[]{:S(2)}) async-start(bf16[32,12,2048]{2,1,0:T(8,128)(2,1)} %reshape.206), calls=%async_computation.1 | async-start | bytes 4194304 | tf_op jit(solution)/shard_map/all_to_all | solution.py:151
  197.7 5.1 %convert_reduce_fusion = f32[128,2048]{1,0:T(8,128)S(1)} fusion(bf16[128,2,2048]{2,1,0:T(2,128)(2,1)} %reshape.256, pred[128,2]{1,0:T(8,128)(4,1)S(1)} %copy.56), kind=kLoop, calls=%fused_computation.33 | loop fusion | flops 1310720 | bytes 2097408 | tf_op jit(solution)/shard_map/reduce_sum | solution.py:164
  204.6 15.6 %all-to-all-done.1 = bf16[32,12,2048]{2,1,0:T(8,128)(2,1)} async-done(((bf16[32,12,2048]{2,1,0:T(8,128)(2,1)}), bf16[32,12,2048]{2,1,0:T(8,128)(2,1)}, u32[]{:S(2)}, u32[]{:S(2)}) %all-to-all-start.1) | async-done | bytes 1572896 | tf_op jit(solution)/shard_map/all_to_all | solution.py:151
  224.8 4.1 %multiply_reduce_fusion = f32[128,2048]{1,0:T(8,128)S(1)} fusion(bf16[128,2,2048]{2,1,0:T(2,128)(2,1)S(1)} %reshape.252, pred[128,2]{1,0:T(8,128)(4,1)S(1)} %copy.51, f32[128,2]{1,0:T(8,128)S(1)} %copy.47), kind=kLoop, calls=%fused_computation.34 | loop fusion | flops 1835008 | bytes 2098432 | tf_op jit(solution)/shard_map/reduce_sum | solution.py:161
  (103 shorter events, 42.2 us)
Async XLA Ops:
  0.6 104.4 %copy-start = (bf16[1,1,768,2048]{3,2,1,0:T(8,128)(2,1)S(1)}, bf16[1,1,768,2048]{3,2,1,0:T(8,128)(2,1)}, u32[]{:S(2)}) copy-start(bf16[1,1,768,2048]{3,2,1,0:T(8,128)(2,1)} %param.19) | copy-start | bytes 9437188
  0.6 11.7 %copy-start.7 = (s32[1,128,2]{1,2,0:T(2,128)S(1)}, s32[1,128,2]{1,2,0:T(2,128)}, u32[]{:S(2)}) copy-start(s32[1,128,2]{1,2,0:T(2,128)} %param.21) | copy-start | bytes 3076
  0.7 36.0 %collective-permute-start.1 = (bf16[1,128,2048]{2,1,0:T(8,128)(2,1)}, bf16[1,128,2048]{2,1,0:T(8,128)(2,1)}, u32[]{:S(2)}, u32[]{:S(2)}) collective-permute-start(bf16[1,128,2048]{2,1,0:T(8,128)(2,1)} %param.13), channel_id=1, source_target_pairs={{0,224},{32,0},{64,32},{96,64},{128,96},{160,128},{192,160},{224,1... | collective-permute-start | bytes 1572872 | tf_op jit(solution)/shard_map/ppermute | solution.py:12
  13.3 14.9 %all-to-all-start.2 = ((bf16[32,1,12]{2,1,0:T(2,128)(2,1)}), bf16[32,1,12]{2,1,0:T(2,128)(2,1)S(1)}, u32[]{:S(2)}, u32[]{:S(2)}) async-start(bf16[32,1,12]{2,1,0:T(2,128)(2,1)} %all_to_all.36), calls=%async_computation.2 | async-start | bytes 32768 | tf_op jit(solution)/shard_map/all_to_all | solution.py:135
  21.3 21.8 %collective-permute-start = (bf16[1,128,2048]{2,1,0:T(8,128)(2,1)}, bf16[1,128,2048]{2,1,0:T(8,128)(2,1)}, u32[]{:S(2)}, u32[]{:S(2)}) collective-permute-start(bf16[1,128,2048]{2,1,0:T(8,128)(2,1)} %param.12), channel_id=1, source_target_pairs={{0,32},{32,64},{64,96},{96,128},{128,160},{160,192},{192,224},{224... | collective-permute-start | bytes 1572872 | tf_op jit(solution)/shard_map/ppermute | solution.py:12
  27.9 7.8 %copy-start.8 = (s32[1,128,2]{1,2,0:T(2,128)S(1)}, s32[1,128,2]{1,2,0:T(2,128)}, u32[]{:S(2)}) copy-start(s32[1,128,2]{1,2,0:T(2,128)} %param.20) | copy-start | bytes 3076
  28.2 36.0 %all-to-all-start.4 = ((bf16[32,12,2048]{2,1,0:T(8,128)(2,1)}), bf16[32,12,2048]{2,1,0:T(8,128)(2,1)}, u32[]{:S(2)}, u32[]{:S(2)}) async-start(bf16[32,12,2048]{2,1,0:T(8,128)(2,1)} %reshape.210), calls=%async_computation.4 | async-start | bytes 4194304 | tf_op jit(solution)/shard_map/all_to_all | solution.py:133
  64.2 34.3 %all-to-all-start.3 = ((bf16[32,12,2048]{2,1,0:T(8,128)(2,1)}), bf16[32,12,2048]{2,1,0:T(8,128)(2,1)}, u32[]{:S(2)}, u32[]{:S(2)}) async-start(bf16[32,12,2048]{2,1,0:T(8,128)(2,1)} %reshape.208), calls=%async_computation.3 | async-start | bytes 4194304 | tf_op jit(solution)/shard_map/all_to_all | solution.py:134
  73.0 3.6 %copy-start.6 = (bf16[1,2048,32]{1,2,0:T(8,128)(2,1)S(1)}, bf16[1,2048,32]{1,2,0:T(8,128)(2,1)}, u32[]{:S(2)}) copy-start(bf16[1,2048,32]{1,2,0:T(8,128)(2,1)} %param.16) | copy-start | bytes 393220
  81.7 4.9 %copy-start.5 = (bf16[384,2048]{1,0:T(8,128)(2,1)S(1)}, bf16[384,2048]{1,0:T(8,128)(2,1)}, u32[]{:S(2)}) copy-start(bf16[384,2048]{1,0:T(8,128)(2,1)} %reshape.211) | copy-start | bytes 4718596
  81.7 4.9 %copy-start.9 = (bf16[1,1,2048,768]{3,2,1,0:T(8,128)(2,1)S(1)}, bf16[1,1,2048,768]{3,2,1,0:T(8,128)(2,1)}, u32[]{:S(2)}) copy-start(bf16[1,1,2048,768]{3,2,1,0:T(8,128)(2,1)} %param.18) | copy-start | bytes 9437188
  98.5 34.8 %all-to-all-start = ((bf16[32,12,2048]{2,1,0:T(8,128)(2,1)}), bf16[32,12,2048]{2,1,0:T(8,128)(2,1)}, u32[]{:S(2)}, u32[]{:S(2)}) async-start(bf16[32,12,2048]{2,1,0:T(8,128)(2,1)} %reshape.204), calls=%async_computation | async-start | bytes 4194304 | tf_op jit(solution)/shard_map/all_to_all | solution.py:132
  121.8 4.0 %copy-start.10 = (bf16[1,1,2048,768]{3,2,1,0:T(8,128)(2,1)S(1)}, bf16[1,1,2048,768]{3,2,1,0:T(8,128)(2,1)}, u32[]{:S(2)}) copy-start(bf16[1,1,2048,768]{3,2,1,0:T(8,128)(2,1)} %param.18) | copy-start | bytes 9437188
  121.8 4.0 %copy-start.11 = (f32[384,768]{1,0:T(8,128)S(1)}, f32[384,768]{1,0:T(8,128)}, u32[]{:S(2)}) copy-start(f32[384,768]{1,0:T(8,128)} %fusion.16) | copy-start | bytes 3538948
  124.8 1.0 copy-start.12
  133.3 16.0 %all-to-all-start.6 = ((bf16[32,1,12]{2,1,0:T(2,128)(2,1)}), bf16[32,1,12]{2,1,0:T(2,128)(2,1)S(1)}, u32[]{:S(2)}, u32[]{:S(2)}) async-start(bf16[32,1,12]{2,1,0:T(2,128)(2,1)} %copy.59), calls=%async_computation.6 | async-start | bytes 32768 | tf_op jit(solution)/shard_map/all_to_all | solution.py:157
  149.3 36.3 %all-to-all-start.5 = ((bf16[32,12,2048]{2,1,0:T(8,128)(2,1)}), bf16[32,12,2048]{2,1,0:T(8,128)(2,1)}, u32[]{:S(2)}, u32[]{:S(2)}) async-start(bf16[32,12,2048]{2,1,0:T(8,128)(2,1)} %reshape.212), calls=%async_computation.5 | async-start | bytes 4194304 | tf_op jit(solution)/shard_map/all_to_all | solution.py:154
  185.6 34.6 %all-to-all-start.1 = ((bf16[32,12,2048]{2,1,0:T(8,128)(2,1)}), bf16[32,12,2048]{2,1,0:T(8,128)(2,1)}, u32[]{:S(2)}, u32[]{:S(2)}) async-start(bf16[32,12,2048]{2,1,0:T(8,128)(2,1)} %reshape.206), calls=%async_computation.1 | async-start | bytes 4194304 | tf_op jit(solution)/shard_map/all_to_all | solution.py:151
  197.7 5.1 %copy-start.2 = (bf16[1,128,2048]{2,1,0:T(8,128)(2,1)S(1)}, bf16[1,128,2048]{2,1,0:T(8,128)(2,1)}, u32[]{:S(2)}) copy-start(bf16[1,128,2048]{2,1,0:T(8,128)(2,1)} %param.14) | copy-start | bytes 1572868
  228.9 2.2 copy-start.3
  228.9 2.1 copy-start.4
  228.9 4.4 %copy-start.1 = (bf16[1,1,768,2048]{3,2,1,0:T(8,128)(2,1)S(1)}, bf16[1,1,768,2048]{3,2,1,0:T(8,128)(2,1)}, u32[]{:S(2)}) copy-start(bf16[1,1,768,2048]{3,2,1,0:T(8,128)(2,1)} %param.19) | copy-start | bytes 9437188
where the time goes:
time: 235 us; the launch traced here: 233 us
  waiting for transfers between devices  56.8 us (24%)
  starting transfers between devices  53.7 us (23%)
  matrix products  49.3 us (21%)
  local copies, waits for them, and re-layouts  48.9 us (21%)
  other arithmetic  23.6 us (10%)
    all_to_all x1, waiting for transfers between devices, body(): lax.all_to_all(buffer_b, 'expert', split_axis=0, concat_axis=0, tiled=True)  19.8 us
    all_to_all x1, waiting for transfers between devices, body(): lax.all_to_all(front_out.reshape(block_shape), 'expert', split_axis=0, co...  15.6 us
    dot_general x2, matrix products, expert_forward(): jnp.dot(hidden, down_mat, preferred_element_type=jnp.float32)  11.2 us
    dot_general x2, matrix products, expert_forward(): gate = jnp.dot(slot_rows, gate_mat, preferred_element_type=jnp.float32)  9.76 us
    all_to_all x1, waiting for transfers between devices, body(): lax.all_to_all(grad_buffer, 'expert', split_axis=0, concat_axis=0, tiled=...  9.43 us
    all_to_all x1, starting transfers between devices, body(): lax.all_to_all(scale_slots, 'expert', split_axis=0, concat_axis=0, tiled=...  8.04 us
    all_to_all x1, starting transfers between devices, body(): lax.all_to_all(back_grad.reshape(block_shape), 'expert', split_axis=0, co...  7.55 us
    all_to_all x1, starting transfers between devices, body(): lax.all_to_all(buffer_b, 'expert', split_axis=0, concat_axis=0, tiled=True)  7.24 us
  transfers between devices with their start and end apart: 9, of which 6 were waited for; matrix products, arithmetic and copies ran while one was open for 46% of the time, Pallas kernels for 0%

commit v1 on v0

v1 whole, which is shorter than its diff:
```python
import functools

import jax
import jax.numpy as jnp
from jax import lax
from jax.experimental import pallas as pl
from jax.experimental.pallas import tpu as pltpu
from jax.sharding import PartitionSpec as P

NORM_EPS = 1e-06
LOW = 8
HIGH = 4
F32 = jnp.float32
BF16 = jnp.bfloat16
NT = (((1,), (1,)), ((), ()))


def passed_along(value, axis, steps):
    count = lax.axis_size(axis)
    pairs = [(source, (source + steps) % count) for source in range(count)]
    return lax.ppermute(value, axis, pairs)


def mm(a, b):
    return jnp.dot(a, b, preferred_element_type=F32)


def mm_nt(a, b):
    return lax.dot_general(a, b, NT, preferred_element_type=F32)


def iota(shape, dim):
    return lax.broadcasted_iota(jnp.int32, shape, dim)


def normalized(tokens, gain_row):
    values = tokens.astype(F32)
    inverse = lax.rsqrt(jnp.mean(values * values, axis=-1, keepdims=True) + NORM_EPS)
    return (values * inverse * gain_row.astype(F32)).astype(BF16), inverse


def places(routes, experts):
    rows = routes.shape[0]
    columns = iota((rows, experts), 1)
    matches = [routes[:, k : k + 1] == columns for k in range(2)]
    named = jnp.where(matches[0] | matches[1], 1.0, 0.0).astype(BF16)
    before = (iota((rows, rows), 0) > iota((rows, rows), 1)).astype(F32).astype(BF16)
    earlier = mm(before, named)
    found = []
    for k in range(2):
        slot = jnp.sum(jnp.where(matches[k], earlier, 0.0), axis=1, keepdims=True).astype(jnp.int32)
        base = routes[:, k : k + 1] * LOW
        whole = jnp.where(slot < LOW, base + slot, -LOW)
        half = jnp.where(slot < LOW, -LOW, base + slot - LOW)
        found.append((whole, half, matches[k]))
    return found


def table(lanes, spots, scales):
    total = jnp.where(lanes == spots[0], scales[0], 0.0)
    return total + jnp.where(lanes == spots[1], scales[1], 0.0)


def pack(tokens, whole, left, right, out_ref, at):
    width = tokens.shape[1]
    half = width // 2
    out_ref[:, at : at + width] = mm(whole.T.astype(BF16), tokens).astype(BF16)
    both = mm(left.T.astype(BF16), tokens[:, :half]) + mm(right.T.astype(BF16), tokens[:, half:])
    out_ref[:, at + width : at + width + half] = both.astype(BF16)


def pack_stored(stored_ref, gain_ref, routes_ref, out_ref, *, experts):
    normed, _ = normalized(stored_ref[...], gain_ref[...])
    (w0, h0, _), (w1, h1, _) = places(routes_ref[...], experts)
    lanes = iota((normed.shape[0], experts * LOW), 1)
    ones = (1.0, 1.0)
    pack(
        normed,
        table(lanes, (w0, w1), ones),
        table(lanes, (h0, h1), ones),
        table(lanes, (h0 + HIGH, h1 + HIGH), ones),
        out_ref,
        0,
    )


def weights_of(normed, router_mat, found):
    logits = mm(normed, router_mat)
    sig = [
        jax.nn.sigmoid(jnp.sum(jnp.where(match, logits, 0.0), axis=1, keepdims=True))
        for _, _, match in found
    ]
    total = sig[0] + sig[1]
    return [s / total for s in sig], sig


def split(value):
    high = value.astype(BF16)
    return high, (value - high.astype(F32)).astype(BF16)


def pack_both(
    stored_ref, cotangent_ref, arrived_ref, gain_ref, router_ref, routes_b_ref, routes_f_ref,
    out_ref, tables_ref, scalars_ref, *, experts,
):
    gain_row = gain_ref[...]
    router_mat = router_ref[...]
    rows, width = stored_ref.shape
    lanes = iota((rows, experts * LOW), 1)
    span = experts * LOW
    saved = 0

    def save(value):
        nonlocal saved
        tables_ref[:, saved * span : (saved + 1) * span] = value.astype(BF16)
        saved += 1

    normed_b, inverse_b = normalized(stored_ref[...], gain_row)
    found_b = places(routes_b_ref[...], experts)
    weights_b, sig_b = weights_of(normed_b, router_mat, found_b)
    scales = [w.astype(BF16).astype(F32) for w in weights_b]
    (w0, h0, _), (w1, h1, _) = found_b
    pack(
        cotangent_ref[...],
        table(lanes, (w0, w1), scales),
        table(lanes, (h0, h1), scales),
        table(lanes, (h0 + HIGH, h1 + HIGH), scales),
        out_ref,
        0,
    )
    ones = (1.0, 1.0)
    save(table(lanes, (w0, w1), ones))
    save(table(lanes, (h0, h1), ones))
    save(table(lanes, (h0 + HIGH, h1 + HIGH), ones))
    for spot in (w0, w1, h0, h1):
        save(jnp.where(lanes == spot, 1.0, 0.0))

    normed_f, _ = normalized(arrived_ref[...], gain_row)
    found_f = places(routes_f_ref[...], experts)
    weights_f, _ = weights_of(normed_f, router_mat, found_f)
    (w0, h0, _), (w1, h1, _) = found_f
    spots = ((w0, w1), (h0, h1), (h0 + HIGH, h1 + HIGH))
    pack(normed_f, *(table(lanes, s, ones) for s in spots), out_ref, width + width // 2)
    for s in spots:
        for part in split(table(lanes, s, weights_f)):
            save(part)
    ratio = [jnp.where(s > 0.0, w / s, 1.0) for w, s in zip(weights_b, scales)]
    kept = [inverse_b, weights_b[0], weights_b[1], sig_b[0], sig_b[1], ratio[0], ratio[1]]
    at = iota((rows, 128), 1)
    scalars = jnp.zeros((rows, 128), F32)
    for i, value in enumerate(kept):
        scalars = jnp.where(at == i, value, scalars)
    scalars_ref[...] = scalars


def half_rows(part, count):
    i = iota((count * HIGH, count * LOW), 0)
    j = iota((count * HIGH, count * LOW), 1)
    left = 2 * i - (i & (HIGH - 1))
    take_left = (j == left).astype(F32).astype(BF16)
    take_right = (j == left + HIGH).astype(F32).astype(BF16)
    return mm(take_left, part).astype(BF16), mm(take_right, part).astype(BF16)


def half_tables(count):
    i = iota((count * LOW, count * HIGH), 1)
    j = iota((count * LOW, count * HIGH), 0)
    left = 2 * i - (i & (HIGH - 1))
    put_left = (j == left).astype(F32).astype(BF16)
    put_right = (j == left + HIGH).astype(F32).astype(BF16)
    return put_left, put_right


def spread(rows_ref, block, sources):
    low = sources * LOW
    width = rows_ref.shape[1]
    half = width // 2
    rows_ref[:low, :] = block[:, :width]
    left, right = half_rows(block[:, width:], sources)
    rows_ref[low:, :half] = left
    rows_ref[low:, half:] = right


def expert_stored(block_ref, gate_ref, up_ref, silu_ref, slope_ref, hidden_ref, rows_ref, *, sources):
    spread(rows_ref, block_ref[...], sources)
    rows = rows_ref[...]
    for f in range(0, gate_ref.shape[1], 256):
        gate = mm(rows, gate_ref[:, f : f + 256])
        up = mm(rows, up_ref[:, f : f + 256])
        sig = jax.nn.sigmoid(gate)
        silu = gate * sig
        silu_ref[:, f : f + 256] = silu
        slope_ref[:, f : f + 256] = up * sig * (1.0 + gate * (1.0 - sig))
        hidden_ref[:, f : f + 256] = (silu * up).astype(BF16)


def expert_both(
    block_ref, silu_ref, slope_ref, hidden_ref, gate_ref, up_ref, down_ref,
    out_ref, rows_ref, grad_gate_ref, grad_up_ref, made_ref, *, sources,
):
    low = sources * LOW
    width = rows_ref.shape[1]
    half = width // 2
    span = width + half
    inner = gate_ref.shape[1]
    put_left, put_right = half_tables(sources)

    def give(at, base):
        both = mm(put_left, made_ref[:, :half]) + mm(put_right, made_ref[:, half:])
        out_ref[:, at + width : at + span] = both.astype(BF16)

    block = block_ref[:, :span]
    spread(rows_ref, block, sources)
    rows = rows_ref[...]
    scores = jnp.zeros((rows.shape[0], 1), F32)
    for f in range(0, inner, 256):
        grad_hidden = mm_nt(rows, down_ref[f : f + 256, :])
        scores += jnp.sum(grad_hidden * hidden_ref[:, f : f + 256].astype(F32), axis=1, keepdims=True)
        grad_up_ref[:, f : f + 256] = (grad_hidden * silu_ref[:, f : f + 256]).astype(BF16)
        grad_gate_ref[:, f : f + 256] = (grad_hidden * slope_ref[:, f : f + 256]).astype(BF16)
    grad_gate = grad_gate_ref[...]
    grad_up = grad_up_ref[...]
    for n in range(0, width, 512):
        made = mm_nt(grad_gate, gate_ref[n : n + 512, :]) + mm_nt(grad_up, up_ref[n : n + 512, :])
        made = made.astype(BF16)
        out_ref[:, n : n + 512] = made[:low]
        made_ref[:, n : n + 512] = made[low:]
    give(0, 0)
    at = iota((low, 128), 1)
    high, rest = split(scores)
    zero = jnp.zeros((low, 128), F32)
    tail = jnp.where(at == 0, high[:low].astype(F32), jnp.where(at == 1, rest[:low].astype(F32), zero))
    at = iota((low // 2, 128), 1)
    zero = jnp.zeros((low // 2, 128), F32)
    more = jnp.where(at == 2, high[low:].astype(F32), jnp.where(at == 3, rest[low:].astype(F32), zero))
    tail = tail + mm(put_left, more.astype(BF16))
    out_ref[:, 2 * span : 2 * span + 128] = tail.astype(BF16)

    spread(rows_ref, block_ref[:, span:], sources)
    rows = rows_ref[...]
    for f in range(0, inner, 256):
        gate = mm(rows, gate_ref[:, f : f + 256])
        up = mm(rows, up_ref[:, f : f + 256])
        grad_up_ref[:, f : f + 256] = (gate * jax.nn.sigmoid(gate) * up).astype(BF16)
    hidden = grad_up_ref[...]
    for n in range(0, width, 512):
        made = mm(hidden, down_ref[:, n : n + 512]).astype(BF16)
        out_ref[:, span + n : span + n + 512] = made[:low]
        made_ref[:, n : n + 512] = made[low:]
    give(span, 0)


def combine(
    back_ref, tables_ref, scalars_ref, arrived_ref, stored_ref, cotangent_ref, gain_ref, router_ref, routes_ref,
    layer_ref, grad_ref, *, experts,
):
    rows, width = arrived_ref.shape
    half = width // 2
    span = width + half
    slots = experts * LOW

    def t(i):
        return tables_ref[:, i * slots : (i + 1) * slots]

    for s, side in ((0, 9), (1, 11)):
        cols = slice(s * half, (s + 1) * half)
        low = back_ref[:, span + s * half : span + (s + 1) * half]
        high = back_ref[:, span + width : 2 * span]
        mixed = mm(t(7), low) + mm(t(8), low) + mm(t(side), high) + mm(t(side + 1), high)
        layer_ref[:, cols] = (arrived_ref[:, cols].astype(F32) + mixed).astype(BF16)

    inverse, w0, w1, s0, s1, r0, r1 = (scalars_ref[:, i : i + 1] for i in range(7))
    extra = back_ref[:, 2 * span : 2 * span + 128]
    u = []
    for k, ratio in ((0, r0), (1, r1)):
        got = mm(t(3 + k), extra)
        more = mm(t(5 + k), extra)
        u.append((got[:, 0:1] + got[:, 1:2] + more[:, 2:3] + more[:, 3:4]) * ratio)
    cross = u[0] * w1 - w0 * u[1]
    columns = iota((rows, experts), 1)
    picks = jnp.where(routes_ref[:, 0:1] == columns, cross * (1.0 - s0), 0.0)
    picks = picks - jnp.where(routes_ref[:, 1:2] == columns, cross * (1.0 - s1), 0.0)
    p0, p1 = split(picks)
    p2 = (picks - p0.astype(F32) - p1.astype(F32)).astype(BF16)

    total = jnp.zeros((rows, 1), F32)
    scaled = []
    for s in range(2):
        cols = slice(s * half, (s + 1) * half)
        high = back_ref[:, width : span]
        grad = mm(t(0), back_ref[:, cols]) + mm(t(1 + s), high)
        router_cols = router_ref[cols, :]
        grad = grad + mm_nt(p0, router_cols) + mm_nt(p1, router_cols) + mm_nt(p2, router_cols)
        grad = grad * gain_ref[:, cols].astype(F32)
        total += jnp.sum(grad * stored_ref[:, cols].astype(F32), axis=1, keepdims=True)
        scaled.append(grad)
    pull = inverse * inverse * inverse * (total / width)
    for s in range(2):
        cols = slice(s * half, (s + 1) * half)
        value = cotangent_ref[:, cols].astype(F32) + inverse * scaled[s]
        grad_ref[:, cols] = (value - stored_ref[:, cols].astype(F32) * pull).astype(BF16)


def call(kernel, outs, scratch=(), limit=48, flops=0, moved=0):
    return pl.pallas_call(
        kernel,
        out_shape=outs,
        scratch_shapes=list(scratch),
        compiler_params=pltpu.CompilerParams(vmem_limit_bytes=limit * 2**20),
        cost_estimate=pl.CostEstimate(flops=flops, bytes_accessed=moved, transcendentals=0),
    )


def body(
    activations, gradients, stashed, norm_gain, router, gate_weight, up_weight, down_weight, routes_forward, routes_backward
):
    shape = jax.ShapeDtypeStruct
    experts = lax.axis_size("expert")
    rows, width = stashed.shape[1:]
    span = width + width // 2
    inner = gate_weight.shape[3]
    low, slots = experts * LOW, experts * (LOW + HIGH)
    gate_mat, up_mat, down_mat = gate_weight[0, 0], up_weight[0, 0], down_weight[0, 0]
    router_mat, stored = router[0], stashed[0]
    routes_f, routes_b = routes_forward[0], routes_backward[0]

    def exchange(block):
        blocks = block.reshape(experts, LOW, block.shape[1])
        return lax.all_to_all(blocks, "expert", split_axis=0, concat_axis=0, tiled=True).reshape(block.shape)

    arrived = passed_along(activations, "section", 1)[0]
    cotangent = passed_along(gradients, "section", -1)[0]

    sent_b = call(
        functools.partial(pack_stored, experts=experts), shape((low, span), BF16), flops=4 * low * rows * width, moved=2**22
    )(stored, norm_gain, routes_b)
    got_b = exchange(sent_b)
    sent, tables, scalars = call(
        functools.partial(pack_both, experts=experts),
        (shape((low, 2 * span), BF16), shape((rows, 13 * low), BF16), shape((rows, 128), F32)),
        flops=10 * low * rows * width,
        moved=2**23,
    )(stored, cotangent, arrived, norm_gain, router_mat, routes_b, routes_f)
    got = exchange(sent)
    silu, slope, hidden = call(
        functools.partial(expert_stored, sources=experts),
        (shape((slots, inner), F32), shape((slots, inner), F32), shape((slots, inner), BF16)),
        scratch=[pltpu.VMEM((slots, width), BF16)],
        flops=4 * slots * width * inner,
        moved=2**24,
    )(got_b, gate_mat, up_mat)
    made = call(
        functools.partial(expert_both, sources=experts),
        shape((low, 2 * span + 128), BF16),
        scratch=[
            pltpu.VMEM((slots, width), BF16),
            pltpu.VMEM((slots, inner), BF16),
            pltpu.VMEM((slots, inner), BF16),
            pltpu.VMEM((slots - low, width), BF16),
        ],
        flops=12 * slots * width * inner,
        moved=2**24,
    )(got, silu, slope, hidden, gate_mat, up_mat, down_mat)
    back = exchange(made)
    layer_out, input_grad = call(
        functools.partial(combine, experts=experts),
        (shape((rows, width), BF16), shape((rows, width), BF16)),
        flops=20 * low * rows * width,
        moved=2**23,
    )(back, tables, scalars, arrived, stored, cotangent, norm_gain, router_mat, routes_b)
    return layer_out[None], input_grad[None]


def solution(mesh):
    spread_rows = P("section", "expert", None)
    weights = P("section", "expert", None, None)
    placed = (
        spread_rows,
        spread_rows,
        spread_rows,
        P("section", None),
        P("section", None, None),
        weights,
        weights,
        weights,
        spread_rows,
        spread_rows,
    )
    return jax.shard_map(body, mesh=mesh, in_specs=placed, out_specs=(spread_rows, spread_rows), check_vma=False)
```

time: 235 us -> 159 us (0.68)
  matrix products: 49.3 us -> 0 us
  blocking collectives: 0 us -> 48.4 us
  local copies, waits for them, and re-layouts: 48.9 us -> 12.9 us
  Pallas kernels: 0 us -> 33 us
  starting transfers between devices: 53.7 us -> 22.1 us
  other arithmetic: 23.6 us -> 0 us
  waiting for transfers between devices: 56.8 us -> 41.2 us
    dot_general x14 -> x0, matrix products: 49.3 us -> none  [the longest x2 11.2 us: expert_forward(): jnp.dot(hidden, down_mat, preferred_element_type=jnp.float32)]
    all_to_all x0 -> x1, blocking collectives: none -> 48.4 us  [exchange(): lax.all_to_all(blocks, 'expert', split_axis=0, concat_axis=0, tiled=True)]
    reshape x12 -> x0, local copies, waits for them, and re-layouts: 37.7 us -> none  [the longest x1 3.67 us: body(): front_rows.reshape(-1, model_width)]
    pallas_call x0 -> x5, Pallas kernels: none -> 33 us  [the longest x1 14.8 us: body(): call(functools.partial(expert_both, sources=experts), shape((low, 2 * spa...]
    all_to_all x7 -> x2, starting transfers between devices: 47.1 us -> 16.4 us  [exchange(): lax.all_to_all(blocks, 'expert', split_axis=0, concat_axis=0, tiled=True)]
    all_to_all x7 -> x2, waiting for transfers between devices: 56.8 us -> 29.4 us  [exchange(): lax.all_to_all(blocks, 'expert', split_axis=0, concat_axis=0, tiled=True)]
    reduce_sum x17 -> x0, other arithmetic: 13.5 us -> none  [the longest x1 5.14 us: body(): grad_normed = jnp.sum(picked_dn.astype(jnp.float32), axis=1)]
    unnamed x26 -> x45, local copies, waits for them, and re-layouts: 1.09 us -> 12.9 us
  transfers between devices with their start and end apart: 9 -> 4, of which waited for: 6 -> 2; matrix products, arithmetic and copies ran while one was open for 46% -> 0% of each run, Pallas kernels for 0% -> 7%
where the time goes in v1:
time: 159 us; the launch traced here: 158 us
  blocking collectives  48.4 us (30%)
  waiting for transfers between devices  41.2 us (26%)
  Pallas kernels  33 us (21%)
  starting transfers between devices  22.1 us (14%)
  local copies, waits for them, and re-layouts  12.9 us (8%)
    all_to_all x1, blocking collectives, exchange(): lax.all_to_all(blocks, 'expert', split_axis=0, concat_axis=0, tiled=True)  48.4 us
    all_to_all x2, waiting for transfers between devices, exchange(): lax.all_to_all(blocks, 'expert', split_axis=0, concat_axis=0, tiled=True)  29.4 us
    all_to_all x2, starting transfers between devices, exchange(): lax.all_to_all(blocks, 'expert', split_axis=0, concat_axis=0, tiled=True)  16.4 us
    pallas_call x1, Pallas kernels, body(): call(functools.partial(expert_both, sources=experts), shape((low, 2 * spa...  14.8 us
    unnamed x45, local copies, waits for them, and re-layouts  12.9 us
    ppermute x2, waiting for transfers between devices, passed_along(): return lax.ppermute(value, axis, pairs)  11.8 us
    ppermute x2, starting transfers between devices, passed_along(): return lax.ppermute(value, axis, pairs)  5.74 us
    pallas_call x1, Pallas kernels, body(): call(functools.partial(expert_stored, sources=experts), (shape((slots, in...  5.67 us
  transfers between devices with their start and end apart: 4, of which 2 were waited for; matrix products, arithmetic and copies ran while one was open for 0% of the time, Pallas kernels for 7%

profile of v1, /device:TPU:1, one launch (start us, length us, event | category | flops | bytes accessed | tf_op | source)
XLA Modules:
  0.0 158.4 jit_solution(14914098127915157484)
XLA Ops:
  0.6 0.0 copy-start.12
  0.6 0.0 copy-start.20
  0.7 0.8 copy.13
  1.5 1.0 copy-done.2
  2.5 0.7 copy-done.11
  3.2 2.4 %shard_map.114 = bf16[256,3072]{1,0:T(8,128)(2,1)} custom-call(bf16[128,2048]{1,0:T(8,128)(2,1)S(1)} %bitcast.20, bf16[1,2048]{1,0:T(2,128)(2,1)S(1)} %copy-done.11, s32[128,2]{1,0:T(8,128)S(1)} %bitcast.24), custom_call_target="tpu_custom_call" | custom-call | flops 268435456 | bytes 4194304 | tf_op jit(solution)/shard_map/pallas_call | solution.py:334
  5.6 8.6 %all-to-all-start.1 = ((bf16[32,8,3072]{2,1,0:T(8,128)(2,1)}), bf16[32,8,3072]{2,1,0:T(8,128)(2,1)S(1)}, u32[]{:S(2)}, u32[]{:S(2)}) async-start(bf16[32,8,3072]{2,1,0:T(8,128)(2,1)} %bitcast.8), calls=%async_computation.1 | async-start | bytes 3145728 | tf_op jit(solution)/shard_map/all_to_all | solution.py:329
  14.2 1.7 %collective-permute-start.1 = (bf16[1,128,2048]{2,1,0:T(8,128)(2,1)}, bf16[1,128,2048]{2,1,0:T(8,128)(2,1)S(1)}, u32[]{:S(2)}, u32[]{:S(2)}) collective-permute-start(bf16[1,128,2048]{2,1,0:T(8,128)(2,1)} %param.10), channel_id=1, source_target_pairs={{0,32},{32,64},{64,96},{96,128},{128,160},{160,192},{192,224},{224... | collective-permute-start | bytes 1572872 | tf_op jit(solution)/shard_map/ppermute | solution.py:21
  15.9 4.0 %collective-permute-start = (bf16[1,128,2048]{2,1,0:T(8,128)(2,1)}, bf16[1,128,2048]{2,1,0:T(8,128)(2,1)}, u32[]{:S(2)}, u32[]{:S(2)}) collective-permute-start(bf16[1,128,2048]{2,1,0:T(8,128)(2,1)} %param.11), channel_id=1, source_target_pairs={{0,224},{32,0},{64,32},{96,64},{128,96},{160,128},{192,160},{224,1... | collective-permute-start | bytes 1572872 | tf_op jit(solution)/shard_map/ppermute | solution.py:21
  19.9 0.0 copy-done.20
  19.9 0.1 copy.14
  20.0 0.3 copy.12
  20.3 0.0 copy-start
  20.3 11.8 %collective-permute-done.1 = bf16[1,128,2048]{2,1,0:T(8,128)(2,1)S(1)} collective-permute-done((bf16[1,128,2048]{2,1,0:T(8,128)(2,1)}, bf16[1,128,2048]{2,1,0:T(8,128)(2,1)S(1)}, u32[]{:S(2)}, u32[]{:S(2)}) %collective-permute-start.1) | collective-permute-done | bytes 524320 | tf_op jit(solution)/shard_map/ppermute | solution.py:21
  32.1 0.0 collective-permute-done
  32.1 5.3 %shard_map.113 = (bf16[256,6144]{1,0:T(8,128)(2,1)}, bf16[128,3328]{1,0:T(8,128)(2,1)S(1)}, f32[128,128]{1,0:T(8,128)S(1)}) custom-call(bf16[128,2048]{1,0:T(8,128)(2,1)S(1)} %bitcast.21, bf16[128,2048]{1,0:T(8,128)(2,1)} %bitcast.1.cotangent_ref, bf16[128,2048]{1,0:T(8,128)(2,1)S(1)} %bitcast.27, bf16[1,2048]{1,0:T(2,128)(2,1)S(1)} %copy-done.12, ...), custom_call_target="tpu_custom_call" | custom-call | flops 671088640 | bytes 8388608 | tf_op jit(solution)/shard_map/pallas_call | solution.py:338
  37.4 0.9 copy-done.7
  38.3 0.0 all-to-all-done.1
  38.3 1.2 copy-done.5
  39.4 7.8 %all-to-all-start = ((bf16[32,8,6144]{2,1,0:T(8,128)(2,1)}), bf16[32,8,6144]{2,1,0:T(8,128)(2,1)S(1)}, u32[]{:S(2)}, u32[]{:S(2)}) async-start(bf16[32,8,6144]{2,1,0:T(8,128)(2,1)} %bitcast.32), calls=%async_computation | async-start | bytes 6291456 | tf_op jit(solution)/shard_map/all_to_all | solution.py:329
  47.3 1.4 copy-done.6
  48.7 5.7 %shard_map.115 = (f32[384,768]{1,0:T(8,128)S(1)}, f32[384,768]{1,0:T(8,128)S(1)}, bf16[384,768]{1,0:T(8,128)(2,1)S(1)}) custom-call(bf16[256,3072]{1,0:T(8,128)(2,1)S(1)} %bitcast.23, bf16[2048,768]{1,0:T(8,128)(2,1)} %bitcast.33, bf16[2048,768]{1,0:T(8,128)(2,1)} %bitcast.35), custom_call_target="tpu_custom_call" | custom-call | flops 2415919104 | bytes 16777216 | tf_op jit(solution)/shard_map/pallas_call | solution.py:345
  54.4 1.0 copy-done.13
  55.4 1.1 copy-done.15
  56.4 0.8 copy-done.17
  57.3 29.4 %all-to-all-done = bf16[32,8,6144]{2,1,0:T(8,128)(2,1)S(1)} async-done(((bf16[32,8,6144]{2,1,0:T(8,128)(2,1)}), bf16[32,8,6144]{2,1,0:T(8,128)(2,1)S(1)}, u32[]{:S(2)}, u32[]{:S(2)}) %all-to-all-start) | async-done | bytes 3145760 | tf_op jit(solution)/shard_map/all_to_all | solution.py:329
  86.7 1.3 copy-done.14
  87.9 1.3 copy-done.16
  89.2 1.1 copy-done.18
  90.3 14.8 %shard_map.116 = bf16[256,6272]{1,0:T(8,128)(2,1)} custom-call(bf16[256,6144]{1,0:T(8,128)(2,1)S(1)} %bitcast.17, f32[384,768]{1,0:T(8,128)S(1)} %copy-done.14, f32[384,768]{1,0:T(8,128)S(1)} %copy-done.16, bf16[384,768]{1,0:T(8,128)(2,1)S(1)} %copy-done.18, bf16[2048,768]{1,0:T(8,128)(2,1)} %bitcast.34, bf16[2048,768]{1,0:T(8,128)(2,1)} %bitcast.36, ...), custom_call_target="tpu_custom_call" | custom-call | flops 7247757312 | bytes 16777216 | tf_op jit(solution)/shard_map/pallas_call | solution.py:352
  105.1 48.4 %all_to_all.15 = bf16[32,8,6272]{2,1,0:T(8,128)(2,1)} all-to-all(bf16[32,8,6272]{2,1,0:T(8,128)(2,1)} %bitcast.31), channel_id=1, replica_groups=mesh['section'=8,'expert'=32] {'expert'}, dimensions={0} | all-to-all | bytes 6422528 | tf_op jit(solution)/shard_map/all_to_all | solution.py:329
  153.5 4.9 %shard_map.117 = (bf16[128,2048]{1,0:T(8,128)(2,1)}, bf16[128,2048]{1,0:T(8,128)(2,1)}) custom-call(bf16[256,6272]{1,0:T(8,128)(2,1)} %bitcast.30, bf16[128,3328]{1,0:T(8,128)(2,1)S(1)} %copy-done.8, f32[128,128]{1,0:T(8,128)S(1)} %get-tuple-element.15.scalars_ref, bf16[128,2048]{1,0:T(8,128)(2,1)S(1)} %bitcast.28, bf16[128,2048]{1,0:T(8,128)(2,1)S(1)} %bitcast.22, ...), custom_call_target="tpu_custom_call" | custom-call | flops 1342177280 | bytes 8388608 | tf_op jit(solution)/shard_map/pallas_call | solution.py:365
  (27 shorter events, 0.0 us)
Async XLA Ops:
  0.6 31.5 %copy-start.12 = (bf16[1,2048]{1,0:T(2,128)(2,1)S(1)}, bf16[1,2048]{1,0:T(2,128)(2,1)}, u32[]{:S(2)}) copy-start(bf16[1,2048]{1,0:T(2,128)(2,1)} %gain_ref.5) | copy-start | bytes 12292
  0.6 19.3 %copy-start.20 = (s32[1,128,2]{1,2,0:T(2,128)S(1)}, s32[1,128,2]{1,2,0:T(2,128)}, u32[]{:S(2)}) copy-start(s32[1,128,2]{1,2,0:T(2,128)} %param.18) | copy-start | bytes 3076
  1.4 1.0 copy-start.2
  2.5 0.7 copy-start.11
  3.2 16.8 %copy-start.19 = (bf16[1,2048,32]{1,2,0:T(8,128)(2,1)S(1)}, bf16[1,2048,32]{1,2,0:T(8,128)(2,1)}, u32[]{:S(2)}) copy-start(bf16[1,2048,32]{1,2,0:T(8,128)(2,1)} %param.14) | copy-start | bytes 393220
  3.2 28.9 %copy-start.3 = (bf16[1,128,2048]{2,1,0:T(8,128)(2,1)S(1)}, bf16[1,128,2048]{2,1,0:T(8,128)(2,1)}, u32[]{:S(2)}) copy-start(bf16[1,128,2048]{2,1,0:T(8,128)(2,1)} %param.12) | copy-start | bytes 1572868
  5.6 32.7 %all-to-all-start.1 = ((bf16[32,8,3072]{2,1,0:T(8,128)(2,1)}), bf16[32,8,3072]{2,1,0:T(8,128)(2,1)S(1)}, u32[]{:S(2)}, u32[]{:S(2)}) async-start(bf16[32,8,3072]{2,1,0:T(8,128)(2,1)} %bitcast.8), calls=%async_computation.1 | async-start | bytes 3145728 | tf_op jit(solution)/shard_map/all_to_all | solution.py:329
  14.2 17.9 %collective-permute-start.1 = (bf16[1,128,2048]{2,1,0:T(8,128)(2,1)}, bf16[1,128,2048]{2,1,0:T(8,128)(2,1)S(1)}, u32[]{:S(2)}, u32[]{:S(2)}) collective-permute-start(bf16[1,128,2048]{2,1,0:T(8,128)(2,1)} %param.10), channel_id=1, source_target_pairs={{0,32},{32,64},{64,96},{96,128},{128,160},{160,192},{192,224},{224... | collective-permute-start | bytes 1572872 | tf_op jit(solution)/shard_map/ppermute | solution.py:21
  15.9 16.2 %collective-permute-start = (bf16[1,128,2048]{2,1,0:T(8,128)(2,1)}, bf16[1,128,2048]{2,1,0:T(8,128)(2,1)}, u32[]{:S(2)}, u32[]{:S(2)}) collective-permute-start(bf16[1,128,2048]{2,1,0:T(8,128)(2,1)} %param.11), channel_id=1, source_target_pairs={{0,224},{32,0},{64,32},{96,64},{128,96},{160,128},{192,160},{224,1... | collective-permute-start | bytes 1572872 | tf_op jit(solution)/shard_map/ppermute | solution.py:21
  20.3 19.1 %copy-start = (bf16[1,2048,32]{2,1,0:T(8,128)(2,1)}, bf16[1,2048,32]{2,1,0:T(8,128)(2,1)S(1)}, u32[]{:S(2)}) copy-start(bf16[1,2048,32]{2,1,0:T(8,128)(2,1)S(1)} %copy.12) | copy-start | bytes 393220
  32.1 7.4 %copy-start.9 = (bf16[1,128,2048]{2,1,0:T(8,128)(2,1)}, bf16[1,128,2048]{2,1,0:T(8,128)(2,1)S(1)}, u32[]{:S(2)}) copy-start(bf16[1,128,2048]{2,1,0:T(8,128)(2,1)S(1)} %collective-permute-done.1) | copy-start | bytes 1572868
  37.4 0.9 copy-start.7
  38.3 1.2 copy-start.5
  39.4 47.2 %all-to-all-start = ((bf16[32,8,6144]{2,1,0:T(8,128)(2,1)}), bf16[32,8,6144]{2,1,0:T(8,128)(2,1)S(1)}, u32[]{:S(2)}, u32[]{:S(2)}) async-start(bf16[32,8,6144]{2,1,0:T(8,128)(2,1)} %bitcast.32), calls=%async_computation | async-start | bytes 6291456 | tf_op jit(solution)/shard_map/all_to_all | solution.py:329
  47.3 1.4 copy-start.6
  54.4 1.0 copy-start.13
  55.4 1.1 copy-start.15
  56.4 0.8 copy-start.17
  86.7 1.3 copy-start.14
  87.9 1.3 copy-start.16
  89.2 1.1 copy-start.18
  105.0 48.4 %copy-start.1 = (bf16[1,2048,32]{2,1,0:T(8,128)(2,1)S(1)}, bf16[1,2048,32]{2,1,0:T(8,128)(2,1)}, u32[]{:S(2)}) copy-start(bf16[1,2048,32]{2,1,0:T(8,128)(2,1)} %copy-done) | copy-start | bytes 393220
  105.0 48.4 %copy-start.4 = (bf16[1,128,2048]{2,1,0:T(8,128)(2,1)S(1)}, bf16[1,128,2048]{2,1,0:T(8,128)(2,1)}, u32[]{:S(2)}) copy-start(bf16[1,128,2048]{2,1,0:T(8,128)(2,1)} %param.12) | copy-start | bytes 1572868
  105.0 48.4 %copy-start.8 = (bf16[128,3328]{1,0:T(8,128)(2,1)S(1)}, bf16[128,3328]{1,0:T(8,128)(2,1)}, u32[]{:S(2)}) copy-start(bf16[128,3328]{1,0:T(8,128)(2,1)} %copy-done.7) | copy-start | bytes 2555908
  105.0 48.4 %copy-start.10 = (bf16[1,128,2048]{2,1,0:T(8,128)(2,1)S(1)}, bf16[1,128,2048]{2,1,0:T(8,128)(2,1)}, u32[]{:S(2)}) copy-start(bf16[1,128,2048]{2,1,0:T(8,128)(2,1)} %copy-done.9) | copy-start | bytes 1572868

commit v2 on v1

v2 whole, which is shorter than its diff:
```python
import functools

import jax
import jax.numpy as jnp
from jax import lax
from jax.experimental import pallas as pl
from jax.experimental.pallas import tpu as pltpu
from jax.sharding import PartitionSpec as P


NORM_EPS = 1e-06
LOW = 8
HIGH = 4
F32 = jnp.float32
BF16 = jnp.bfloat16
NT = (((1,), (1,)), ((), ()))
ANY = pl.BlockSpec(memory_space=pl.ANY)
HBM = pl.BlockSpec(memory_space=pltpu.HBM)
VMEM = pl.BlockSpec(memory_space=pltpu.VMEM)


def passed_along(value, axis, steps):
    count = lax.axis_size(axis)
    pairs = [(source, (source + steps) % count) for source in range(count)]
    return lax.ppermute(value, axis, pairs)


def mm(a, b):
    return jnp.dot(a, b, preferred_element_type=F32)


def mm_nt(a, b):
    return lax.dot_general(a, b, NT, preferred_element_type=F32)


def iota(shape, dim):
    return lax.broadcasted_iota(jnp.int32, shape, dim)


def mask(condition):
    return condition.astype(F32).astype(BF16)


class Copies:
    def __init__(self, sems):
        self.sems = sems
        self.used = 0

    def start(self, source, target):
        copy = pltpu.make_async_copy(source, target, self.sems.at[self.used])
        self.used += 1
        copy.start()
        return copy


def normalized(tokens, gain_row):
    values = tokens.astype(F32)
    inverse = lax.rsqrt(jnp.mean(values * values, axis=-1, keepdims=True) + NORM_EPS)
    return (values * inverse * gain_row.astype(F32)).astype(BF16), inverse


def places(routes, experts):
    count = routes.shape[1]
    experts_at = iota((experts, count), 0)
    matches = [routes[k : k + 1, :] == experts_at for k in range(2)]
    named = mask(matches[0] | matches[1])
    earlier = mm(named, mask(iota((count, count), 0) < iota((count, count), 1)))
    found = []
    for k in range(2):
        slot = jnp.sum(jnp.where(matches[k], earlier, 0.0), axis=0, keepdims=True).astype(jnp.int32)
        base = routes[k : k + 1, :] * LOW
        whole = jnp.where(slot < LOW, base + slot, -LOW)
        half = jnp.where(slot < LOW, -LOW, base + slot - LOW)
        found.append((whole, half, matches[k]))
    return found


def spots_of(found):
    (w0, h0, _), (w1, h1, _) = found
    return (w0, w1), (h0, h1), (h0 + HIGH, h1 + HIGH)


def table(at, spots, scales=(1.0, 1.0)):
    total = jnp.where(at == spots[0], scales[0], 0.0)
    return total + jnp.where(at == spots[1], scales[1], 0.0)


def pack(tokens, tables, made_ref, out_ref, at, copies):
    whole, left, right = (t.astype(BF16) for t in tables)
    half = tokens.shape[1] // 2
    running = []

    def give(value, column):
        cols = slice(at + column, at + column + half)
        made_ref[:, cols] = value.astype(BF16)
        running.append(copies.start(made_ref.at[:, cols], out_ref.at[:, cols]))

    give(mm(whole, tokens[:, :half]), 0)
    give(mm(whole, tokens[:, half:]), half)
    give(mm(left, tokens[:, :half]) + mm(right, tokens[:, half:]), 2 * half)
    return running


def pack_stored(stored_ref, gain_ref, routes_ref, out_ref, made_ref, sems, *, experts):
    found = places(routes_ref[...], experts)
    at = iota((experts * LOW, routes_ref.shape[1]), 0)
    normed, _ = normalized(stored_ref[...], gain_ref[...])
    for copy in pack(normed, [table(at, s) for s in spots_of(found)], made_ref, out_ref, 0, Copies(sems)):
        copy.wait()


def weights_of(normed, router_rows, found):
    logits = mm_nt(router_rows, normed)
    sig = [
        jax.nn.sigmoid(jnp.sum(jnp.where(match, logits, 0.0), axis=0, keepdims=True))
        for _, _, match in found
    ]
    total = sig[0] + sig[1]
    return [s / total for s in sig], sig


def split(value):
    high = value.astype(BF16)
    return high, (value - high.astype(F32)).astype(BF16)


def pack_both(
    stored_ref, cotangent_ref, arrived_ref, gain_ref, router_ref, routes_b_ref, routes_f_ref,
    out_ref, tables_ref, scalars_ref, made_ref, sems, *, experts,
):
    gain_row = gain_ref[...]
    router_rows = router_ref[...]
    rows, width = stored_ref.shape
    span = experts * LOW
    at = iota((span, rows), 0)
    copies = Copies(sems)

    normed_b, inverse_b = normalized(stored_ref[...], gain_row)
    found_b = places(routes_b_ref[...], experts)
    weights_b, sig_b = weights_of(normed_b, router_rows, found_b)
    scales = [w.astype(BF16).astype(F32) for w in weights_b]
    spots_b = spots_of(found_b)
    running = pack(cotangent_ref[...], [table(at, s, scales) for s in spots_b], made_ref, out_ref, 0, copies)
    normed_f, _ = normalized(arrived_ref[...], gain_row)
    found_f = places(routes_f_ref[...], experts)
    spots_f = spots_of(found_f)
    running += pack(normed_f, [table(at, s) for s in spots_f], made_ref, out_ref, width + width // 2, copies)
    weights_f, _ = weights_of(normed_f, router_rows, found_f)

    kept = [table(at, s) for s in spots_b]
    kept += [jnp.where(at == s, 1.0, 0.0) for s in (*spots_b[0], *spots_b[1])]
    for s in spots_f:
        kept += [part.astype(F32) for part in split(table(at, s, weights_f))]
    for i, value in enumerate(kept):
        tables_ref[:, i * span : (i + 1) * span] = value.T.astype(BF16)

    ratio = [jnp.where(s > 0.0, w / s, 1.0) for w, s in zip(weights_b, scales)]
    routes_b = routes_b_ref[...].astype(F32)
    lines = [*weights_b, *sig_b, *ratio, routes_b[0:1], routes_b[1:2]]
    line_at = iota((rows, rows), 0)
    scalars = jnp.zeros((rows, rows), F32)
    for i, value in enumerate(lines):
        scalars = jnp.where(line_at == i, value, scalars)
    scalars_ref[...] = jnp.where(iota((rows, rows), 1) == len(lines), inverse_b, scalars.T)
    for copy in running:
        copy.wait()


def half_places(count):
    i = iota((count * HIGH, count * LOW), 0)
    j = iota((count * HIGH, count * LOW), 1)
    left = 2 * i - (i & (HIGH - 1))
    return mask(j == left), mask(j == left + HIGH)


def half_homes(count):
    i = iota((count * LOW, count * HIGH), 1)
    j = iota((count * LOW, count * HIGH), 0)
    left = 2 * i - (i & (HIGH - 1))
    return mask(j == left), mask(j == left + HIGH)


def join_halves(rows_ref, part, sources):
    low = sources * LOW
    half = rows_ref.shape[1] // 2
    take_left, take_right = half_places(sources)
    rows_ref[low:, :half] = mm(take_left, part).astype(BF16)
    rows_ref[low:, half:] = mm(take_right, part).astype(BF16)


def expert_stored(block_ref, gate_ref, up_ref, kept_ref, rows_ref, *, sources):
    low = sources * LOW
    width = rows_ref.shape[1]
    rows_ref[:low, :] = block_ref[:, :width]
    join_halves(rows_ref, block_ref[:, width:], sources)
    rows = rows_ref[...]
    for f in range(0, gate_ref.shape[1], 256):
        gate = mm(rows, gate_ref[:, f : f + 256])
        up = mm(rows, up_ref[:, f : f + 256])
        sig = jax.nn.sigmoid(gate)
        silu = gate * sig
        kept_ref[:, f * 3 : f * 3 + 256] = silu
        kept_ref[:, f * 3 + 256 : f * 3 + 512] = up * sig * (1.0 + gate * (1.0 - sig))
        kept_ref[:, f * 3 + 512 : f * 3 + 768] = (silu * up).astype(BF16).astype(F32)


def expert_both(
    block_any, kept_any, gate_any, up_any, down_any, out_any,
    rows_b, half_b, rows_f, half_f, kept_ref, gate_ref, up_ref, down_ref, grad_gate_ref, grad_up_ref, made_ref, out_ref, sems, *, sources,
):
    low = sources * LOW
    width = rows_b.shape[1]
    half = width // 2
    span = width + half
    inner = gate_ref.shape[1]
    step = 256
    wide = 512
    copies = Copies(sems)
    part_b = copies.start(block_any.at[:, width:span], half_b)
    low_b = copies.start(block_any.at[:, :width], rows_b.at[:low, :])
    downs = []
    helds = []
    for f in range(0, inner, step):
        downs.append(copies.start(down_any.at[f : f + step, :], down_ref.at[f : f + step, :]))
        cols = slice(3 * f, 3 * f + 3 * step)
        helds.append(copies.start(kept_any.at[:, cols], kept_ref.at[:, cols]))
    put_left, put_right = half_homes(sources)
    part_b.wait()
    join_halves(rows_b, half_b[...], sources)
    low_b.wait()
    gates = []
    ups = []

    rows = rows_b[...]
    scores = jnp.zeros((rows.shape[0], 1), F32)
    for i, f in enumerate(range(0, inner, step)):
        downs[i].wait()
        grad_hidden = mm_nt(rows, down_ref[f : f + step, :])
        helds[i].wait()
        if i == len(range(0, inner, step)) - 1:
            for n in range(0, width, wide):
                gates.append(copies.start(gate_any.at[n : n + wide, :], gate_ref.at[n : n + wide, :]))
                ups.append(copies.start(up_any.at[n : n + wide, :], up_ref.at[n : n + wide, :]))
            part_f = copies.start(block_any.at[:, span + width :], half_f)
            low_f = copies.start(block_any.at[:, span : span + width], rows_f.at[:low, :])
        cols = slice(f, f + step)
        silu, slope, hidden = (kept_ref[:, 3 * f + j * step : 3 * f + (j + 1) * step] for j in range(3))
        scores += jnp.sum(grad_hidden * hidden, axis=1, keepdims=True)
        grad_up_ref[:, cols] = (grad_hidden * silu).astype(BF16)
        grad_gate_ref[:, cols] = (grad_hidden * slope).astype(BF16)

    at = iota((low, 128), 1)
    high, rest = split(scores)
    tail = jnp.where(at == 0, high[:low].astype(F32), jnp.where(at == 1, rest[:low].astype(F32), 0.0))
    at = iota((low // 2, 128), 1)
    more = jnp.where(at == 2, high[low:].astype(F32), jnp.where(at == 3, rest[low:].astype(F32), 0.0))
    out_ref[:, 2 * span :] = (tail + mm(put_left, more.astype(BF16))).astype(BF16)
    given = [copies.start(out_ref.at[:, 2 * span :], out_any.at[:, 2 * span :])]

    def give(columns):
        given.append(copies.start(out_ref.at[:, columns], out_any.at[:, columns]))

    def give_halves(base):
        both = mm(put_left, made_ref[:, :half]) + mm(put_right, made_ref[:, half:])
        out_ref[:, base + width : base + span] = both.astype(BF16)
        give(slice(base + width, base + span))

    grad_gate = grad_gate_ref[...]
    grad_up = grad_up_ref[...]
    for i, n in enumerate(range(0, width, wide)):
        gates[i].wait()
        ups[i].wait()
        cols = slice(n, n + wide)
        made = (mm_nt(grad_gate, gate_ref[cols, :]) + mm_nt(grad_up, up_ref[cols, :])).astype(BF16)
        out_ref[:, cols] = made[:low]
        made_ref[:, cols] = made[low:]
        give(cols)
    give_halves(0)

    part_f.wait()
    join_halves(rows_f, half_f[...], sources)
    low_f.wait()
    rows = rows_f[...]
    for f in range(0, inner, step):
        gate = mm(rows, gate_ref[:, f : f + step])
        up = mm(rows, up_ref[:, f : f + step])
        grad_up_ref[:, f : f + step] = (gate * jax.nn.sigmoid(gate) * up).astype(BF16)
    hidden = grad_up_ref[...]
    for n in range(0, width, wide):
        made = mm(hidden, down_ref[:, n : n + wide]).astype(BF16)
        cols = slice(span + n, span + n + wide)
        out_ref[:, cols] = made[:low]
        made_ref[:, n : n + wide] = made[low:]
        give(cols)
    give_halves(span)
    for copy in given:
        copy.wait()


def combine(
    back_any, tables_any, scalars_ref, arrived_any, stored_any, cotangent_any, gain_ref, router_ref, layer_any, grad_any,
    back_ref, tables_ref, arrived_ref, stored_ref, cotangent_ref, layer_ref, grad_ref, sems, *, experts,
):
    rows, width = arrived_ref.shape
    half = width // 2
    span = width + half
    slots = experts * LOW
    copies = Copies(sems)

    def columns(source, target, cols):
        return copies.start(source.at[:, cols], target.at[:, cols])

    first = [
        columns(back_any, back_ref, slice(2 * span, 2 * span + 128)),
        columns(tables_any, tables_ref, slice(0, 7 * slots)),
        columns(back_any, back_ref, slice(0, span)),
        copies.start(stored_any, stored_ref),
    ]
    second = [
        columns(tables_any, tables_ref, slice(7 * slots, 13 * slots)),
        columns(back_any, back_ref, slice(span, 2 * span)),
        copies.start(arrived_any, arrived_ref),
        copies.start(cotangent_any, cotangent_ref),
    ]

    def t(i):
        return tables_ref[:, i * slots : (i + 1) * slots]

    w0, w1, s0, s1, r0, r1, e0, e1, inverse = (scalars_ref[:, i : i + 1] for i in range(9))
    first[0].wait()
    first[1].wait()
    extra = back_ref[:, 2 * span : 2 * span + 128]
    u = []
    for k, ratio in ((0, r0), (1, r1)):
        got = mm(t(3 + k), extra)
        more = mm(t(5 + k), extra)
        u.append((got[:, 0:1] + got[:, 1:2] + more[:, 2:3] + more[:, 3:4]) * ratio)
    cross = u[0] * w1 - w0 * u[1]
    expert_at = iota((rows, experts), 1).astype(F32)
    picks = jnp.where(e0 == expert_at, cross * (1.0 - s0), 0.0)
    picks = picks - jnp.where(e1 == expert_at, cross * (1.0 - s1), 0.0)
    p0, p1 = split(picks)
    p2 = (picks - p0.astype(F32) - p1.astype(F32)).astype(BF16)
    first[2].wait()
    first[3].wait()
    total = jnp.zeros((rows, 1), F32)
    scaled = []
    high = back_ref[:, width:span]
    for s in range(2):
        cols = slice(s * half, (s + 1) * half)
        grad = mm(t(0), back_ref[:, cols]) + mm(t(1 + s), high)
        router_cols = router_ref[:, cols]
        grad = grad + mm(p0, router_cols) + mm(p1, router_cols) + mm(p2, router_cols)
        grad = grad * gain_ref[:, cols].astype(F32)
        total += jnp.sum(grad * stored_ref[:, cols].astype(F32), axis=1, keepdims=True)
        scaled.append(grad)
    pull = inverse * inverse * inverse * (total / width)
    for copy in second:
        copy.wait()
    given = []
    for s in range(2):
        cols = slice(s * half, (s + 1) * half)
        value = cotangent_ref[:, cols].astype(F32) + inverse * scaled[s]
        grad_ref[:, cols] = (value - stored_ref[:, cols].astype(F32) * pull).astype(BF16)
        given.append(columns(grad_ref, grad_any, cols))
    high = back_ref[:, span + width : 2 * span]
    for s, side in ((0, 9), (1, 11)):
        cols = slice(s * half, (s + 1) * half)
        low = back_ref[:, span + s * half : span + (s + 1) * half]
        mixed = mm(t(7), low) + mm(t(8), low) + mm(t(side), high) + mm(t(side + 1), high)
        layer_ref[:, cols] = (arrived_ref[:, cols].astype(F32) + mixed).astype(BF16)
        given.append(columns(layer_ref, layer_any, cols))
    for copy in given:
        copy.wait()


def call(kernel, ins, outs, out_specs, scratch=(), sems=0, flops=0, moved=0, limit=60):
    return pl.pallas_call(
        kernel,
        in_specs=ins,
        out_specs=out_specs,
        out_shape=outs,
        scratch_shapes=list(scratch) + ([pltpu.SemaphoreType.DMA((sems,))] if sems else []),
        compiler_params=pltpu.CompilerParams(vmem_limit_bytes=limit * 2**20),
        cost_estimate=pl.CostEstimate(flops=flops, bytes_accessed=moved, transcendentals=0),
    )


def body(
    activations, gradients, stashed, norm_gain, router, gate_weight, up_weight, down_weight, routes_forward, routes_backward
):
    shape = jax.ShapeDtypeStruct
    experts = lax.axis_size("expert")
    rows, width = stashed.shape[1:]
    span = width + width // 2
    inner = gate_weight.shape[3]
    low, slots = experts * LOW, experts * (LOW + HIGH)
    gate_mat, up_mat, down_mat = gate_weight[0, 0], up_weight[0, 0], down_weight[0, 0]
    router_rows, stored = router[0].T, stashed[0]
    routes_f, routes_b = routes_forward[0].T, routes_backward[0].T

    def exchange(block):
        blocks = block.reshape(experts, LOW, block.shape[1])
        return lax.all_to_all(blocks, "expert", split_axis=0, concat_axis=0, tiled=True).reshape(block.shape)

    arrived = passed_along(activations, "section", 1)[0]
    cotangent = passed_along(gradients, "section", -1)[0]

    sent_b = call(
        functools.partial(pack_stored, experts=experts),
        [VMEM] * 3,
        shape((low, span), BF16),
        HBM,
        scratch=[pltpu.VMEM((low, span), BF16)],
        sems=3,
        flops=4 * low * rows * width,
        moved=2**22,
    )(stored, norm_gain, routes_b)
    got_b = exchange(sent_b)
    sent, tables, scalars = call(
        functools.partial(pack_both, experts=experts),
        [VMEM] * 7,
        (shape((low, 2 * span), BF16), shape((rows, 13 * low), BF16), shape((rows, rows), F32)),
        (HBM, VMEM, VMEM),
        scratch=[pltpu.VMEM((low, 2 * span), BF16)],
        sems=6,
        flops=10 * low * rows * width,
        moved=2**23,
    )(stored, cotangent, arrived, norm_gain, router_rows, routes_b, routes_f)
    got = exchange(sent)
    kept = call(
        functools.partial(expert_stored, sources=experts),
        [VMEM] * 3,
        shape((slots, 3 * inner), F32),
        VMEM,
        scratch=[pltpu.VMEM((slots, width), BF16)],
        limit=40,
        flops=4 * slots * width * inner,
        moved=2**24,
    )(got_b, gate_mat, up_mat)
    made = call(
        functools.partial(expert_both, sources=experts),
        [HBM] * 5,
        shape((low, 2 * span + 128), BF16),
        HBM,
        scratch=[
            pltpu.VMEM((slots, width), BF16),
            pltpu.VMEM((low, width // 2), BF16),
            pltpu.VMEM((slots, width), BF16),
            pltpu.VMEM((low, width // 2), BF16),
            pltpu.VMEM((slots, 3 * inner), F32),
            pltpu.VMEM((width, inner), BF16),
            pltpu.VMEM((width, inner), BF16),
            pltpu.VMEM((inner, width), BF16),
            pltpu.VMEM((slots, inner), BF16),
            pltpu.VMEM((slots, inner), BF16),
            pltpu.VMEM((slots - low, width), BF16),
            pltpu.VMEM((low, 2 * span + 128), BF16),
        ],
        sems=40,
        limit=58,
        flops=12 * slots * width * inner,
        moved=2**24,
    )(got, kept, gate_mat, up_mat, down_mat)
    back = exchange(made)
    layer_out, input_grad = call(
        functools.partial(combine, experts=experts),
        [ANY, HBM, VMEM, HBM, HBM, HBM, VMEM, VMEM],
        (shape((rows, width), BF16), shape((rows, width), BF16)),
        (HBM, HBM),
        scratch=[
            pltpu.VMEM((low, 2 * span + 128), BF16),
            pltpu.VMEM((rows, 13 * low), BF16),
            *[pltpu.VMEM((rows, width), BF16)] * 5,
        ],
        sems=12,
        flops=20 * low * rows * width,
        moved=2**23,
    )(back, tables, scalars, arrived, stored, cotangent, norm_gain, router_rows)
    return layer_out[None], input_grad[None]


def solution(mesh):
    spread_rows = P("section", "expert", None)
    weights = P("section", "expert", None, None)
    placed = (
        spread_rows,
        spread_rows,
        spread_rows,
        P("section", None),
        P("section", None, None),
        weights,
        weights,
        weights,
        spread_rows,
        spread_rows,
    )
    return jax.shard_map(body, mesh=mesh, in_specs=placed, out_specs=(spread_rows, spread_rows), check_vma=False)
```

time: 159 us -> 156 us (0.981)
  local copies, waits for them, and re-layouts: 12.9 us -> 6.53 us
  waiting for transfers between devices: 41.2 us -> 43.1 us
  Pallas kernels: 33 us -> 34.7 us
    unnamed x45 -> x14, local copies, waits for them, and re-layouts: 12.9 us -> 6.53 us
    pallas_call x5, Pallas kernels: 33 us -> 34.7 us  [the longest x1 18.3 us: body(): call(functools.partial(expert_both, sources=experts), [HBM] * 5, shape((l...]
    all_to_all x2, waiting for transfers between devices: 29.4 us -> 31.1 us  [exchange(): lax.all_to_all(blocks, 'expert', split_axis=0, concat_axis=0, tiled=True)]
  transfers between devices with their start and end apart: 4 -> 4, of which waited for: 2 -> 2; matrix products, arithmetic and copies ran while one was open for 0% -> 0% of each run, Pallas kernels for 7% -> 5%
where the time goes in v2:
time: 156 us
  blocking collectives  48.2 us (31%)
  waiting for transfers between devices  43.1 us (28%)
  Pallas kernels  34.7 us (22%)
  starting transfers between devices  22.2 us (14%)
  local copies, waits for them, and re-layouts  6.53 us (4%)
    all_to_all x1, blocking collectives, exchange(): lax.all_to_all(blocks, 'expert', split_axis=0, concat_axis=0, tiled=True)  48.2 us
    all_to_all x2, waiting for transfers between devices, exchange(): lax.all_to_all(blocks, 'expert', split_axis=0, concat_axis=0, tiled=True)  31.1 us
    pallas_call x1, Pallas kernels, body(): call(functools.partial(expert_both, sources=experts), [HBM] * 5, shape((l...  18.3 us
    all_to_all x2, starting transfers between devices, exchange(): lax.all_to_all(blocks, 'expert', split_axis=0, concat_axis=0, tiled=True)  16.5 us
    ppermute x2, waiting for transfers between devices, passed_along(): return lax.ppermute(value, axis, pairs)  12 us
    unnamed x14, local copies, waits for them, and re-layouts  6.53 us
    ppermute x2, starting transfers between devices, passed_along(): return lax.ppermute(value, axis, pairs)  5.77 us
    pallas_call x1, Pallas kernels, body(): call(functools.partial(combine, experts=experts), [ANY, HBM, VMEM, HBM, H...  5.45 us
  transfers between devices with their start and end apart: 4, of which 2 were waited for; matrix products, arithmetic and copies ran while one was open for 0% of the time, Pallas kernels for 5%

profile of v2, /device:TPU:1, one launch (start us, length us, event | category | flops | bytes accessed | tf_op | source)
XLA Modules:
  0.0 155.7 jit_solution(14877082556215613839)
XLA Ops:
  0.6 0.0 copy-start.5
  0.6 0.0 copy-start.6
  0.6 3.0 %shard_map.114 = bf16[256,3072]{1,0:T(8,128)(2,1)} custom-call(bf16[128,2048]{1,0:T(8,128)(2,1)} %bitcast.32, bf16[1,2048]{1,0:T(2,128)(2,1)} %gain_ref.5, s32[2,128]{1,0:T(2,128)} %bitcast.41), custom_call_target="tpu_custom_call" | custom-call | flops 268435456 | bytes 4194304 | tf_op jit(solution)/shard_map/pallas_call | solution.py:409
  3.6 8.6 %all-to-all-start.1 = ((bf16[32,8,3072]{2,1,0:T(8,128)(2,1)}), bf16[32,8,3072]{2,1,0:T(8,128)(2,1)S(1)}, u32[]{:S(2)}, u32[]{:S(2)}) async-start(bf16[32,8,3072]{2,1,0:T(8,128)(2,1)} %bitcast.29), calls=%async_computation.1 | async-start | bytes 3145728 | tf_op jit(solution)/shard_map/all_to_all | solution.py:404
  12.2 0.0 copy-done.5
  12.2 1.7 %collective-permute-start.1 = (bf16[1,128,2048]{2,1,0:T(8,128)(2,1)S(1)}, bf16[1,128,2048]{2,1,0:T(8,128)(2,1)S(1)}, u32[]{:S(2)}, u32[]{:S(2)}) collective-permute-start(bf16[1,128,2048]{2,1,0:T(8,128)(2,1)S(1)} %copy-done.5), channel_id=1, source_target_pairs={{0,32},{32,64},{64,96},{96,128},{128,160},{160,192},{192,224},{224... | collective-permute-start | bytes 1572872 | tf_op jit(solution)/shard_map/ppermute | solution.py:25
  14.0 0.0 copy-done.6
  14.0 4.0 %collective-permute-start = (bf16[1,128,2048]{2,1,0:T(8,128)(2,1)S(1)}, bf16[1,128,2048]{2,1,0:T(8,128)(2,1)S(1)}, u32[]{:S(2)}, u32[]{:S(2)}) collective-permute-start(bf16[1,128,2048]{2,1,0:T(8,128)(2,1)S(1)} %copy-done.6), channel_id=1, source_target_pairs={{0,224},{32,0},{64,32},{96,64},{128,96},{160,128},{192,160},{224,1... | collective-permute-start | bytes 1572872 | tf_op jit(solution)/shard_map/ppermute | solution.py:25
  18.0 12.0 %collective-permute-done.1 = bf16[1,128,2048]{2,1,0:T(8,128)(2,1)S(1)} collective-permute-done((bf16[1,128,2048]{2,1,0:T(8,128)(2,1)S(1)}, bf16[1,128,2048]{2,1,0:T(8,128)(2,1)S(1)}, u32[]{:S(2)}, u32[]{:S(2)}) %collective-permute-start.1) | collective-permute-done | bytes 524320 | tf_op jit(solution)/shard_map/ppermute | solution.py:25
  30.0 0.0 copy-start.3
  30.0 0.0 collective-permute-done
  30.0 0.0 copy-start.4
  30.0 0.8 copy-done.3
  30.8 0.2 copy-done.4
  31.0 5.2 %shard_map.113 = (bf16[256,6144]{1,0:T(8,128)(2,1)}, bf16[128,3328]{1,0:T(8,128)(2,1)}, f32[128,128]{1,0:T(8,128)}) custom-call(bf16[128,2048]{1,0:T(8,128)(2,1)} %bitcast.33, bf16[128,2048]{1,0:T(8,128)(2,1)} %bitcast.37, bf16[128,2048]{1,0:T(8,128)(2,1)} %bitcast.35, bf16[1,2048]{1,0:T(2,128)(2,1)} %gain_ref.5, bf16[32,2048]{1,0:T(8,128)(2,1)} %bitcast.39, ...), custom_call_target="tpu_custom_call" | custom-call | flops 671088640 | bytes 8388608 | tf_op jit(solution)/shard_map/pallas_call | solution.py:420
  36.2 0.0 all-to-all-done.1
  36.2 7.9 %all-to-all-start = ((bf16[32,8,6144]{2,1,0:T(8,128)(2,1)}), bf16[32,8,6144]{2,1,0:T(8,128)(2,1)}, u32[]{:S(2)}, u32[]{:S(2)}) async-start(bf16[32,8,6144]{2,1,0:T(8,128)(2,1)} %bitcast.31), calls=%async_computation | async-start | bytes 6291456 | tf_op jit(solution)/shard_map/all_to_all | solution.py:404
  44.1 0.0 copy-start.1
  44.1 1.9 %copy-done.1 = bf16[1,1,2048,768]{3,2,1,0:T(8,128)(2,1)S(1)} copy-done((bf16[1,1,2048,768]{3,2,1,0:T(8,128)(2,1)S(1)}, bf16[1,1,2048,768]{3,2,1,0:T(8,128)(2,1)}, u32[]{:S(2)}) %copy-start.1) | copy-done | bytes 3145752
  46.0 0.0 copy-start.2
  46.0 1.9 %copy-done.2 = bf16[1,1,2048,768]{3,2,1,0:T(8,128)(2,1)S(1)} copy-done((bf16[1,1,2048,768]{3,2,1,0:T(8,128)(2,1)S(1)}, bf16[1,1,2048,768]{3,2,1,0:T(8,128)(2,1)}, u32[]{:S(2)}) %copy-start.2) | copy-done | bytes 3145752
  47.9 2.8 %shard_map.115.kept_any = f32[384,2304]{1,0:T(8,128)S(1)} custom-call(bf16[256,3072]{1,0:T(8,128)(2,1)S(1)} %bitcast.23, bf16[2048,768]{1,0:T(8,128)(2,1)S(1)} %bitcast.25, bf16[2048,768]{1,0:T(8,128)(2,1)S(1)} %bitcast.27), custom_call_target="tpu_custom_call" | custom-call | flops 2415919104 | bytes 16777216 | tf_op jit(solution)/shard_map/pallas_call | solution.py:431
  50.7 0.0 copy-start
  50.7 1.7 %copy-done = f32[384,2304]{1,0:T(8,128)} copy-done((f32[384,2304]{1,0:T(8,128)}, f32[384,2304]{1,0:T(8,128)S(1)}, u32[]{:S(2)}) %copy-start) | copy-done | bytes 3538968
  52.4 31.1 %all-to-all-done = bf16[32,8,6144]{2,1,0:T(8,128)(2,1)} async-done(((bf16[32,8,6144]{2,1,0:T(8,128)(2,1)}), bf16[32,8,6144]{2,1,0:T(8,128)(2,1)}, u32[]{:S(2)}, u32[]{:S(2)}) %all-to-all-start) | async-done | bytes 3145760 | tf_op jit(solution)/shard_map/all_to_all | solution.py:404
  83.5 18.3 %shard_map.116 = bf16[256,6272]{1,0:T(8,128)(2,1)} custom-call(bf16[256,6144]{1,0:T(8,128)(2,1)} %bitcast.10.block_any, f32[384,2304]{1,0:T(8,128)} %copy-done, bf16[2048,768]{1,0:T(8,128)(2,1)} %bitcast.24, bf16[2048,768]{1,0:T(8,128)(2,1)} %bitcast.26, bf16[768,2048]{1,0:T(8,128)(2,1)} %bitcast.43), custom_call_target="tpu_custom_call" | custom-call | flops 7247757312 | bytes 16777216 | tf_op jit(solution)/shard_map/pallas_call | solution.py:441
  101.8 48.2 %all_to_all.15 = bf16[32,8,6272]{2,1,0:T(8,128)(2,1)} all-to-all(bf16[32,8,6272]{2,1,0:T(8,128)(2,1)} %bitcast.30), channel_id=1, replica_groups=mesh['section'=8,'expert'=32] {'expert'}, dimensions={0} | all-to-all | bytes 6422528 | tf_op jit(solution)/shard_map/all_to_all | solution.py:404
  150.1 5.5 %shard_map.117 = (bf16[128,2048]{1,0:T(8,128)(2,1)}, bf16[128,2048]{1,0:T(8,128)(2,1)}) custom-call(bf16[256,6272]{1,0:T(8,128)(2,1)} %bitcast.28, bf16[128,3328]{1,0:T(8,128)(2,1)} %get-tuple-element.8.tables_any, f32[128,128]{1,0:T(8,128)} %get-tuple-element.9.scalars_ref, bf16[128,2048]{1,0:T(8,128)(2,1)} %bitcast.36, bf16[128,2048]{1,0:T(8,128)(2,1)} %bitcast.34, ...), custom_call_target="tpu_custom_call" | custom-call | flops 1342177280 | bytes 8388608 | tf_op jit(solution)/shard_map/pallas_call | solution.py:466
Async XLA Ops:
  0.6 11.6 %copy-start.5 = (bf16[1,128,2048]{2,1,0:T(8,128)(2,1)S(1)}, bf16[1,128,2048]{2,1,0:T(8,128)(2,1)}, u32[]{:S(2)}) copy-start(bf16[1,128,2048]{2,1,0:T(8,128)(2,1)} %param.10) | copy-start | bytes 1572868
  0.6 13.3 %copy-start.6 = (bf16[1,128,2048]{2,1,0:T(8,128)(2,1)S(1)}, bf16[1,128,2048]{2,1,0:T(8,128)(2,1)}, u32[]{:S(2)}) copy-start(bf16[1,128,2048]{2,1,0:T(8,128)(2,1)} %param.11) | copy-start | bytes 1572868
  3.6 32.6 %all-to-all-start.1 = ((bf16[32,8,3072]{2,1,0:T(8,128)(2,1)}), bf16[32,8,3072]{2,1,0:T(8,128)(2,1)S(1)}, u32[]{:S(2)}, u32[]{:S(2)}) async-start(bf16[32,8,3072]{2,1,0:T(8,128)(2,1)} %bitcast.29), calls=%async_computation.1 | async-start | bytes 3145728 | tf_op jit(solution)/shard_map/all_to_all | solution.py:404
  12.2 17.7 %collective-permute-start.1 = (bf16[1,128,2048]{2,1,0:T(8,128)(2,1)S(1)}, bf16[1,128,2048]{2,1,0:T(8,128)(2,1)S(1)}, u32[]{:S(2)}, u32[]{:S(2)}) collective-permute-start(bf16[1,128,2048]{2,1,0:T(8,128)(2,1)S(1)} %copy-done.5), channel_id=1, source_target_pairs={{0,32},{32,64},{64,96},{96,128},{128,160},{160,192},{192,224},{224... | collective-permute-start | bytes 1572872 | tf_op jit(solution)/shard_map/ppermute | solution.py:25
  14.0 16.0 %collective-permute-start = (bf16[1,128,2048]{2,1,0:T(8,128)(2,1)S(1)}, bf16[1,128,2048]{2,1,0:T(8,128)(2,1)S(1)}, u32[]{:S(2)}, u32[]{:S(2)}) collective-permute-start(bf16[1,128,2048]{2,1,0:T(8,128)(2,1)S(1)} %copy-done.6), channel_id=1, source_target_pairs={{0,224},{32,0},{64,32},{96,64},{128,96},{160,128},{192,160},{224,1... | collective-permute-start | bytes 1572872 | tf_op jit(solution)/shard_map/ppermute | solution.py:25
  30.0 0.8 copy-start.3
  30.0 1.0 copy-start.4
  36.2 47.3 %all-to-all-start = ((bf16[32,8,6144]{2,1,0:T(8,128)(2,1)}), bf16[32,8,6144]{2,1,0:T(8,128)(2,1)}, u32[]{:S(2)}, u32[]{:S(2)}) async-start(bf16[32,8,6144]{2,1,0:T(8,128)(2,1)} %bitcast.31), calls=%async_computation | async-start | bytes 6291456 | tf_op jit(solution)/shard_map/all_to_all | solution.py:404
  44.1 1.9 %copy-start.1 = (bf16[1,1,2048,768]{3,2,1,0:T(8,128)(2,1)S(1)}, bf16[1,1,2048,768]{3,2,1,0:T(8,128)(2,1)}, u32[]{:S(2)}) copy-start(bf16[1,1,2048,768]{3,2,1,0:T(8,128)(2,1)} %param.15) | copy-start | bytes 9437188
  46.0 1.9 %copy-start.2 = (bf16[1,1,2048,768]{3,2,1,0:T(8,128)(2,1)S(1)}, bf16[1,1,2048,768]{3,2,1,0:T(8,128)(2,1)}, u32[]{:S(2)}) copy-start(bf16[1,1,2048,768]{3,2,1,0:T(8,128)(2,1)} %param.16) | copy-start | bytes 9437188
  50.7 1.8 %copy-start = (f32[384,2304]{1,0:T(8,128)}, f32[384,2304]{1,0:T(8,128)S(1)}, u32[]{:S(2)}) copy-start(f32[384,2304]{1,0:T(8,128)S(1)} %shard_map.115.kept_any) | copy-start | bytes 10616836

commit v3 on v2

--- a/solution.py
+++ b/solution.py
@@ -188,7 +188,7 @@
     rows_ref[low:, half:] = mm(take_right, part).astype(BF16)
 
 
-def expert_stored(block_ref, gate_ref, up_ref, kept_ref, rows_ref, *, sources):
+def expert_stored(block_ref, gate_ref, up_ref, silu_ref, slope_ref, hidden_ref, rows_ref, *, sources):
     low = sources * LOW
     width = rows_ref.shape[1]
     rows_ref[:low, :] = block_ref[:, :width]
@@ -199,14 +199,15 @@
         up = mm(rows, up_ref[:, f : f + 256])
         sig = jax.nn.sigmoid(gate)
         silu = gate * sig
-        kept_ref[:, f * 3 : f * 3 + 256] = silu
-        kept_ref[:, f * 3 + 256 : f * 3 + 512] = up * sig * (1.0 + gate * (1.0 - sig))
-        kept_ref[:, f * 3 + 512 : f * 3 + 768] = (silu * up).astype(BF16).astype(F32)
+        silu_ref[:, f : f + 256] = silu
+        slope_ref[:, f : f + 256] = up * sig * (1.0 + gate * (1.0 - sig))
+        hidden_ref[:, f : f + 256] = (silu * up).astype(BF16)
 
 
 def expert_both(
-    block_any, kept_any, gate_any, up_any, down_any, out_any,
-    rows_b, half_b, rows_f, half_f, kept_ref, gate_ref, up_ref, down_ref, grad_gate_ref, grad_up_ref, made_ref, out_ref, sems, *, sources,
+    block_any, silu_ref, slope_ref, hidden_ref, gate_any, up_any, down_any, out_any,
+    rows_b, half_b, rows_f, half_f, gate_ref, up_ref, down_ref, grad_gate_ref, grad_up_ref, made_ref, out_ref, sems,
+    *, sources,
 ):
     low = sources * LOW
     width = rows_b.shape[1]
@@ -216,39 +217,34 @@
     step = 256
     wide = 512
     copies = Copies(sems)
-    part_b = copies.start(block_any.at[:, width:span], half_b)
-    low_b = copies.start(block_any.at[:, :width], rows_b.at[:low, :])
-    downs = []
-    helds = []
+
+    def started(source, target, step):
+        count = target.shape[0]
+        return [copies.start(source.at[i : i + step, :], target.at[i : i + step, :]) for i in range(0, count, step)]
+
+    def taken(running):
+        for copy in running:
+            copy.wait()
+
+    first = [
+        copies.start(block_any.at[:, width:span], half_b),
+        copies.start(block_any.at[:, :width], rows_b.at[:low, :]),
+        *started(down_any, down_ref, inner // 2),
+    ]
+    taken(first[:2])
+    second = started(gate_any, gate_ref, width // 2)
+    join_halves(rows_b, half_b[...], sources)
+    taken(first[2:])
+    second += started(up_any, up_ref, width // 2)
+    scores = jnp.zeros((rows_b.shape[0], 1), F32)
     for f in range(0, inner, step):
-        downs.append(copies.start(down_any.at[f : f + step, :], down_ref.at[f : f + step, :]))
-        cols = slice(3 * f, 3 * f + 3 * step)
-        helds.append(copies.start(kept_any.at[:, cols], kept_ref.at[:, cols]))
-    put_left, put_right = half_homes(sources)
-    part_b.wait()
-    join_halves(rows_b, half_b[...], sources)
-    low_b.wait()
-    gates = []
-    ups = []
-
-    rows = rows_b[...]
-    scores = jnp.zeros((rows.shape[0], 1), F32)
-    for i, f in enumerate(range(0, inner, step)):
-        downs[i].wait()
-        grad_hidden = mm_nt(rows, down_ref[f : f + step, :])
-        helds[i].wait()
-        if i == len(range(0, inner, step)) - 1:
-            for n in range(0, width, wide):
-                gates.append(copies.start(gate_any.at[n : n + wide, :], gate_ref.at[n : n + wide, :]))
-                ups.append(copies.start(up_any.at[n : n + wide, :], up_ref.at[n : n + wide, :]))
-            part_f = copies.start(block_any.at[:, span + width :], half_f)
-            low_f = copies.start(block_any.at[:, span : span + width], rows_f.at[:low, :])
         cols = slice(f, f + step)
-        silu, slope, hidden = (kept_ref[:, 3 * f + j * step : 3 * f + (j + 1) * step] for j in range(3))
-        scores += jnp.sum(grad_hidden * hidden, axis=1, keepdims=True)
-        grad_up_ref[:, cols] = (grad_hidden * silu).astype(BF16)
-        grad_gate_ref[:, cols] = (grad_hidden * slope).astype(BF16)
-
+        grad_hidden = mm_nt(rows_b[...], down_ref[cols, :])
+        scores += jnp.sum(grad_hidden * hidden_ref[:, cols].astype(F32), axis=1, keepdims=True)
+        grad_up_ref[:, cols] = (grad_hidden * silu_ref[:, cols]).astype(BF16)
+        grad_gate_ref[:, cols] = (grad_hidden * slope_ref[:, cols]).astype(BF16)
+
+    put_left, _ = half_homes(sources)
     at = iota((low, 128), 1)
     high, rest = split(scores)
     tail = jnp.where(at == 0, high[:low].astype(F32), jnp.where(at == 1, rest[:low].astype(F32), 0.0))
@@ -261,33 +257,32 @@
         given.append(copies.start(out_ref.at[:, columns], out_any.at[:, columns]))
 
     def give_halves(base):
+        put_left, put_right = half_homes(sources)
         both = mm(put_left, made_ref[:, :half]) + mm(put_right, made_ref[:, half:])
         out_ref[:, base + width : base + span] = both.astype(BF16)
         give(slice(base + width, base + span))
 
-    grad_gate = grad_gate_ref[...]
-    grad_up = grad_up_ref[...]
-    for i, n in enumerate(range(0, width, wide)):
-        gates[i].wait()
-        ups[i].wait()
+    taken(second)
+    third = [
+        copies.start(block_any.at[:, span + width :], half_f),
+        copies.start(block_any.at[:, span : span + width], rows_f.at[:low, :]),
+    ]
+    for n in range(0, width, wide):
         cols = slice(n, n + wide)
-        made = (mm_nt(grad_gate, gate_ref[cols, :]) + mm_nt(grad_up, up_ref[cols, :])).astype(BF16)
+        made = (mm_nt(grad_gate_ref[...], gate_ref[cols, :]) + mm_nt(grad_up_ref[...], up_ref[cols, :])).astype(BF16)
         out_ref[:, cols] = made[:low]
         made_ref[:, cols] = made[low:]
         give(cols)
     give_halves(0)
 
-    part_f.wait()
+    taken(third)
     join_halves(rows_f, half_f[...], sources)
-    low_f.wait()
-    rows = rows_f[...]
     for f in range(0, inner, step):
-        gate = mm(rows, gate_ref[:, f : f + step])
-        up = mm(rows, up_ref[:, f : f + step])
+        gate = mm(rows_f[...], gate_ref[:, f : f + step])
+        up = mm(rows_f[...], up_ref[:, f : f + step])
         grad_up_ref[:, f : f + step] = (gate * jax.nn.sigmoid(gate) * up).astype(BF16)
-    hidden = grad_up_ref[...]
     for n in range(0, width, wide):
-        made = mm(hidden, down_ref[:, n : n + wide]).astype(BF16)
+        made = mm(grad_up_ref[...], down_ref[:, n : n + wide]).astype(BF16)
         cols = slice(span + n, span + n + wide)
         out_ref[:, cols] = made[:low]
         made_ref[:, n : n + wide] = made[low:]
@@ -298,37 +293,25 @@
 
 
 def combine(
-    back_any, tables_any, scalars_ref, arrived_any, stored_any, cotangent_any, gain_ref, router_ref, layer_any, grad_any,
-    back_ref, tables_ref, arrived_ref, stored_ref, cotangent_ref, layer_ref, grad_ref, sems, *, experts,
+    back_ref, tables_ref, scalars_ref, arrived_ref, stored_ref, cotangent_ref, gain_ref, router_ref, layer_ref, grad_ref,
+    *, experts,
 ):
     rows, width = arrived_ref.shape
     half = width // 2
     span = width + half
     slots = experts * LOW
-    copies = Copies(sems)
-
-    def columns(source, target, cols):
-        return copies.start(source.at[:, cols], target.at[:, cols])
-
-    first = [
-        columns(back_any, back_ref, slice(2 * span, 2 * span + 128)),
-        columns(tables_any, tables_ref, slice(0, 7 * slots)),
-        columns(back_any, back_ref, slice(0, span)),
-        copies.start(stored_any, stored_ref),
-    ]
-    second = [
-        columns(tables_any, tables_ref, slice(7 * slots, 13 * slots)),
-        columns(back_any, back_ref, slice(span, 2 * span)),
-        copies.start(arrived_any, arrived_ref),
-        copies.start(cotangent_any, cotangent_ref),
-    ]
 
     def t(i):
         return tables_ref[:, i * slots : (i + 1) * slots]
 
+    high = back_ref[:, span + width : 2 * span]
+    for s, side in ((0, 9), (1, 11)):
+        cols = slice(s * half, (s + 1) * half)
+        low = back_ref[:, span + s * half : span + (s + 1) * half]
+        mixed = mm(t(7), low) + mm(t(8), low) + mm(t(side), high) + mm(t(side + 1), high)
+        layer_ref[:, cols] = (arrived_ref[:, cols].astype(F32) + mixed).astype(BF16)
+
     w0, w1, s0, s1, r0, r1, e0, e1, inverse = (scalars_ref[:, i : i + 1] for i in range(9))
-    first[0].wait()
-    first[1].wait()
     extra = back_ref[:, 2 * span : 2 * span + 128]
     u = []
     for k, ratio in ((0, r0), (1, r1)):
@@ -341,8 +324,6 @@
     picks = picks - jnp.where(e1 == expert_at, cross * (1.0 - s1), 0.0)
     p0, p1 = split(picks)
     p2 = (picks - p0.astype(F32) - p1.astype(F32)).astype(BF16)
-    first[2].wait()
-    first[3].wait()
     total = jnp.zeros((rows, 1), F32)
     scaled = []
     high = back_ref[:, width:span]
@@ -355,23 +336,10 @@
         total += jnp.sum(grad * stored_ref[:, cols].astype(F32), axis=1, keepdims=True)
         scaled.append(grad)
     pull = inverse * inverse * inverse * (total / width)
-    for copy in second:
-        copy.wait()
-    given = []
     for s in range(2):
         cols = slice(s * half, (s + 1) * half)
         value = cotangent_ref[:, cols].astype(F32) + inverse * scaled[s]
         grad_ref[:, cols] = (value - stored_ref[:, cols].astype(F32) * pull).astype(BF16)
-        given.append(columns(grad_ref, grad_any, cols))
-    high = back_ref[:, span + width : 2 * span]
-    for s, side in ((0, 9), (1, 11)):
-        cols = slice(s * half, (s + 1) * half)
-        low = back_ref[:, span + s * half : span + (s + 1) * half]
-        mixed = mm(t(7), low) + mm(t(8), low) + mm(t(side), high) + mm(t(side + 1), high)
-        layer_ref[:, cols] = (arrived_ref[:, cols].astype(F32) + mixed).astype(BF16)
-        given.append(columns(layer_ref, layer_any, cols))
-    for copy in given:
-        copy.wait()
 
 
 def call(kernel, ins, outs, out_specs, scratch=(), sems=0, flops=0, moved=0, limit=60):
@@ -428,11 +396,11 @@
         moved=2**23,
     )(stored, cotangent, arrived, norm_gain, router_rows, routes_b, routes_f)
     got = exchange(sent)
-    kept = call(
+    silu, slope, hidden = call(
         functools.partial(expert_stored, sources=experts),
         [VMEM] * 3,
-        shape((slots, 3 * inner), F32),
-        VMEM,
+        (shape((slots, inner), F32), shape((slots, inner), F32), shape((slots, inner), BF16)),
+        (VMEM,) * 3,
         scratch=[pltpu.VMEM((slots, width), BF16)],
         limit=40,
         flops=4 * slots * width * inner,
@@ -440,7 +408,7 @@
     )(got_b, gate_mat, up_mat)
     made = call(
         functools.partial(expert_both, sources=experts),
-        [HBM] * 5,
+        [HBM] + [VMEM] * 3 + [HBM] * 3,
         shape((low, 2 * span + 128), BF16),
         HBM,
         scratch=[
@@ -448,7 +416,6 @@
             pltpu.VMEM((low, width // 2), BF16),
             pltpu.VMEM((slots, width), BF16),
             pltpu.VMEM((low, width // 2), BF16),
-            pltpu.VMEM((slots, 3 * inner), F32),
             pltpu.VMEM((width, inner), BF16),
             pltpu.VMEM((width, inner), BF16),
             pltpu.VMEM((inner, width), BF16),
@@ -458,22 +425,17 @@
             pltpu.VMEM((low, 2 * span + 128), BF16),
         ],
         sems=40,
-        limit=58,
+        limit=50,
         flops=12 * slots * width * inner,
         moved=2**24,
-    )(got, kept, gate_mat, up_mat, down_mat)
+    )(got, silu, slope, hidden, gate_mat, up_mat, down_mat)
     back = exchange(made)
     layer_out, input_grad = call(
         functools.partial(combine, experts=experts),
-        [ANY, HBM, VMEM, HBM, HBM, HBM, VMEM, VMEM],
+        [VMEM] * 8,
         (shape((rows, width), BF16), shape((rows, width), BF16)),
-        (HBM, HBM),
-        scratch=[
-            pltpu.VMEM((low, 2 * span + 128), BF16),
-            pltpu.VMEM((rows, 13 * low), BF16),
-            *[pltpu.VMEM((rows, width), BF16)] * 5,
-        ],
-        sems=12,
+        (VMEM, VMEM),
+        limit=48,
         flops=20 * low * rows * width,
         moved=2**23,
     )(back, tables, scalars, arrived, stored, cotangent, norm_gain, router_rows)

time: 156 us -> 149 us (0.955)
  Pallas kernels: 34.7 us -> 27.2 us
    pallas_call x3, Pallas kernels: 26.5 us -> 18.9 us  [the longest x1 13.3 us: body(): call(functools.partial(expert_both, sources=experts), [HBM] + [VMEM] * 3...]
    unnamed x14 -> x30, local copies, waits for them, and re-layouts: 6.53 us -> 7.05 us
where the time goes in v3:
time: 149 us
  blocking collectives  47.6 us (32%)
  waiting for transfers between devices  43.8 us (29%)
  Pallas kernels  27.2 us (18%)
  starting transfers between devices  22.2 us (15%)
  local copies, waits for them, and re-layouts  7.05 us (5%)
    all_to_all x1, blocking collectives, exchange(): lax.all_to_all(blocks, 'expert', split_axis=0, concat_axis=0, tiled=True)  47.6 us
    all_to_all x2, waiting for transfers between devices, exchange(): lax.all_to_all(blocks, 'expert', split_axis=0, concat_axis=0, tiled=True)  31.9 us
    all_to_all x2, starting transfers between devices, exchange(): lax.all_to_all(blocks, 'expert', split_axis=0, concat_axis=0, tiled=True)  16.5 us
    pallas_call x1, Pallas kernels, body(): call(functools.partial(expert_both, sources=experts), [HBM] + [VMEM] * 3...  13.3 us
    ppermute x2, waiting for transfers between devices, passed_along(): return lax.ppermute(value, axis, pairs)  12 us
    unnamed x30, local copies, waits for them, and re-layouts  7.05 us
    ppermute x2, starting transfers between devices, passed_along(): return lax.ppermute(value, axis, pairs)  5.77 us
    pallas_call x1, Pallas kernels, body(): call(functools.partial(pack_both, experts=experts), [VMEM] * 7, (shape((l...  5.32 us
  transfers between devices with their start and end apart: 4, of which 2 were waited for; matrix products, arithmetic and copies ran while one was open for 0% of the time, Pallas kernels for 5%

profile of v3, /device:TPU:1, one launch (start us, length us, event | category | flops | bytes accessed | tf_op | source)
XLA Modules:
  0.0 148.8 jit_solution(7132205042650616923)
XLA Ops:
  0.6 0.0 copy-start.13
  0.6 3.0 %shard_map.114 = bf16[256,3072]{1,0:T(8,128)(2,1)} custom-call(bf16[128,2048]{1,0:T(8,128)(2,1)} %bitcast.24, bf16[1,2048]{1,0:T(2,128)(2,1)} %gain_ref.5, s32[2,128]{1,0:T(2,128)} %bitcast.41), custom_call_target="tpu_custom_call" | custom-call | flops 268435456 | bytes 4194304 | tf_op jit(solution)/shard_map/pallas_call | solution.py:377
  3.6 8.6 %all-to-all-start.1 = ((bf16[32,8,3072]{2,1,0:T(8,128)(2,1)}), bf16[32,8,3072]{2,1,0:T(8,128)(2,1)S(1)}, u32[]{:S(2)}, u32[]{:S(2)}) async-start(bf16[32,8,3072]{2,1,0:T(8,128)(2,1)} %bitcast.38), calls=%async_computation.1 | async-start | bytes 3145728 | tf_op jit(solution)/shard_map/all_to_all | solution.py:372
  12.2 1.7 %collective-permute-start.1 = (bf16[1,128,2048]{2,1,0:T(8,128)(2,1)S(1)}, bf16[1,128,2048]{2,1,0:T(8,128)(2,1)S(1)}, u32[]{:S(2)}, u32[]{:S(2)}) collective-permute-start(bf16[1,128,2048]{2,1,0:T(8,128)(2,1)S(1)} %copy-done.13), channel_id=1, source_target_pairs={{0,32},{32,64},{64,96},{96,128},{128,160},{160,192},{192,224},{224... | collective-permute-start | bytes 1572872 | tf_op jit(solution)/shard_map/ppermute | solution.py:25
  13.9 4.0 %collective-permute-start = (bf16[1,128,2048]{2,1,0:T(8,128)(2,1)S(1)}, bf16[1,128,2048]{2,1,0:T(8,128)(2,1)S(1)}, u32[]{:S(2)}, u32[]{:S(2)}) collective-permute-start(bf16[1,128,2048]{2,1,0:T(8,128)(2,1)S(1)} %copy-done.14), channel_id=1, source_target_pairs={{0,224},{32,0},{64,32},{96,64},{128,96},{160,128},{192,160},{224,1... | collective-permute-start | bytes 1572872 | tf_op jit(solution)/shard_map/ppermute | solution.py:25
  18.0 12.0 %collective-permute-done.1 = bf16[1,128,2048]{2,1,0:T(8,128)(2,1)S(1)} collective-permute-done((bf16[1,128,2048]{2,1,0:T(8,128)(2,1)S(1)}, bf16[1,128,2048]{2,1,0:T(8,128)(2,1)S(1)}, u32[]{:S(2)}, u32[]{:S(2)}) %collective-permute-start.1) | collective-permute-done | bytes 524320 | tf_op jit(solution)/shard_map/ppermute | solution.py:25
  29.9 0.0 collective-permute-done
  29.9 0.8 copy-done.2
  30.7 0.2 copy-done.4
  30.9 5.3 %shard_map.113 = (bf16[256,6144]{1,0:T(8,128)(2,1)}, bf16[128,3328]{1,0:T(8,128)(2,1)}, f32[128,128]{1,0:T(8,128)}) custom-call(bf16[128,2048]{1,0:T(8,128)(2,1)} %bitcast.25, bf16[128,2048]{1,0:T(8,128)(2,1)} %bitcast.30, bf16[128,2048]{1,0:T(8,128)(2,1)} %bitcast.28, bf16[1,2048]{1,0:T(2,128)(2,1)} %gain_ref.5, bf16[32,2048]{1,0:T(8,128)(2,1)} %bitcast.32, ...), custom_call_target="tpu_custom_call" | custom-call | flops 671088640 | bytes 8388608 | tf_op jit(solution)/shard_map/pallas_call | solution.py:388
  36.2 0.0 all-to-all-done.1
  36.2 7.9 %all-to-all-start = ((bf16[32,8,6144]{2,1,0:T(8,128)(2,1)}), bf16[32,8,6144]{2,1,0:T(8,128)(2,1)}, u32[]{:S(2)}, u32[]{:S(2)}) async-start(bf16[32,8,6144]{2,1,0:T(8,128)(2,1)} %bitcast.40), calls=%async_computation | async-start | bytes 6291456 | tf_op jit(solution)/shard_map/all_to_all | solution.py:372
  44.1 0.0 copy-start.9
  44.1 1.9 %copy-done.9 = bf16[1,1,2048,768]{3,2,1,0:T(8,128)(2,1)S(1)} copy-done((bf16[1,1,2048,768]{3,2,1,0:T(8,128)(2,1)S(1)}, bf16[1,1,2048,768]{3,2,1,0:T(8,128)(2,1)}, u32[]{:S(2)}) %copy-start.9) | copy-done | bytes 3145752
  46.0 1.9 %copy-done.10 = bf16[1,1,2048,768]{3,2,1,0:T(8,128)(2,1)S(1)} copy-done((bf16[1,1,2048,768]{3,2,1,0:T(8,128)(2,1)S(1)}, bf16[1,1,2048,768]{3,2,1,0:T(8,128)(2,1)}, u32[]{:S(2)}) %copy-start.10) | copy-done | bytes 3145752
  47.9 2.8 %shard_map.115 = (f32[384,768]{1,0:T(8,128)S(1)}, f32[384,768]{1,0:T(8,128)S(1)}, bf16[384,768]{1,0:T(8,128)(2,1)S(1)}) custom-call(bf16[256,3072]{1,0:T(8,128)(2,1)S(1)} %bitcast.27, bf16[2048,768]{1,0:T(8,128)(2,1)S(1)} %bitcast.35, bf16[2048,768]{1,0:T(8,128)(2,1)S(1)} %bitcast.37), custom_call_target="tpu_custom_call" | custom-call | flops 2415919104 | bytes 16777216 | tf_op jit(solution)/shard_map/pallas_call | solution.py:399
  50.7 1.0 copy-done.11
  51.7 31.9 %all-to-all-done = bf16[32,8,6144]{2,1,0:T(8,128)(2,1)} async-done(((bf16[32,8,6144]{2,1,0:T(8,128)(2,1)}), bf16[32,8,6144]{2,1,0:T(8,128)(2,1)}, u32[]{:S(2)}, u32[]{:S(2)}) %all-to-all-start) | async-done | bytes 3145760 | tf_op jit(solution)/shard_map/all_to_all | solution.py:372
  83.6 1.3 copy-done.12
  84.8 13.3 %shard_map.116 = bf16[256,6272]{1,0:T(8,128)(2,1)} custom-call(bf16[256,6144]{1,0:T(8,128)(2,1)} %bitcast.10.block_any, f32[384,768]{1,0:T(8,128)S(1)} %get-tuple-element.11.silu_ref, f32[384,768]{1,0:T(8,128)S(1)} %copy-done.12, bf16[384,768]{1,0:T(8,128)(2,1)S(1)} %get-tuple-element.13.hidden_ref, bf16[2048,768]{1,0:T(8,128)(2,1)} %bitcast.34, ...), custom_call_target="tpu_custom_call" | custom-call | flops 7247757312 | bytes 16777216 | tf_op jit(solution)/shard_map/pallas_call | solution.py:409
  98.2 0.0 copy-start
  98.2 0.0 copy-start.1
  98.2 0.0 copy-start.3
  98.2 0.0 copy-start.5
  98.2 0.0 copy-start.6
  98.3 0.0 copy-start.8
  98.3 47.6 %all_to_all.15 = bf16[32,8,6272]{2,1,0:T(8,128)(2,1)S(1)} all-to-all(bf16[32,8,6272]{2,1,0:T(8,128)(2,1)} %bitcast.39), channel_id=1, replica_groups=mesh['section'=8,'expert'=32] {'expert'}, dimensions={0} | all-to-all | bytes 6422528 | tf_op jit(solution)/shard_map/all_to_all | solution.py:372
  145.9 0.0 copy-done.5
  145.9 0.0 copy-done.6
  145.9 0.0 copy-done.7
  145.9 0.0 copy-done.8
  145.9 2.8 %shard_map.117 = (bf16[128,2048]{1,0:T(8,128)(2,1)}, bf16[128,2048]{1,0:T(8,128)(2,1)}) custom-call(bf16[256,6272]{1,0:T(8,128)(2,1)S(1)} %bitcast.23, bf16[128,3328]{1,0:T(8,128)(2,1)S(1)} %copy-done.1, f32[128,128]{1,0:T(8,128)S(1)} %copy-done.7, bf16[128,2048]{1,0:T(8,128)(2,1)S(1)} %bitcast.29, bf16[128,2048]{1,0:T(8,128)(2,1)S(1)} %bitcast.26, ...), custom_call_target="tpu_custom_call" | custom-call | flops 1342177280 | bytes 8388608 | tf_op jit(solution)/shard_map/pallas_call | solution.py:433
  (12 shorter events, 0.0 us)
Async XLA Ops:
  0.6 11.6 %copy-start.13 = (bf16[1,128,2048]{2,1,0:T(8,128)(2,1)S(1)}, bf16[1,128,2048]{2,1,0:T(8,128)(2,1)}, u32[]{:S(2)}) copy-start(bf16[1,128,2048]{2,1,0:T(8,128)(2,1)} %param.10) | copy-start | bytes 1572868
  0.6 13.3 %copy-start.14 = (bf16[1,128,2048]{2,1,0:T(8,128)(2,1)S(1)}, bf16[1,128,2048]{2,1,0:T(8,128)(2,1)}, u32[]{:S(2)}) copy-start(bf16[1,128,2048]{2,1,0:T(8,128)(2,1)} %param.11) | copy-start | bytes 1572868
  3.6 32.6 %all-to-all-start.1 = ((bf16[32,8,3072]{2,1,0:T(8,128)(2,1)}), bf16[32,8,3072]{2,1,0:T(8,128)(2,1)S(1)}, u32[]{:S(2)}, u32[]{:S(2)}) async-start(bf16[32,8,3072]{2,1,0:T(8,128)(2,1)} %bitcast.38), calls=%async_computation.1 | async-start | bytes 3145728 | tf_op jit(solution)/shard_map/all_to_all | solution.py:372
  12.2 17.7 %collective-permute-start.1 = (bf16[1,128,2048]{2,1,0:T(8,128)(2,1)S(1)}, bf16[1,128,2048]{2,1,0:T(8,128)(2,1)S(1)}, u32[]{:S(2)}, u32[]{:S(2)}) collective-permute-start(bf16[1,128,2048]{2,1,0:T(8,128)(2,1)S(1)} %copy-done.13), channel_id=1, source_target_pairs={{0,32},{32,64},{64,96},{96,128},{128,160},{160,192},{192,224},{224... | collective-permute-start | bytes 1572872 | tf_op jit(solution)/shard_map/ppermute | solution.py:25
  13.9 16.0 %collective-permute-start = (bf16[1,128,2048]{2,1,0:T(8,128)(2,1)S(1)}, bf16[1,128,2048]{2,1,0:T(8,128)(2,1)S(1)}, u32[]{:S(2)}, u32[]{:S(2)}) collective-permute-start(bf16[1,128,2048]{2,1,0:T(8,128)(2,1)S(1)} %copy-done.14), channel_id=1, source_target_pairs={{0,224},{32,0},{64,32},{96,64},{128,96},{160,128},{192,160},{224,1... | collective-permute-start | bytes 1572872 | tf_op jit(solution)/shard_map/ppermute | solution.py:25
  29.9 0.8 copy-start.2
  29.9 1.0 copy-start.4
  36.2 47.3 %all-to-all-start = ((bf16[32,8,6144]{2,1,0:T(8,128)(2,1)}), bf16[32,8,6144]{2,1,0:T(8,128)(2,1)}, u32[]{:S(2)}, u32[]{:S(2)}) async-start(bf16[32,8,6144]{2,1,0:T(8,128)(2,1)} %bitcast.40), calls=%async_computation | async-start | bytes 6291456 | tf_op jit(solution)/shard_map/all_to_all | solution.py:372
  44.1 1.9 %copy-start.9 = (bf16[1,1,2048,768]{3,2,1,0:T(8,128)(2,1)S(1)}, bf16[1,1,2048,768]{3,2,1,0:T(8,128)(2,1)}, u32[]{:S(2)}) copy-start(bf16[1,1,2048,768]{3,2,1,0:T(8,128)(2,1)} %param.15) | copy-start | bytes 9437188
  46.0 1.9 %copy-start.10 = (bf16[1,1,2048,768]{3,2,1,0:T(8,128)(2,1)S(1)}, bf16[1,1,2048,768]{3,2,1,0:T(8,128)(2,1)}, u32[]{:S(2)}) copy-start(bf16[1,1,2048,768]{3,2,1,0:T(8,128)(2,1)} %param.16) | copy-start | bytes 9437188
  50.7 1.0 copy-start.11
  83.6 1.3 copy-start.12
  98.2 47.7 %copy-start = (bf16[1,128,2048]{2,1,0:T(8,128)(2,1)S(1)}, bf16[1,128,2048]{2,1,0:T(8,128)(2,1)}, u32[]{:S(2)}) copy-start(bf16[1,128,2048]{2,1,0:T(8,128)(2,1)} %param.12) | copy-start | bytes 1572868
  98.2 47.7 %copy-start.1 = (bf16[128,3328]{1,0:T(8,128)(2,1)S(1)}, bf16[128,3328]{1,0:T(8,128)(2,1)}, u32[]{:S(2)}) copy-start(bf16[128,3328]{1,0:T(8,128)(2,1)} %get-tuple-element.14.tables_ref) | copy-start | bytes 2555908
  98.2 47.7 %copy-start.3 = (bf16[1,128,2048]{2,1,0:T(8,128)(2,1)S(1)}, bf16[1,128,2048]{2,1,0:T(8,128)(2,1)}, u32[]{:S(2)}) copy-start(bf16[1,128,2048]{2,1,0:T(8,128)(2,1)} %copy-done.2) | copy-start | bytes 1572868
  98.2 47.7 %copy-start.5 = (bf16[1,128,2048]{2,1,0:T(8,128)(2,1)S(1)}, bf16[1,128,2048]{2,1,0:T(8,128)(2,1)}, u32[]{:S(2)}) copy-start(bf16[1,128,2048]{2,1,0:T(8,128)(2,1)} %copy-done.4) | copy-start | bytes 1572868
  98.2 47.7 %copy-start.6 = (bf16[1,2048,32]{1,2,0:T(8,128)(2,1)S(1)}, bf16[1,2048,32]{1,2,0:T(8,128)(2,1)}, u32[]{:S(2)}) copy-start(bf16[1,2048,32]{1,2,0:T(8,128)(2,1)} %param.14) | copy-start | bytes 393220
  98.2 47.7 %copy-start.7 = (f32[128,128]{1,0:T(8,128)S(1)}, f32[128,128]{1,0:T(8,128)}, u32[]{:S(2)}) copy-start(f32[128,128]{1,0:T(8,128)} %get-tuple-element.15.scalars_ref) | copy-start | bytes 196612
  98.3 47.7 %copy-start.8 = (bf16[1,2048]{1,0:T(2,128)(2,1)S(1)}, bf16[1,2048]{1,0:T(2,128)(2,1)}, u32[]{:S(2)}) copy-start(bf16[1,2048]{1,0:T(2,128)(2,1)} %gain_ref.5) | copy-start | bytes 12292

commit v4 on v3

--- a/solution.py
+++ b/solution.py
@@ -188,25 +188,20 @@
     rows_ref[low:, half:] = mm(take_right, part).astype(BF16)
 
 
-def expert_stored(block_ref, gate_ref, up_ref, silu_ref, slope_ref, hidden_ref, rows_ref, *, sources):
+def expert_stored(block_ref, gate_ref, up_ref, gated_ref, upper_ref, rows_ref, *, sources):
     low = sources * LOW
     width = rows_ref.shape[1]
     rows_ref[:low, :] = block_ref[:, :width]
     join_halves(rows_ref, block_ref[:, width:], sources)
     rows = rows_ref[...]
     for f in range(0, gate_ref.shape[1], 256):
-        gate = mm(rows, gate_ref[:, f : f + 256])
-        up = mm(rows, up_ref[:, f : f + 256])
-        sig = jax.nn.sigmoid(gate)
-        silu = gate * sig
-        silu_ref[:, f : f + 256] = silu
-        slope_ref[:, f : f + 256] = up * sig * (1.0 + gate * (1.0 - sig))
-        hidden_ref[:, f : f + 256] = (silu * up).astype(BF16)
+        gated_ref[:, f : f + 256] = mm(rows, gate_ref[:, f : f + 256])
+        upper_ref[:, f : f + 256] = mm(rows, up_ref[:, f : f + 256])
 
 
 def expert_both(
-    block_any, silu_ref, slope_ref, hidden_ref, gate_any, up_any, down_any, out_any,
-    rows_b, half_b, rows_f, half_f, gate_ref, up_ref, down_ref, grad_gate_ref, grad_up_ref, made_ref, out_ref, sems,
+    block_any, gated_any, upper_any, gate_any, up_any, down_any, out_any,
+    gated_ref, upper_ref, rows_b, half_b, rows_f, half_f, gate_ref, up_ref, down_ref, grad_gate_ref, grad_up_ref, made_ref, out_ref, sems,
     *, sources,
 ):
     low = sources * LOW
@@ -231,6 +226,7 @@
         copies.start(block_any.at[:, :width], rows_b.at[:low, :]),
         *started(down_any, down_ref, inner // 2),
     ]
+    held = [copies.start(gated_any, gated_ref), copies.start(upper_any, upper_ref)]
     taken(first[:2])
     second = started(gate_any, gate_ref, width // 2)
     join_halves(rows_b, half_b[...], sources)
@@ -240,9 +236,17 @@
     for f in range(0, inner, step):
         cols = slice(f, f + step)
         grad_hidden = mm_nt(rows_b[...], down_ref[cols, :])
-        scores += jnp.sum(grad_hidden * hidden_ref[:, cols].astype(F32), axis=1, keepdims=True)
-        grad_up_ref[:, cols] = (grad_hidden * silu_ref[:, cols]).astype(BF16)
-        grad_gate_ref[:, cols] = (grad_hidden * slope_ref[:, cols]).astype(BF16)
+        if f == 0:
+            taken(held)
+        gated = gated_ref[:, cols]
+        upper = upper_ref[:, cols]
+        sig = jax.nn.sigmoid(gated)
+        silu = gated * sig
+        hidden = (silu * upper).astype(BF16).astype(F32)
+        scores += jnp.sum(grad_hidden * hidden, axis=1, keepdims=True)
+        grad_up_ref[:, cols] = (grad_hidden * silu).astype(BF16)
+        slope = upper * sig * (1.0 + gated * (1.0 - sig))
+        grad_gate_ref[:, cols] = (grad_hidden * slope).astype(BF16)
 
     put_left, _ = half_homes(sources)
     at = iota((low, 128), 1)
@@ -396,11 +400,11 @@
         moved=2**23,
     )(stored, cotangent, arrived, norm_gain, router_rows, routes_b, routes_f)
     got = exchange(sent)
-    silu, slope, hidden = call(
+    gated, upper = call(
         functools.partial(expert_stored, sources=experts),
         [VMEM] * 3,
-        (shape((slots, inner), F32), shape((slots, inner), F32), shape((slots, inner), BF16)),
-        (VMEM,) * 3,
+        (shape((slots, inner), F32), shape((slots, inner), F32)),
+        (VMEM, VMEM),
         scratch=[pltpu.VMEM((slots, width), BF16)],
         limit=40,
         flops=4 * slots * width * inner,
@@ -408,10 +412,12 @@
     )(got_b, gate_mat, up_mat)
     made = call(
         functools.partial(expert_both, sources=experts),
-        [HBM] + [VMEM] * 3 + [HBM] * 3,
+        [HBM] * 6,
         shape((low, 2 * span + 128), BF16),
         HBM,
         scratch=[
+            pltpu.VMEM((slots, inner), F32),
+            pltpu.VMEM((slots, inner), F32),
             pltpu.VMEM((slots, width), BF16),
             pltpu.VMEM((low, width // 2), BF16),
             pltpu.VMEM((slots, width), BF16),
@@ -425,10 +431,10 @@
             pltpu.VMEM((low, 2 * span + 128), BF16),
         ],
         sems=40,
-        limit=50,
+        limit=54,
         flops=12 * slots * width * inner,
         moved=2**24,
-    )(got, silu, slope, hidden, gate_mat, up_mat, down_mat)
+    )(got, gated, upper, gate_mat, up_mat, down_mat)
     back = exchange(made)
     layer_out, input_grad = call(
         functools.partial(combine, experts=experts),

time: 149 us -> 148 us (level)
  no operation moved by 1% of the time
where the time goes in v4:
time: 148 us
  blocking collectives  47.6 us (32%)
  waiting for transfers between devices  42.8 us (29%)
  Pallas kernels  27.6 us (19%)
  starting transfers between devices  22.2 us (15%)
  local copies, waits for them, and re-layouts  6.9 us (5%)
    all_to_all x1, blocking collectives, exchange(): lax.all_to_all(blocks, 'expert', split_axis=0, concat_axis=0, tiled=True)  47.6 us
    all_to_all x2, waiting for transfers between devices, exchange(): lax.all_to_all(blocks, 'expert', split_axis=0, concat_axis=0, tiled=True)  30.8 us
    all_to_all x2, starting transfers between devices, exchange(): lax.all_to_all(blocks, 'expert', split_axis=0, concat_axis=0, tiled=True)  16.5 us
    pallas_call x1, Pallas kernels, body(): call(functools.partial(expert_both, sources=experts), [HBM] * 6, shape((l...  13.9 us
    ppermute x2, waiting for transfers between devices, passed_along(): return lax.ppermute(value, axis, pairs)  12 us
    unnamed x30, local copies, waits for them, and re-layouts  6.9 us
    ppermute x2, starting transfers between devices, passed_along(): return lax.ppermute(value, axis, pairs)  5.77 us
    pallas_call x1, Pallas kernels, body(): call(functools.partial(pack_both, experts=experts), [VMEM] * 7, (shape((l...  5.25 us
  transfers between devices with their start and end apart: 4, of which 2 were waited for; matrix products, arithmetic and copies ran while one was open for 0% of the time, Pallas kernels for 5%

profile of v4, /device:TPU:1, one launch (start us, length us, event | category | flops | bytes accessed | tf_op | source)
XLA Modules:
  0.0 147.9 jit_solution(6196053888051086764)
XLA Ops:
  0.6 0.0 copy-start.13
  0.6 0.0 copy-start.14
  0.6 3.0 %shard_map.114 = bf16[256,3072]{1,0:T(8,128)(2,1)} custom-call(bf16[128,2048]{1,0:T(8,128)(2,1)} %bitcast.24, bf16[1,2048]{1,0:T(2,128)(2,1)} %gain_ref.5, s32[2,128]{1,0:T(2,128)} %bitcast.41), custom_call_target="tpu_custom_call" | custom-call | flops 268435456 | bytes 4194304 | tf_op jit(solution)/shard_map/pallas_call | solution.py:381
  3.6 8.6 %all-to-all-start.1 = ((bf16[32,8,3072]{2,1,0:T(8,128)(2,1)}), bf16[32,8,3072]{2,1,0:T(8,128)(2,1)S(1)}, u32[]{:S(2)}, u32[]{:S(2)}) async-start(bf16[32,8,3072]{2,1,0:T(8,128)(2,1)} %bitcast.38), calls=%async_computation.1 | async-start | bytes 3145728 | tf_op jit(solution)/shard_map/all_to_all | solution.py:376
  12.2 0.0 copy-done.13
  12.2 1.7 %collective-permute-start.1 = (bf16[1,128,2048]{2,1,0:T(8,128)(2,1)S(1)}, bf16[1,128,2048]{2,1,0:T(8,128)(2,1)S(1)}, u32[]{:S(2)}, u32[]{:S(2)}) collective-permute-start(bf16[1,128,2048]{2,1,0:T(8,128)(2,1)S(1)} %copy-done.13), channel_id=1, source_target_pairs={{0,32},{32,64},{64,96},{96,128},{128,160},{160,192},{192,224},{224... | collective-permute-start | bytes 1572872 | tf_op jit(solution)/shard_map/ppermute | solution.py:25
  13.9 0.0 copy-done.14
  13.9 4.0 %collective-permute-start = (bf16[1,128,2048]{2,1,0:T(8,128)(2,1)S(1)}, bf16[1,128,2048]{2,1,0:T(8,128)(2,1)S(1)}, u32[]{:S(2)}, u32[]{:S(2)}) collective-permute-start(bf16[1,128,2048]{2,1,0:T(8,128)(2,1)S(1)} %copy-done.14), channel_id=1, source_target_pairs={{0,224},{32,0},{64,32},{96,64},{128,96},{160,128},{192,160},{224,1... | collective-permute-start | bytes 1572872 | tf_op jit(solution)/shard_map/ppermute | solution.py:25
  18.0 12.0 %collective-permute-done.1 = bf16[1,128,2048]{2,1,0:T(8,128)(2,1)S(1)} collective-permute-done((bf16[1,128,2048]{2,1,0:T(8,128)(2,1)S(1)}, bf16[1,128,2048]{2,1,0:T(8,128)(2,1)S(1)}, u32[]{:S(2)}, u32[]{:S(2)}) %collective-permute-start.1) | collective-permute-done | bytes 524320 | tf_op jit(solution)/shard_map/ppermute | solution.py:25
  29.9 0.0 collective-permute-done
  29.9 0.8 copy-done.2
  30.7 0.2 copy-done.4
  30.9 5.2 %shard_map.113 = (bf16[256,6144]{1,0:T(8,128)(2,1)}, bf16[128,3328]{1,0:T(8,128)(2,1)}, f32[128,128]{1,0:T(8,128)}) custom-call(bf16[128,2048]{1,0:T(8,128)(2,1)} %bitcast.25, bf16[128,2048]{1,0:T(8,128)(2,1)} %bitcast.30, bf16[128,2048]{1,0:T(8,128)(2,1)} %bitcast.28, bf16[1,2048]{1,0:T(2,128)(2,1)} %gain_ref.5, bf16[32,2048]{1,0:T(8,128)(2,1)} %bitcast.32, ...), custom_call_target="tpu_custom_call" | custom-call | flops 671088640 | bytes 8388608 | tf_op jit(solution)/shard_map/pallas_call | solution.py:392
  36.2 0.0 all-to-all-done.1
  36.2 7.9 %all-to-all-start = ((bf16[32,8,6144]{2,1,0:T(8,128)(2,1)}), bf16[32,8,6144]{2,1,0:T(8,128)(2,1)}, u32[]{:S(2)}, u32[]{:S(2)}) async-start(bf16[32,8,6144]{2,1,0:T(8,128)(2,1)} %bitcast.40), calls=%async_computation | async-start | bytes 6291456 | tf_op jit(solution)/shard_map/all_to_all | solution.py:376
  44.1 0.0 copy-start.9
  44.1 1.9 %copy-done.9 = bf16[1,1,2048,768]{3,2,1,0:T(8,128)(2,1)S(1)} copy-done((bf16[1,1,2048,768]{3,2,1,0:T(8,128)(2,1)S(1)}, bf16[1,1,2048,768]{3,2,1,0:T(8,128)(2,1)}, u32[]{:S(2)}) %copy-start.9) | copy-done | bytes 3145752
  46.0 1.9 %copy-done.10 = bf16[1,1,2048,768]{3,2,1,0:T(8,128)(2,1)S(1)} copy-done((bf16[1,1,2048,768]{3,2,1,0:T(8,128)(2,1)S(1)}, bf16[1,1,2048,768]{3,2,1,0:T(8,128)(2,1)}, u32[]{:S(2)}) %copy-start.10) | copy-done | bytes 3145752
  47.8 2.7 %shard_map.115 = (f32[384,768]{1,0:T(8,128)S(1)}, f32[384,768]{1,0:T(8,128)S(1)}) custom-call(bf16[256,3072]{1,0:T(8,128)(2,1)S(1)} %bitcast.27, bf16[2048,768]{1,0:T(8,128)(2,1)S(1)} %bitcast.35, bf16[2048,768]{1,0:T(8,128)(2,1)S(1)} %bitcast.37), custom_call_target="tpu_custom_call" | custom-call | flops 2415919104 | bytes 16777216 | tf_op jit(solution)/shard_map/pallas_call | solution.py:403
  50.6 1.0 copy-done.11
  51.6 1.1 copy-done.12
  52.7 30.8 %all-to-all-done = bf16[32,8,6144]{2,1,0:T(8,128)(2,1)} async-done(((bf16[32,8,6144]{2,1,0:T(8,128)(2,1)}), bf16[32,8,6144]{2,1,0:T(8,128)(2,1)}, u32[]{:S(2)}, u32[]{:S(2)}) %all-to-all-start) | async-done | bytes 3145760 | tf_op jit(solution)/shard_map/all_to_all | solution.py:376
  83.5 13.9 %shard_map.116 = bf16[256,6272]{1,0:T(8,128)(2,1)} custom-call(bf16[256,6144]{1,0:T(8,128)(2,1)} %bitcast.10.block_any, f32[384,768]{1,0:T(8,128)} %copy-done.11, f32[384,768]{1,0:T(8,128)} %copy-done.12, bf16[2048,768]{1,0:T(8,128)(2,1)} %bitcast.34, bf16[2048,768]{1,0:T(8,128)(2,1)} %bitcast.36, bf16[768,2048]{1,0:T(8,128)(2,1)} %bitcast.43), custom_call_target="tpu_custom_call" | custom-call | flops 7247757312 | bytes 16777216 | tf_op jit(solution)/shard_map/pallas_call | solution.py:413
  97.4 0.0 copy-start
  97.4 0.0 copy-start.3
  97.4 0.0 copy-start.5
  97.4 0.0 copy-start.6
  97.5 0.0 copy-start.8
  97.5 47.6 %all_to_all.15 = bf16[32,8,6272]{2,1,0:T(8,128)(2,1)S(1)} all-to-all(bf16[32,8,6272]{2,1,0:T(8,128)(2,1)} %bitcast.39), channel_id=1, replica_groups=mesh['section'=8,'expert'=32] {'expert'}, dimensions={0} | all-to-all | bytes 6422528 | tf_op jit(solution)/shard_map/all_to_all | solution.py:376
  145.1 0.0 copy-done
  145.1 0.0 copy-done.3
  145.1 2.8 %shard_map.117 = (bf16[128,2048]{1,0:T(8,128)(2,1)}, bf16[128,2048]{1,0:T(8,128)(2,1)}) custom-call(bf16[256,6272]{1,0:T(8,128)(2,1)S(1)} %bitcast.23, bf16[128,3328]{1,0:T(8,128)(2,1)S(1)} %copy-done.1, f32[128,128]{1,0:T(8,128)S(1)} %copy-done.7, bf16[128,2048]{1,0:T(8,128)(2,1)S(1)} %bitcast.29, bf16[128,2048]{1,0:T(8,128)(2,1)S(1)} %bitcast.26, ...), custom_call_target="tpu_custom_call" | custom-call | flops 1342177280 | bytes 8388608 | tf_op jit(solution)/shard_map/pallas_call | solution.py:439
  (12 shorter events, 0.0 us)
Async XLA Ops:
  0.6 11.6 %copy-start.13 = (bf16[1,128,2048]{2,1,0:T(8,128)(2,1)S(1)}, bf16[1,128,2048]{2,1,0:T(8,128)(2,1)}, u32[]{:S(2)}) copy-start(bf16[1,128,2048]{2,1,0:T(8,128)(2,1)} %param.10) | copy-start | bytes 1572868
  0.6 13.3 %copy-start.14 = (bf16[1,128,2048]{2,1,0:T(8,128)(2,1)S(1)}, bf16[1,128,2048]{2,1,0:T(8,128)(2,1)}, u32[]{:S(2)}) copy-start(bf16[1,128,2048]{2,1,0:T(8,128)(2,1)} %param.11) | copy-start | bytes 1572868
  3.6 32.6 %all-to-all-start.1 = ((bf16[32,8,3072]{2,1,0:T(8,128)(2,1)}), bf16[32,8,3072]{2,1,0:T(8,128)(2,1)S(1)}, u32[]{:S(2)}, u32[]{:S(2)}) async-start(bf16[32,8,3072]{2,1,0:T(8,128)(2,1)} %bitcast.38), calls=%async_computation.1 | async-start | bytes 3145728 | tf_op jit(solution)/shard_map/all_to_all | solution.py:376
  12.2 17.7 %collective-permute-start.1 = (bf16[1,128,2048]{2,1,0:T(8,128)(2,1)S(1)}, bf16[1,128,2048]{2,1,0:T(8,128)(2,1)S(1)}, u32[]{:S(2)}, u32[]{:S(2)}) collective-permute-start(bf16[1,128,2048]{2,1,0:T(8,128)(2,1)S(1)} %copy-done.13), channel_id=1, source_target_pairs={{0,32},{32,64},{64,96},{96,128},{128,160},{160,192},{192,224},{224... | collective-permute-start | bytes 1572872 | tf_op jit(solution)/shard_map/ppermute | solution.py:25
  13.9 16.0 %collective-permute-start = (bf16[1,128,2048]{2,1,0:T(8,128)(2,1)S(1)}, bf16[1,128,2048]{2,1,0:T(8,128)(2,1)S(1)}, u32[]{:S(2)}, u32[]{:S(2)}) collective-permute-start(bf16[1,128,2048]{2,1,0:T(8,128)(2,1)S(1)} %copy-done.14), channel_id=1, source_target_pairs={{0,224},{32,0},{64,32},{96,64},{128,96},{160,128},{192,160},{224,1... | collective-permute-start | bytes 1572872 | tf_op jit(solution)/shard_map/ppermute | solution.py:25
  29.9 0.8 copy-start.2
  29.9 1.0 copy-start.4
  36.2 47.3 %all-to-all-start = ((bf16[32,8,6144]{2,1,0:T(8,128)(2,1)}), bf16[32,8,6144]{2,1,0:T(8,128)(2,1)}, u32[]{:S(2)}, u32[]{:S(2)}) async-start(bf16[32,8,6144]{2,1,0:T(8,128)(2,1)} %bitcast.40), calls=%async_computation | async-start | bytes 6291456 | tf_op jit(solution)/shard_map/all_to_all | solution.py:376
  44.1 1.9 %copy-start.9 = (bf16[1,1,2048,768]{3,2,1,0:T(8,128)(2,1)S(1)}, bf16[1,1,2048,768]{3,2,1,0:T(8,128)(2,1)}, u32[]{:S(2)}) copy-start(bf16[1,1,2048,768]{3,2,1,0:T(8,128)(2,1)} %param.15) | copy-start | bytes 9437188
  46.0 1.9 %copy-start.10 = (bf16[1,1,2048,768]{3,2,1,0:T(8,128)(2,1)S(1)}, bf16[1,1,2048,768]{3,2,1,0:T(8,128)(2,1)}, u32[]{:S(2)}) copy-start(bf16[1,1,2048,768]{3,2,1,0:T(8,128)(2,1)} %param.16) | copy-start | bytes 9437188
  50.6 1.0 copy-start.11
  51.6 1.1 copy-start.12
  97.4 47.7 %copy-start = (bf16[1,128,2048]{2,1,0:T(8,128)(2,1)S(1)}, bf16[1,128,2048]{2,1,0:T(8,128)(2,1)}, u32[]{:S(2)}) copy-start(bf16[1,128,2048]{2,1,0:T(8,128)(2,1)} %param.12) | copy-start | bytes 1572868
  97.4 47.7 %copy-start.1 = (bf16[128,3328]{1,0:T(8,128)(2,1)S(1)}, bf16[128,3328]{1,0:T(8,128)(2,1)}, u32[]{:S(2)}) copy-start(bf16[128,3328]{1,0:T(8,128)(2,1)} %get-tuple-element.12.tables_ref) | copy-start | bytes 2555908
  97.4 47.7 %copy-start.3 = (bf16[1,128,2048]{2,1,0:T(8,128)(2,1)S(1)}, bf16[1,128,2048]{2,1,0:T(8,128)(2,1)}, u32[]{:S(2)}) copy-start(bf16[1,128,2048]{2,1,0:T(8,128)(2,1)} %copy-done.2) | copy-start | bytes 1572868
  97.4 47.7 %copy-start.5 = (bf16[1,128,2048]{2,1,0:T(8,128)(2,1)S(1)}, bf16[1,128,2048]{2,1,0:T(8,128)(2,1)}, u32[]{:S(2)}) copy-start(bf16[1,128,2048]{2,1,0:T(8,128)(2,1)} %copy-done.4) | copy-start | bytes 1572868
  97.4 47.7 %copy-start.6 = (bf16[1,2048,32]{1,2,0:T(8,128)(2,1)S(1)}, bf16[1,2048,32]{1,2,0:T(8,128)(2,1)}, u32[]{:S(2)}) copy-start(bf16[1,2048,32]{1,2,0:T(8,128)(2,1)} %param.14) | copy-start | bytes 393220
  97.4 47.7 %copy-start.7 = (f32[128,128]{1,0:T(8,128)S(1)}, f32[128,128]{1,0:T(8,128)}, u32[]{:S(2)}) copy-start(f32[128,128]{1,0:T(8,128)} %get-tuple-element.13.scalars_ref) | copy-start | bytes 196612
  97.5 47.7 %copy-start.8 = (bf16[1,2048]{1,0:T(2,128)(2,1)S(1)}, bf16[1,2048]{1,0:T(2,128)(2,1)}, u32[]{:S(2)}) copy-start(bf16[1,2048]{1,0:T(2,128)(2,1)} %gain_ref.5) | copy-start | bytes 12292

commit v5 on v4

--- a/solution.py
+++ b/solution.py
@@ -124,44 +124,61 @@
     return high, (value - high.astype(F32)).astype(BF16)
 
 
-def pack_both(
-    stored_ref, cotangent_ref, arrived_ref, gain_ref, router_ref, routes_b_ref, routes_f_ref,
-    out_ref, tables_ref, scalars_ref, made_ref, sems, *, experts,
+def save(kept, tables_ref, span):
+    for i, value in enumerate(kept):
+        tables_ref[:, i * span : (i + 1) * span] = value.T.astype(BF16)
+
+
+def prepare_stored(
+    stored_ref, gain_ref, router_ref, routes_ref, scaled_ref, tables_ref, scalars_ref, *, experts,
 ):
-    gain_row = gain_ref[...]
-    router_rows = router_ref[...]
-    rows, width = stored_ref.shape
+    rows = stored_ref.shape[0]
     span = experts * LOW
     at = iota((span, rows), 0)
-    copies = Copies(sems)
-
-    normed_b, inverse_b = normalized(stored_ref[...], gain_row)
-    found_b = places(routes_b_ref[...], experts)
-    weights_b, sig_b = weights_of(normed_b, router_rows, found_b)
-    scales = [w.astype(BF16).astype(F32) for w in weights_b]
-    spots_b = spots_of(found_b)
-    running = pack(cotangent_ref[...], [table(at, s, scales) for s in spots_b], made_ref, out_ref, 0, copies)
-    normed_f, _ = normalized(arrived_ref[...], gain_row)
-    found_f = places(routes_f_ref[...], experts)
-    spots_f = spots_of(found_f)
-    running += pack(normed_f, [table(at, s) for s in spots_f], made_ref, out_ref, width + width // 2, copies)
-    weights_f, _ = weights_of(normed_f, router_rows, found_f)
-
-    kept = [table(at, s) for s in spots_b]
-    kept += [jnp.where(at == s, 1.0, 0.0) for s in (*spots_b[0], *spots_b[1])]
-    for s in spots_f:
-        kept += [part.astype(F32) for part in split(table(at, s, weights_f))]
-    for i, value in enumerate(kept):
-        tables_ref[:, i * span : (i + 1) * span] = value.T.astype(BF16)
-
-    ratio = [jnp.where(s > 0.0, w / s, 1.0) for w, s in zip(weights_b, scales)]
-    routes_b = routes_b_ref[...].astype(F32)
-    lines = [*weights_b, *sig_b, *ratio, routes_b[0:1], routes_b[1:2]]
+    normed, inverse = normalized(stored_ref[...], gain_ref[...])
+    found = places(routes_ref[...], experts)
+    weights, sig = weights_of(normed, router_ref[...], found)
+    scales = [w.astype(BF16).astype(F32) for w in weights]
+    spots = spots_of(found)
+    for i, s in enumerate(spots):
+        scaled_ref[:, i * rows : (i + 1) * rows] = table(at, s, scales).astype(BF16)
+    kept = [table(at, s) for s in spots]
+    kept += [jnp.where(at == s, 1.0, 0.0) for s in (*spots[0], *spots[1])]
+    save(kept, tables_ref, span)
+    ratio = [jnp.where(s > 0.0, w / s, 1.0) for w, s in zip(weights, scales)]
+    routes = routes_ref[...].astype(F32)
+    lines = [*weights, *sig, *ratio, routes[0:1], routes[1:2]]
     line_at = iota((rows, rows), 0)
     scalars = jnp.zeros((rows, rows), F32)
     for i, value in enumerate(lines):
         scalars = jnp.where(line_at == i, value, scalars)
-    scalars_ref[...] = jnp.where(iota((rows, rows), 1) == len(lines), inverse_b, scalars.T)
+    scalars_ref[...] = jnp.where(iota((rows, rows), 1) == len(lines), inverse, scalars.T)
+
+
+def prepare_front(arrived_ref, gain_ref, router_ref, routes_ref, tables_ref, *, experts):
+    rows = arrived_ref.shape[0]
+    span = experts * LOW
+    at = iota((span, rows), 0)
+    normed, _ = normalized(arrived_ref[...], gain_ref[...])
+    found = places(routes_ref[...], experts)
+    weights, _ = weights_of(normed, router_ref[...], found)
+    kept = []
+    for s in spots_of(found):
+        kept += [part.astype(F32) for part in split(table(at, s, weights))]
+    save(kept, tables_ref, span)
+
+
+def pack_both(
+    cotangent_ref, arrived_ref, gain_ref, routes_ref, scaled_ref, out_ref, made_ref, sems, *, experts,
+):
+    rows, width = arrived_ref.shape
+    at = iota((experts * LOW, rows), 0)
+    copies = Copies(sems)
+    scaled = [scaled_ref[:, i * rows : (i + 1) * rows] for i in range(3)]
+    running = pack(cotangent_ref[...], scaled, made_ref, out_ref, 0, copies)
+    normed, _ = normalized(arrived_ref[...], gain_ref[...])
+    tables = [table(at, s) for s in spots_of(places(routes_ref[...], experts))]
+    running += pack(normed, tables, made_ref, out_ref, width + width // 2, copies)
     for copy in running:
         copy.wait()
 
@@ -297,7 +314,8 @@
 
 
 def combine(
-    back_ref, tables_ref, scalars_ref, arrived_ref, stored_ref, cotangent_ref, gain_ref, router_ref, layer_ref, grad_ref,
+    back_ref, front_ref, tables_ref, scalars_ref, arrived_ref, stored_ref, cotangent_ref, gain_ref, router_ref,
+    layer_ref, grad_ref,
     *, experts,
 ):
     rows, width = arrived_ref.shape
@@ -308,11 +326,14 @@
     def t(i):
         return tables_ref[:, i * slots : (i + 1) * slots]
 
+    def w(i):
+        return front_ref[:, i * slots : (i + 1) * slots]
+
     high = back_ref[:, span + width : 2 * span]
-    for s, side in ((0, 9), (1, 11)):
+    for s, side in ((0, 2), (1, 4)):
         cols = slice(s * half, (s + 1) * half)
         low = back_ref[:, span + s * half : span + (s + 1) * half]
-        mixed = mm(t(7), low) + mm(t(8), low) + mm(t(side), high) + mm(t(side + 1), high)
+        mixed = mm(w(0), low) + mm(w(1), low) + mm(w(side), high) + mm(w(side + 1), high)
         layer_ref[:, cols] = (arrived_ref[:, cols].astype(F32) + mixed).astype(BF16)
 
     w0, w1, s0, s1, r0, r1, e0, e1, inverse = (scalars_ref[:, i : i + 1] for i in range(9))
@@ -389,16 +410,32 @@
         moved=2**22,
     )(stored, norm_gain, routes_b)
     got_b = exchange(sent_b)
-    sent, tables, scalars = call(
+    scaled, tables, scalars = call(
+        functools.partial(prepare_stored, experts=experts),
+        [VMEM] * 4,
+        (shape((low, 3 * rows), BF16), shape((rows, 7 * low), BF16), shape((rows, rows), F32)),
+        (VMEM,) * 3,
+        flops=4 * low * rows * width,
+        moved=2**21,
+    )(stored, norm_gain, router_rows, routes_b)
+    sent = call(
         functools.partial(pack_both, experts=experts),
-        [VMEM] * 7,
-        (shape((low, 2 * span), BF16), shape((rows, 13 * low), BF16), shape((rows, rows), F32)),
-        (HBM, VMEM, VMEM),
+        [VMEM] * 5,
+        shape((low, 2 * span), BF16),
+        HBM,
         scratch=[pltpu.VMEM((low, 2 * span), BF16)],
         sems=6,
         flops=10 * low * rows * width,
         moved=2**23,
-    )(stored, cotangent, arrived, norm_gain, router_rows, routes_b, routes_f)
+    )(cotangent, arrived, norm_gain, routes_f, scaled)
+    front = call(
+        functools.partial(prepare_front, experts=experts),
+        [VMEM] * 4,
+        shape((rows, 6 * low), BF16),
+        VMEM,
+        flops=4 * low * rows * width,
+        moved=2**21,
+    )(arrived, norm_gain, router_rows, routes_f)
     got = exchange(sent)
     gated, upper = call(
         functools.partial(expert_stored, sources=experts),
@@ -438,13 +475,13 @@
     back = exchange(made)
     layer_out, input_grad = call(
         functools.partial(combine, experts=experts),
-        [VMEM] * 8,
+        [VMEM] * 9,
         (shape((rows, width), BF16), shape((rows, width), BF16)),
         (VMEM, VMEM),
         limit=48,
         flops=20 * low * rows * width,
         moved=2**23,
-    )(back, tables, scalars, arrived, stored, cotangent, norm_gain, router_rows)
+    )(back, front, tables, scalars, arrived, stored, cotangent, norm_gain, router_rows)
     return layer_out[None], input_grad[None]
 
 

time: 148 us -> 153 us (1.034); the launches traced: 148 us -> 151 us
  blocking collectives: 47.6 us -> 0 us
  waiting for transfers between devices: 42.8 us -> 77.8 us
  starting transfers between devices: 22.2 us -> 28.9 us
  local copies, waits for them, and re-layouts: 6.9 us -> 12 us
  Pallas kernels: 27.6 us -> 31.2 us
    all_to_all x1 -> x0, blocking collectives: 47.6 us -> none  [exchange(): lax.all_to_all(blocks, 'expert', split_axis=0, concat_axis=0, tiled=True)]
    all_to_all x2 -> x3, waiting for transfers between devices: 30.8 us -> 68.5 us  [exchange(): lax.all_to_all(blocks, 'expert', split_axis=0, concat_axis=0, tiled=True)]
    all_to_all x2 -> x3, starting transfers between devices: 16.5 us -> 23.2 us  [exchange(): lax.all_to_all(blocks, 'expert', split_axis=0, concat_axis=0, tiled=True)]
    unnamed x30 -> x32, local copies, waits for them, and re-layouts: 6.9 us -> 12 us
    pallas_call x2 -> x4, Pallas kernels: 8.05 us -> 11.6 us  [the longest x1 3.63 us: body(): call(functools.partial(pack_both, experts=experts), [VMEM] * 5, shape((lo...]
    ppermute x2, waiting for transfers between devices: 12 us -> 9.3 us  [passed_along(): return lax.ppermute(value, axis, pairs)]
  transfers between devices with their start and end apart: 4 -> 5, of which waited for: 2 -> 3; matrix products, arithmetic and copies ran while one was open for 0% -> 0% of each run, Pallas kernels for 5% -> 8%
where the time goes in v5:
time: 153 us; the launch traced here: 151 us
  waiting for transfers between devices  77.8 us (51%)
  Pallas kernels  31.2 us (20%)
  starting transfers between devices  28.9 us (19%)
  local copies, waits for them, and re-layouts  12 us (8%)
    all_to_all x3, waiting for transfers between devices, exchange(): lax.all_to_all(blocks, 'expert', split_axis=0, concat_axis=0, tiled=True)  68.5 us
    all_to_all x3, starting transfers between devices, exchange(): lax.all_to_all(blocks, 'expert', split_axis=0, concat_axis=0, tiled=True)  23.2 us
    pallas_call x1, Pallas kernels, body(): call(functools.partial(expert_both, sources=experts), [HBM] * 6, shape((l...  13.8 us
    unnamed x32, local copies, waits for them, and re-layouts  12 us
    ppermute x2, waiting for transfers between devices, passed_along(): return lax.ppermute(value, axis, pairs)  9.3 us
    ppermute x2, starting transfers between devices, passed_along(): return lax.ppermute(value, axis, pairs)  5.77 us
    pallas_call x1, Pallas kernels, body(): call(functools.partial(pack_both, experts=experts), [VMEM] * 5, shape((lo...  3.63 us
  transfers between devices with their start and end apart: 5, of which 3 were waited for; matrix products, arithmetic and copies ran while one was open for 0% of the time, Pallas kernels for 8%

profile of v5, /device:TPU:1, one launch (start us, length us, event | category | flops | bytes accessed | tf_op | source)
XLA Modules:
  0.0 150.7 jit_solution(1607731123169832720)
XLA Ops:
  0.6 2.9 %shard_map.115 = bf16[256,3072]{1,0:T(8,128)(2,1)} custom-call(bf16[128,2048]{1,0:T(8,128)(2,1)} %bitcast.29, bf16[1,2048]{1,0:T(2,128)(2,1)} %gain_ref.9, s32[2,128]{1,0:T(2,128)} %bitcast.45), custom_call_target="tpu_custom_call" | custom-call | flops 268435456 | bytes 4194304 | tf_op jit(solution)/shard_map/pallas_call | solution.py:402
  3.6 8.6 %all-to-all-start.1 = ((bf16[32,8,3072]{2,1,0:T(8,128)(2,1)}), bf16[32,8,3072]{2,1,0:T(8,128)(2,1)S(1)}, u32[]{:S(2)}, u32[]{:S(2)}) async-start(bf16[32,8,3072]{2,1,0:T(8,128)(2,1)} %bitcast.41), calls=%async_computation.1 | async-start | bytes 3145728 | tf_op jit(solution)/shard_map/all_to_all | solution.py:397
  12.2 1.7 %collective-permute-start.1 = (bf16[1,128,2048]{2,1,0:T(8,128)(2,1)S(1)}, bf16[1,128,2048]{2,1,0:T(8,128)(2,1)S(1)}, u32[]{:S(2)}, u32[]{:S(2)}) collective-permute-start(bf16[1,128,2048]{2,1,0:T(8,128)(2,1)S(1)} %copy-done.14), channel_id=1, source_target_pairs={{0,32},{32,64},{64,96},{96,128},{128,160},{160,192},{192,224},{224... | collective-permute-start | bytes 1572872 | tf_op jit(solution)/shard_map/ppermute | solution.py:25
  13.9 4.0 %collective-permute-start = (bf16[1,128,2048]{2,1,0:T(8,128)(2,1)S(1)}, bf16[1,128,2048]{2,1,0:T(8,128)(2,1)S(1)}, u32[]{:S(2)}, u32[]{:S(2)}) collective-permute-start(bf16[1,128,2048]{2,1,0:T(8,128)(2,1)S(1)} %copy-done.15), channel_id=1, source_target_pairs={{0,224},{32,0},{64,32},{96,64},{128,96},{160,128},{192,160},{224,1... | collective-permute-start | bytes 1572872 | tf_op jit(solution)/shard_map/ppermute | solution.py:25
  18.0 2.7 %shard_map.113 = (bf16[256,384]{1,0:T(8,128)(2,1)}, bf16[128,1792]{1,0:T(8,128)(2,1)}, f32[128,128]{1,0:T(8,128)}) custom-call(bf16[128,2048]{1,0:T(8,128)(2,1)} %bitcast.30, bf16[1,2048]{1,0:T(2,128)(2,1)} %gain_ref.9, bf16[32,2048]{1,0:T(8,128)(2,1)} %bitcast.33, s32[2,128]{1,0:T(2,128)} %bitcast.46), custom_call_target="tpu_custom_call" | custom-call | flops 268435456 | bytes 2097152 | tf_op jit(solution)/shard_map/pallas_call | solution.py:413
  20.6 9.3 %collective-permute-done.1 = bf16[1,128,2048]{2,1,0:T(8,128)(2,1)S(1)} collective-permute-done((bf16[1,128,2048]{2,1,0:T(8,128)(2,1)S(1)}, bf16[1,128,2048]{2,1,0:T(8,128)(2,1)S(1)}, u32[]{:S(2)}, u32[]{:S(2)}) %collective-permute-start.1) | collective-permute-done | bytes 524320 | tf_op jit(solution)/shard_map/ppermute | solution.py:25
  29.9 0.0 collective-permute-done
  29.9 0.8 copy-done
  30.7 0.2 copy-done.2
  30.9 3.6 %shard_map.114 = bf16[256,6144]{1,0:T(8,128)(2,1)} custom-call(bf16[128,2048]{1,0:T(8,128)(2,1)} %bitcast.27, bf16[128,2048]{1,0:T(8,128)(2,1)} %bitcast.24, bf16[1,2048]{1,0:T(2,128)(2,1)} %gain_ref.9, s32[2,128]{1,0:T(2,128)} %bitcast.43, bf16[256,384]{1,0:T(8,128)(2,1)} %get-tuple-element.9.scaled_ref), custom_call_target="tpu_custom_call" | custom-call | flops 671088640 | bytes 8388608 | tf_op jit(solution)/shard_map/pallas_call | solution.py:421
  34.5 0.0 all-to-all-done.1
  34.5 7.9 %all-to-all-start = ((bf16[32,8,6144]{2,1,0:T(8,128)(2,1)}), bf16[32,8,6144]{2,1,0:T(8,128)(2,1)}, u32[]{:S(2)}, u32[]{:S(2)}) async-start(bf16[32,8,6144]{2,1,0:T(8,128)(2,1)} %bitcast.40), calls=%async_computation | async-start | bytes 6291456 | tf_op jit(solution)/shard_map/all_to_all | solution.py:397
  42.4 0.0 copy-start.10
  42.4 1.9 %copy-done.10 = bf16[1,1,2048,768]{3,2,1,0:T(8,128)(2,1)S(1)} copy-done((bf16[1,1,2048,768]{3,2,1,0:T(8,128)(2,1)S(1)}, bf16[1,1,2048,768]{3,2,1,0:T(8,128)(2,1)}, u32[]{:S(2)}) %copy-start.10) | copy-done | bytes 3145752
  44.3 1.9 %copy-done.11 = bf16[1,1,2048,768]{3,2,1,0:T(8,128)(2,1)S(1)} copy-done((bf16[1,1,2048,768]{3,2,1,0:T(8,128)(2,1)S(1)}, bf16[1,1,2048,768]{3,2,1,0:T(8,128)(2,1)}, u32[]{:S(2)}) %copy-start.11) | copy-done | bytes 3145752
  46.2 2.7 %shard_map.116 = (f32[384,768]{1,0:T(8,128)S(1)}, f32[384,768]{1,0:T(8,128)S(1)}) custom-call(bf16[256,3072]{1,0:T(8,128)(2,1)S(1)} %bitcast.32, bf16[2048,768]{1,0:T(8,128)(2,1)S(1)} %bitcast.37, bf16[2048,768]{1,0:T(8,128)(2,1)S(1)} %bitcast.39), custom_call_target="tpu_custom_call" | custom-call | flops 2415919104 | bytes 16777216 | tf_op jit(solution)/shard_map/pallas_call | solution.py:440
  49.0 1.0 copy-done.12
  50.0 1.1 copy-done.13
  51.1 30.8 %all-to-all-done = bf16[32,8,6144]{2,1,0:T(8,128)(2,1)} async-done(((bf16[32,8,6144]{2,1,0:T(8,128)(2,1)}), bf16[32,8,6144]{2,1,0:T(8,128)(2,1)}, u32[]{:S(2)}, u32[]{:S(2)}) %all-to-all-start) | async-done | bytes 3145760 | tf_op jit(solution)/shard_map/all_to_all | solution.py:397
  81.9 13.8 %shard_map.117 = bf16[256,6272]{1,0:T(8,128)(2,1)} custom-call(bf16[256,6144]{1,0:T(8,128)(2,1)} %bitcast.10.block_any, f32[384,768]{1,0:T(8,128)} %copy-done.12, f32[384,768]{1,0:T(8,128)} %copy-done.13, bf16[2048,768]{1,0:T(8,128)(2,1)} %bitcast.36, bf16[2048,768]{1,0:T(8,128)(2,1)} %bitcast.38, bf16[768,2048]{1,0:T(8,128)(2,1)} %bitcast.47), custom_call_target="tpu_custom_call" | custom-call | flops 7247757312 | bytes 16777216 | tf_op jit(solution)/shard_map/pallas_call | solution.py:450
  95.7 0.0 copy-start.6
  95.7 0.0 copy-start.8
  95.8 6.7 %all-to-all-start.2 = ((bf16[32,8,6272]{2,1,0:T(8,128)(2,1)}), bf16[32,8,6272]{2,1,0:T(8,128)(2,1)S(1)}, u32[]{:S(2)}, u32[]{:S(2)}) async-start(bf16[32,8,6272]{2,1,0:T(8,128)(2,1)} %bitcast.42), calls=%async_computation.2 | async-start | bytes 6422528 | tf_op jit(solution)/shard_map/all_to_all | solution.py:397
  102.5 2.5 %shard_map.118.front_ref = bf16[128,1536]{1,0:T(8,128)(2,1)} custom-call(bf16[128,2048]{1,0:T(8,128)(2,1)} %bitcast.25, bf16[1,2048]{1,0:T(2,128)(2,1)} %gain_ref.9, bf16[32,2048]{1,0:T(8,128)(2,1)} %bitcast.34, s32[2,128]{1,0:T(2,128)} %bitcast.44), custom_call_target="tpu_custom_call" | custom-call | flops 268435456 | bytes 2097152 | tf_op jit(solution)/shard_map/pallas_call | solution.py:431
  105.0 37.7 %all-to-all-done.2 = bf16[32,8,6272]{2,1,0:T(8,128)(2,1)S(1)} async-done(((bf16[32,8,6272]{2,1,0:T(8,128)(2,1)}), bf16[32,8,6272]{2,1,0:T(8,128)(2,1)S(1)}, u32[]{:S(2)}, u32[]{:S(2)}) %all-to-all-start.2) | async-done | bytes 3211296 | tf_op jit(solution)/shard_map/all_to_all | solution.py:397
  142.7 0.0 copy-start.1
  142.7 1.0 copy-done.1
  143.8 1.0 copy-done.3
  144.8 1.0 copy-done.4
  145.9 1.0 copy-done.5
  146.9 1.0 copy-done.7
  147.9 2.8 %shard_map.119 = (bf16[128,2048]{1,0:T(8,128)(2,1)}, bf16[128,2048]{1,0:T(8,128)(2,1)}) custom-call(bf16[256,6272]{1,0:T(8,128)(2,1)S(1)} %bitcast.23, bf16[128,1536]{1,0:T(8,128)(2,1)S(1)} %copy-done.5, bf16[128,1792]{1,0:T(8,128)(2,1)S(1)} %copy-done.7, f32[128,128]{1,0:T(8,128)S(1)} %copy-done.9, bf16[128,2048]{1,0:T(8,128)(2,1)S(1)} %bitcast.26, ...), custom_call_target="tpu_custom_call" | custom-call | flops 1342177280 | bytes 8388608 | tf_op jit(solution)/shard_map/pallas_call | solution.py:476
  (17 shorter events, 0.0 us)
Async XLA Ops:
  0.6 11.6 %copy-start.14 = (bf16[1,128,2048]{2,1,0:T(8,128)(2,1)S(1)}, bf16[1,128,2048]{2,1,0:T(8,128)(2,1)}, u32[]{:S(2)}) copy-start(bf16[1,128,2048]{2,1,0:T(8,128)(2,1)} %param.10) | copy-start | bytes 1572868
  0.6 13.3 %copy-start.15 = (bf16[1,128,2048]{2,1,0:T(8,128)(2,1)S(1)}, bf16[1,128,2048]{2,1,0:T(8,128)(2,1)}, u32[]{:S(2)}) copy-start(bf16[1,128,2048]{2,1,0:T(8,128)(2,1)} %param.11) | copy-start | bytes 1572868
  3.6 30.9 %all-to-all-start.1 = ((bf16[32,8,3072]{2,1,0:T(8,128)(2,1)}), bf16[32,8,3072]{2,1,0:T(8,128)(2,1)S(1)}, u32[]{:S(2)}, u32[]{:S(2)}) async-start(bf16[32,8,3072]{2,1,0:T(8,128)(2,1)} %bitcast.41), calls=%async_computation.1 | async-start | bytes 3145728 | tf_op jit(solution)/shard_map/all_to_all | solution.py:397
  12.2 17.7 %collective-permute-start.1 = (bf16[1,128,2048]{2,1,0:T(8,128)(2,1)S(1)}, bf16[1,128,2048]{2,1,0:T(8,128)(2,1)S(1)}, u32[]{:S(2)}, u32[]{:S(2)}) collective-permute-start(bf16[1,128,2048]{2,1,0:T(8,128)(2,1)S(1)} %copy-done.14), channel_id=1, source_target_pairs={{0,32},{32,64},{64,96},{96,128},{128,160},{160,192},{192,224},{224... | collective-permute-start | bytes 1572872 | tf_op jit(solution)/shard_map/ppermute | solution.py:25
  13.9 16.0 %collective-permute-start = (bf16[1,128,2048]{2,1,0:T(8,128)(2,1)S(1)}, bf16[1,128,2048]{2,1,0:T(8,128)(2,1)S(1)}, u32[]{:S(2)}, u32[]{:S(2)}) collective-permute-start(bf16[1,128,2048]{2,1,0:T(8,128)(2,1)S(1)} %copy-done.15), channel_id=1, source_target_pairs={{0,224},{32,0},{64,32},{96,64},{128,96},{160,128},{192,160},{224,1... | collective-permute-start | bytes 1572872 | tf_op jit(solution)/shard_map/ppermute | solution.py:25
  29.9 0.8 copy-start
  29.9 1.0 copy-start.2
  34.5 47.3 %all-to-all-start = ((bf16[32,8,6144]{2,1,0:T(8,128)(2,1)}), bf16[32,8,6144]{2,1,0:T(8,128)(2,1)}, u32[]{:S(2)}, u32[]{:S(2)}) async-start(bf16[32,8,6144]{2,1,0:T(8,128)(2,1)} %bitcast.40), calls=%async_computation | async-start | bytes 6291456 | tf_op jit(solution)/shard_map/all_to_all | solution.py:397
  42.4 1.9 %copy-start.10 = (bf16[1,1,2048,768]{3,2,1,0:T(8,128)(2,1)S(1)}, bf16[1,1,2048,768]{3,2,1,0:T(8,128)(2,1)}, u32[]{:S(2)}) copy-start(bf16[1,1,2048,768]{3,2,1,0:T(8,128)(2,1)} %param.15) | copy-start | bytes 9437188
  44.3 1.9 %copy-start.11 = (bf16[1,1,2048,768]{3,2,1,0:T(8,128)(2,1)S(1)}, bf16[1,1,2048,768]{3,2,1,0:T(8,128)(2,1)}, u32[]{:S(2)}) copy-start(bf16[1,1,2048,768]{3,2,1,0:T(8,128)(2,1)} %param.16) | copy-start | bytes 9437188
  48.9 1.0 copy-start.12
  50.0 1.1 copy-start.13
  95.7 47.0 %copy-start.6 = (bf16[1,2048,32]{1,2,0:T(8,128)(2,1)S(1)}, bf16[1,2048,32]{1,2,0:T(8,128)(2,1)}, u32[]{:S(2)}) copy-start(bf16[1,2048,32]{1,2,0:T(8,128)(2,1)} %param.14) | copy-start | bytes 393220
  95.7 47.0 %copy-start.8 = (bf16[1,2048]{1,0:T(2,128)(2,1)S(1)}, bf16[1,2048]{1,0:T(2,128)(2,1)}, u32[]{:S(2)}) copy-start(bf16[1,2048]{1,0:T(2,128)(2,1)} %gain_ref.9) | copy-start | bytes 12292
  95.7 47.0 %copy-start.9 = (f32[128,128]{1,0:T(8,128)S(1)}, f32[128,128]{1,0:T(8,128)}, u32[]{:S(2)}) copy-start(f32[128,128]{1,0:T(8,128)} %get-tuple-element.13.scalars_ref) | copy-start | bytes 196612
  95.8 47.0 %all-to-all-start.2 = ((bf16[32,8,6272]{2,1,0:T(8,128)(2,1)}), bf16[32,8,6272]{2,1,0:T(8,128)(2,1)S(1)}, u32[]{:S(2)}, u32[]{:S(2)}) async-start(bf16[32,8,6272]{2,1,0:T(8,128)(2,1)} %bitcast.42), calls=%async_computation.2 | async-start | bytes 6422528 | tf_op jit(solution)/shard_map/all_to_all | solution.py:397
  142.7 1.0 copy-start.1
  143.8 1.0 copy-start.3
  144.8 1.0 copy-start.4
  145.9 1.0 copy-start.5
  146.9 1.0 copy-start.7

commit v6 on v5

--- a/solution.py
+++ b/solution.py
@@ -101,11 +101,10 @@
     return running
 
 
-def pack_stored(stored_ref, gain_ref, routes_ref, out_ref, made_ref, sems, *, experts):
+def pack_stored(stored_ref, routes_ref, out_ref, made_ref, sems, *, experts):
     found = places(routes_ref[...], experts)
     at = iota((experts * LOW, routes_ref.shape[1]), 0)
-    normed, _ = normalized(stored_ref[...], gain_ref[...])
-    for copy in pack(normed, [table(at, s) for s in spots_of(found)], made_ref, out_ref, 0, Copies(sems)):
+    for copy in pack(stored_ref[...], [table(at, s) for s in spots_of(found)], made_ref, out_ref, 0, Copies(sems)):
         copy.wait()
 
 
@@ -205,11 +204,13 @@
     rows_ref[low:, half:] = mm(take_right, part).astype(BF16)
 
 
-def expert_stored(block_ref, gate_ref, up_ref, gated_ref, upper_ref, rows_ref, *, sources):
+def expert_stored(block_ref, gain_ref, gate_ref, up_ref, gated_ref, upper_ref, rows_ref, *, sources):
     low = sources * LOW
     width = rows_ref.shape[1]
     rows_ref[:low, :] = block_ref[:, :width]
     join_halves(rows_ref, block_ref[:, width:], sources)
+    for r in range(0, rows_ref.shape[0], 128):
+        rows_ref[r : r + 128, :], _ = normalized(rows_ref[r : r + 128, :], gain_ref[...])
     rows = rows_ref[...]
     for f in range(0, gate_ref.shape[1], 256):
         gated_ref[:, f : f + 256] = mm(rows, gate_ref[:, f : f + 256])
@@ -401,14 +402,14 @@
 
     sent_b = call(
         functools.partial(pack_stored, experts=experts),
-        [VMEM] * 3,
+        [VMEM] * 2,
         shape((low, span), BF16),
         HBM,
         scratch=[pltpu.VMEM((low, span), BF16)],
         sems=3,
         flops=4 * low * rows * width,
         moved=2**22,
-    )(stored, norm_gain, routes_b)
+    )(stored, routes_b)
     got_b = exchange(sent_b)
     scaled, tables, scalars = call(
         functools.partial(prepare_stored, experts=experts),
@@ -439,14 +440,14 @@
     got = exchange(sent)
     gated, upper = call(
         functools.partial(expert_stored, sources=experts),
-        [VMEM] * 3,
+        [VMEM] * 4,
         (shape((slots, inner), F32), shape((slots, inner), F32)),
         (VMEM, VMEM),
         scratch=[pltpu.VMEM((slots, width), BF16)],
         limit=40,
         flops=4 * slots * width * inner,
         moved=2**24,
-    )(got_b, gate_mat, up_mat)
+    )(got_b, norm_gain, gate_mat, up_mat)
     made = call(
         functools.partial(expert_both, sources=experts),
         [HBM] * 6,

time: 153 us -> 152 us (level)
    unnamed x32 -> x34, local copies, waits for them, and re-layouts: 12 us -> 12 us
where the time goes in v6:
time: 152 us; the launch traced here: 151 us
  waiting for transfers between devices  77.5 us (51%)
  Pallas kernels  31.4 us (21%)
  starting transfers between devices  28.9 us (19%)
  local copies, waits for them, and re-layouts  12 us (8%)
    all_to_all x3, waiting for transfers between devices, exchange(): lax.all_to_all(blocks, 'expert', split_axis=0, concat_axis=0, tiled=True)  68.2 us
    all_to_all x3, starting transfers between devices, exchange(): lax.all_to_all(blocks, 'expert', split_axis=0, concat_axis=0, tiled=True)  23.2 us
    pallas_call x1, Pallas kernels, body(): call(functools.partial(expert_both, sources=experts), [HBM] * 6, shape((l...  13.9 us
    unnamed x34, local copies, waits for them, and re-layouts  12 us
    ppermute x2, waiting for transfers between devices, passed_along(): return lax.ppermute(value, axis, pairs)  9.3 us
    ppermute x2, starting transfers between devices, passed_along(): return lax.ppermute(value, axis, pairs)  5.75 us
    pallas_call x1, Pallas kernels, body(): call(functools.partial(pack_both, experts=experts), [VMEM] * 5, shape((lo...  3.63 us
    pallas_call x1, Pallas kernels, body(): call(functools.partial(expert_stored, sources=experts), [VMEM] * 4, (shap...  3.07 us
  transfers between devices with their start and end apart: 5, of which 3 were waited for; matrix products, arithmetic and copies ran while one was open for 0% of the time, Pallas kernels for 8%

profile of v6, /device:TPU:1, one launch (start us, length us, event | category | flops | bytes accessed | tf_op | source)
XLA Modules:
  0.0 150.6 jit_solution(15402881763652266778)
XLA Ops:
  0.6 2.8 %shard_map.115 = bf16[256,3072]{1,0:T(8,128)(2,1)} custom-call(bf16[128,2048]{1,0:T(8,128)(2,1)} %bitcast.29, s32[2,128]{1,0:T(2,128)} %bitcast.45), custom_call_target="tpu_custom_call" | custom-call | flops 268435456 | bytes 4194304 | tf_op jit(solution)/shard_map/pallas_call | solution.py:403
  3.5 8.6 %all-to-all-start.1 = ((bf16[32,8,3072]{2,1,0:T(8,128)(2,1)}), bf16[32,8,3072]{2,1,0:T(8,128)(2,1)S(1)}, u32[]{:S(2)}, u32[]{:S(2)}) async-start(bf16[32,8,3072]{2,1,0:T(8,128)(2,1)} %bitcast.41), calls=%async_computation.1 | async-start | bytes 3145728 | tf_op jit(solution)/shard_map/all_to_all | solution.py:398
  12.1 1.7 %collective-permute-start.1 = (bf16[1,128,2048]{2,1,0:T(8,128)(2,1)S(1)}, bf16[1,128,2048]{2,1,0:T(8,128)(2,1)S(1)}, u32[]{:S(2)}, u32[]{:S(2)}) collective-permute-start(bf16[1,128,2048]{2,1,0:T(8,128)(2,1)S(1)} %copy-done.15), channel_id=1, source_target_pairs={{0,32},{32,64},{64,96},{96,128},{128,160},{160,192},{192,224},{224... | collective-permute-start | bytes 1572872 | tf_op jit(solution)/shard_map/ppermute | solution.py:25
  13.8 4.0 %collective-permute-start = (bf16[1,128,2048]{2,1,0:T(8,128)(2,1)S(1)}, bf16[1,128,2048]{2,1,0:T(8,128)(2,1)S(1)}, u32[]{:S(2)}, u32[]{:S(2)}) collective-permute-start(bf16[1,128,2048]{2,1,0:T(8,128)(2,1)S(1)} %copy-done.16), channel_id=1, source_target_pairs={{0,224},{32,0},{64,32},{96,64},{128,96},{160,128},{192,160},{224,1... | collective-permute-start | bytes 1572872 | tf_op jit(solution)/shard_map/ppermute | solution.py:25
  17.9 2.7 %shard_map.113 = (bf16[256,384]{1,0:T(8,128)(2,1)}, bf16[128,1792]{1,0:T(8,128)(2,1)}, f32[128,128]{1,0:T(8,128)}) custom-call(bf16[128,2048]{1,0:T(8,128)(2,1)} %bitcast.30, bf16[1,2048]{1,0:T(2,128)(2,1)} %gain_ref.9, bf16[32,2048]{1,0:T(8,128)(2,1)} %bitcast.33, s32[2,128]{1,0:T(2,128)} %bitcast.46), custom_call_target="tpu_custom_call" | custom-call | flops 268435456 | bytes 2097152 | tf_op jit(solution)/shard_map/pallas_call | solution.py:414
  20.5 9.3 %collective-permute-done.1 = bf16[1,128,2048]{2,1,0:T(8,128)(2,1)S(1)} collective-permute-done((bf16[1,128,2048]{2,1,0:T(8,128)(2,1)S(1)}, bf16[1,128,2048]{2,1,0:T(8,128)(2,1)S(1)}, u32[]{:S(2)}, u32[]{:S(2)}) %collective-permute-start.1) | collective-permute-done | bytes 524320 | tf_op jit(solution)/shard_map/ppermute | solution.py:25
  29.8 0.8 copy-done
  30.6 0.2 copy-done.2
  30.8 3.6 %shard_map.114 = bf16[256,6144]{1,0:T(8,128)(2,1)} custom-call(bf16[128,2048]{1,0:T(8,128)(2,1)} %bitcast.27, bf16[128,2048]{1,0:T(8,128)(2,1)} %bitcast.24, bf16[1,2048]{1,0:T(2,128)(2,1)} %gain_ref.9, s32[2,128]{1,0:T(2,128)} %bitcast.43, bf16[256,384]{1,0:T(8,128)(2,1)} %get-tuple-element.9.scaled_ref), custom_call_target="tpu_custom_call" | custom-call | flops 671088640 | bytes 8388608 | tf_op jit(solution)/shard_map/pallas_call | solution.py:422
  34.4 0.0 all-to-all-done.1
  34.4 0.0 copy-start.8
  34.5 7.9 %all-to-all-start = ((bf16[32,8,6144]{2,1,0:T(8,128)(2,1)}), bf16[32,8,6144]{2,1,0:T(8,128)(2,1)}, u32[]{:S(2)}, u32[]{:S(2)}) async-start(bf16[32,8,6144]{2,1,0:T(8,128)(2,1)} %bitcast.40), calls=%async_computation | async-start | bytes 6291456 | tf_op jit(solution)/shard_map/all_to_all | solution.py:398
  42.4 0.0 copy-start.11
  42.4 1.9 %copy-done.11 = bf16[1,1,2048,768]{3,2,1,0:T(8,128)(2,1)S(1)} copy-done((bf16[1,1,2048,768]{3,2,1,0:T(8,128)(2,1)S(1)}, bf16[1,1,2048,768]{3,2,1,0:T(8,128)(2,1)}, u32[]{:S(2)}) %copy-start.11) | copy-done | bytes 3145752
  44.3 1.9 %copy-done.12 = bf16[1,1,2048,768]{3,2,1,0:T(8,128)(2,1)S(1)} copy-done((bf16[1,1,2048,768]{3,2,1,0:T(8,128)(2,1)S(1)}, bf16[1,1,2048,768]{3,2,1,0:T(8,128)(2,1)}, u32[]{:S(2)}) %copy-start.12) | copy-done | bytes 3145752
  46.1 3.1 %shard_map.116 = (f32[384,768]{1,0:T(8,128)S(1)}, f32[384,768]{1,0:T(8,128)S(1)}) custom-call(bf16[256,3072]{1,0:T(8,128)(2,1)S(1)} %bitcast.32, bf16[1,2048]{1,0:T(2,128)(2,1)S(1)} %copy-done.8, bf16[2048,768]{1,0:T(8,128)(2,1)S(1)} %bitcast.37, bf16[2048,768]{1,0:T(8,128)(2,1)S(1)} %bitcast.39), custom_call_target="tpu_custom_call" | custom-call | flops 2415919104 | bytes 16777216 | tf_op jit(solution)/shard_map/pallas_call | solution.py:441
  49.2 1.0 copy-done.13
  50.2 1.1 copy-done.14
  51.3 30.4 %all-to-all-done = bf16[32,8,6144]{2,1,0:T(8,128)(2,1)} async-done(((bf16[32,8,6144]{2,1,0:T(8,128)(2,1)}), bf16[32,8,6144]{2,1,0:T(8,128)(2,1)}, u32[]{:S(2)}, u32[]{:S(2)}) %all-to-all-start) | async-done | bytes 3145760 | tf_op jit(solution)/shard_map/all_to_all | solution.py:398
  81.8 13.9 %shard_map.117 = bf16[256,6272]{1,0:T(8,128)(2,1)} custom-call(bf16[256,6144]{1,0:T(8,128)(2,1)} %bitcast.10.block_any, f32[384,768]{1,0:T(8,128)} %copy-done.13, f32[384,768]{1,0:T(8,128)} %copy-done.14, bf16[2048,768]{1,0:T(8,128)(2,1)} %bitcast.36, bf16[2048,768]{1,0:T(8,128)(2,1)} %bitcast.38, bf16[768,2048]{1,0:T(8,128)(2,1)} %bitcast.47), custom_call_target="tpu_custom_call" | custom-call | flops 7247757312 | bytes 16777216 | tf_op jit(solution)/shard_map/pallas_call | solution.py:451
  95.7 0.0 copy-start.6
  95.7 0.0 copy-start.9
  95.7 6.7 %all-to-all-start.2 = ((bf16[32,8,6272]{2,1,0:T(8,128)(2,1)}), bf16[32,8,6272]{2,1,0:T(8,128)(2,1)S(1)}, u32[]{:S(2)}, u32[]{:S(2)}) async-start(bf16[32,8,6272]{2,1,0:T(8,128)(2,1)} %bitcast.42), calls=%async_computation.2 | async-start | bytes 6422528 | tf_op jit(solution)/shard_map/all_to_all | solution.py:398
  102.4 2.5 %shard_map.118.front_ref = bf16[128,1536]{1,0:T(8,128)(2,1)} custom-call(bf16[128,2048]{1,0:T(8,128)(2,1)} %bitcast.25, bf16[1,2048]{1,0:T(2,128)(2,1)} %gain_ref.9, bf16[32,2048]{1,0:T(8,128)(2,1)} %bitcast.34, s32[2,128]{1,0:T(2,128)} %bitcast.44), custom_call_target="tpu_custom_call" | custom-call | flops 268435456 | bytes 2097152 | tf_op jit(solution)/shard_map/pallas_call | solution.py:432
  104.9 37.7 %all-to-all-done.2 = bf16[32,8,6272]{2,1,0:T(8,128)(2,1)S(1)} async-done(((bf16[32,8,6272]{2,1,0:T(8,128)(2,1)}), bf16[32,8,6272]{2,1,0:T(8,128)(2,1)S(1)}, u32[]{:S(2)}, u32[]{:S(2)}) %all-to-all-start.2) | async-done | bytes 3211296 | tf_op jit(solution)/shard_map/all_to_all | solution.py:398
  142.7 0.0 copy-start.1
  142.7 1.0 copy-done.1
  143.7 1.0 copy-done.3
  144.8 1.0 copy-done.4
  145.8 1.0 copy-done.5
  146.8 1.0 copy-done.7
  147.8 2.8 %shard_map.119 = (bf16[128,2048]{1,0:T(8,128)(2,1)}, bf16[128,2048]{1,0:T(8,128)(2,1)}) custom-call(bf16[256,6272]{1,0:T(8,128)(2,1)S(1)} %bitcast.23, bf16[128,1536]{1,0:T(8,128)(2,1)S(1)} %copy-done.5, bf16[128,1792]{1,0:T(8,128)(2,1)S(1)} %copy-done.7, f32[128,128]{1,0:T(8,128)S(1)} %copy-done.10, bf16[128,2048]{1,0:T(8,128)(2,1)S(1)} %bitcast.26, ...), custom_call_target="tpu_custom_call" | custom-call | flops 1342177280 | bytes 8388608 | tf_op jit(solution)/shard_map/pallas_call | solution.py:477
  (19 shorter events, 0.0 us)
Async XLA Ops:
  0.6 11.5 %copy-start.15 = (bf16[1,128,2048]{2,1,0:T(8,128)(2,1)S(1)}, bf16[1,128,2048]{2,1,0:T(8,128)(2,1)}, u32[]{:S(2)}) copy-start(bf16[1,128,2048]{2,1,0:T(8,128)(2,1)} %param.10) | copy-start | bytes 1572868
  0.6 13.2 %copy-start.16 = (bf16[1,128,2048]{2,1,0:T(8,128)(2,1)S(1)}, bf16[1,128,2048]{2,1,0:T(8,128)(2,1)}, u32[]{:S(2)}) copy-start(bf16[1,128,2048]{2,1,0:T(8,128)(2,1)} %param.11) | copy-start | bytes 1572868
  3.5 30.9 %all-to-all-start.1 = ((bf16[32,8,3072]{2,1,0:T(8,128)(2,1)}), bf16[32,8,3072]{2,1,0:T(8,128)(2,1)S(1)}, u32[]{:S(2)}, u32[]{:S(2)}) async-start(bf16[32,8,3072]{2,1,0:T(8,128)(2,1)} %bitcast.41), calls=%async_computation.1 | async-start | bytes 3145728 | tf_op jit(solution)/shard_map/all_to_all | solution.py:398
  12.1 17.7 %collective-permute-start.1 = (bf16[1,128,2048]{2,1,0:T(8,128)(2,1)S(1)}, bf16[1,128,2048]{2,1,0:T(8,128)(2,1)S(1)}, u32[]{:S(2)}, u32[]{:S(2)}) collective-permute-start(bf16[1,128,2048]{2,1,0:T(8,128)(2,1)S(1)} %copy-done.15), channel_id=1, source_target_pairs={{0,32},{32,64},{64,96},{96,128},{128,160},{160,192},{192,224},{224... | collective-permute-start | bytes 1572872 | tf_op jit(solution)/shard_map/ppermute | solution.py:25
  13.8 16.0 %collective-permute-start = (bf16[1,128,2048]{2,1,0:T(8,128)(2,1)S(1)}, bf16[1,128,2048]{2,1,0:T(8,128)(2,1)S(1)}, u32[]{:S(2)}, u32[]{:S(2)}) collective-permute-start(bf16[1,128,2048]{2,1,0:T(8,128)(2,1)S(1)} %copy-done.16), channel_id=1, source_target_pairs={{0,224},{32,0},{64,32},{96,64},{128,96},{160,128},{192,160},{224,1... | collective-permute-start | bytes 1572872 | tf_op jit(solution)/shard_map/ppermute | solution.py:25
  29.8 0.8 copy-start
  29.8 1.0 copy-start.2
  34.4 7.9 %copy-start.8 = (bf16[1,2048]{1,0:T(2,128)(2,1)S(1)}, bf16[1,2048]{1,0:T(2,128)(2,1)}, u32[]{:S(2)}) copy-start(bf16[1,2048]{1,0:T(2,128)(2,1)} %gain_ref.9) | copy-start | bytes 12292
  34.5 47.3 %all-to-all-start = ((bf16[32,8,6144]{2,1,0:T(8,128)(2,1)}), bf16[32,8,6144]{2,1,0:T(8,128)(2,1)}, u32[]{:S(2)}, u32[]{:S(2)}) async-start(bf16[32,8,6144]{2,1,0:T(8,128)(2,1)} %bitcast.40), calls=%async_computation | async-start | bytes 6291456 | tf_op jit(solution)/shard_map/all_to_all | solution.py:398
  42.4 1.9 %copy-start.11 = (bf16[1,1,2048,768]{3,2,1,0:T(8,128)(2,1)S(1)}, bf16[1,1,2048,768]{3,2,1,0:T(8,128)(2,1)}, u32[]{:S(2)}) copy-start(bf16[1,1,2048,768]{3,2,1,0:T(8,128)(2,1)} %param.15) | copy-start | bytes 9437188
  44.3 1.9 %copy-start.12 = (bf16[1,1,2048,768]{3,2,1,0:T(8,128)(2,1)S(1)}, bf16[1,1,2048,768]{3,2,1,0:T(8,128)(2,1)}, u32[]{:S(2)}) copy-start(bf16[1,1,2048,768]{3,2,1,0:T(8,128)(2,1)} %param.16) | copy-start | bytes 9437188
  49.2 1.0 copy-start.13
  50.2 1.1 copy-start.14
  95.7 47.0 %copy-start.6 = (bf16[1,2048,32]{1,2,0:T(8,128)(2,1)S(1)}, bf16[1,2048,32]{1,2,0:T(8,128)(2,1)}, u32[]{:S(2)}) copy-start(bf16[1,2048,32]{1,2,0:T(8,128)(2,1)} %param.14) | copy-start | bytes 393220
  95.7 47.0 %copy-start.9 = (bf16[1,2048]{1,0:T(2,128)(2,1)S(1)}, bf16[1,2048]{1,0:T(2,128)(2,1)}, u32[]{:S(2)}) copy-start(bf16[1,2048]{1,0:T(2,128)(2,1)} %gain_ref.9) | copy-start | bytes 12292
  95.7 47.0 %copy-start.10 = (f32[128,128]{1,0:T(8,128)S(1)}, f32[128,128]{1,0:T(8,128)}, u32[]{:S(2)}) copy-start(f32[128,128]{1,0:T(8,128)} %get-tuple-element.13.scalars_ref) | copy-start | bytes 196612
  95.7 47.0 %all-to-all-start.2 = ((bf16[32,8,6272]{2,1,0:T(8,128)(2,1)}), bf16[32,8,6272]{2,1,0:T(8,128)(2,1)S(1)}, u32[]{:S(2)}, u32[]{:S(2)}) async-start(bf16[32,8,6272]{2,1,0:T(8,128)(2,1)} %bitcast.42), calls=%async_computation.2 | async-start | bytes 6422528 | tf_op jit(solution)/shard_map/all_to_all | solution.py:398
  142.7 1.0 copy-start.1
  143.7 1.0 copy-start.3
  144.8 1.0 copy-start.4
  145.8 1.0 copy-start.5
  146.8 1.0 copy-start.7
